TPU v7x, 32 devices: a whole 2x2x4 slice. The times are simulated.
32 devices in a mesh: band: 4 (over y, core), comp: 8 (over z, x).
Axes of the slice: x: 2, y: 2, z: 4, core: 2. Of those that a mesh axis runs over, the one named last changes fastest.
Arguments:
- tracer_mass: float32 [192, 8, 64, 512], P('comp', None, 'band'), may hold values from -6 to 6
- layer_mass: float32 [8, 64, 512], P('comp', 'band'), may hold values from 0.3 to 1.7
- zonal_wind: float32 [8, 64, 512], P('comp', 'band'), may hold values from -4 to 4
- merid_wind: float32 [8, 64, 512], P('comp', 'band'), may hold values from -4 to 4
- group_counts: int32 [8], replicated, may hold values from 1 to 24, 96 in all
- limiter_flags: int32 [96], replicated, may hold values 0 or 1
Outputs:
- tracers_out: float32 [192, 8, 64, 512], P('comp', None, 'band')
- height_out: float32 [8, 64, 512], P('comp', 'band')
- zonal_out: float32 [8, 64, 512], P('comp', 'band')
- merid_out: float32 [8, 64, 512], P('comp', 'band')
Inputs may be any that keep to these rules, and one draw needn't show every extreme that they name: Group g lists the tracers numbered from the sum of the earlier groups' counts on, in its first group_counts[g] slots; the counts sum to 96 and the largest is exactly 24.
All inputs are finite; a program needn't handle non-finite values.
Results may differ from a plain program's by a relative error of at most 0.0003.
Values sent between devices are 32-bit elements; how exact they have to be, the bound alone decides.
No kernel may reach another device: no remote copies, remote signals or barrier semaphores. Data moves between devices by JAX's collectives and lax.ppermute only.
A program may use at most 128 MiB of HBM per device.

v0:
```python
import functools

import jax
import jax.numpy as jnp
from jax import lax
from jax.experimental import pallas as pl
from jax.experimental.pallas import tpu as pltpu
from jax.sharding import PartitionSpec as P

STEPS = 4
HALO = 2 * STEPS

time_step = 0.1
gravity = 0.25
coriolis = 0.5
mass_floor = 0.5


def lane_roll(x, shift):
    return pltpu.roll(x, shift % x.shape[-1], x.ndim - 1)


def band_shift(block, offset):
    count = lax.axis_size("band")
    pairs = [(i, i + offset) for i in range(count) if 0 <= i + offset < count]
    return lax.ppermute(block, "band", pairs)


def face_value(left_out, left_in, right_in, right_out, limited):
    raw_face = 7.0 / 12.0 * (left_in + right_in) - 1.0 / 12.0 * (left_out + right_out)
    if limited:
        low = jnp.minimum(left_in, right_in)
        high = jnp.maximum(left_in, right_in)
        raw_face = jnp.minimum(jnp.maximum(raw_face, low), high)
    return raw_face


def dynamics_kernel(place, own, north, south, inv_ref, east_ref, south_ref,
                    h_out, u_out, v_out, h0, u0, v0, h1, u1, v1, geo):
    levels, _, rows, _ = own.shape
    halo = north.shape[2]
    total = rows + 2 * halo
    for field, dst in enumerate((h0, u0, v0)):
        for q in range(0, halo, 8):
            dst[q:q + 8] = jnp.swapaxes(north[:, field, q:q + 8], 0, 1)
            dst[halo + rows + q:halo + rows + q + 8] = jnp.swapaxes(south[:, field, q:q + 8], 0, 1)
        for q in range(0, rows, 8):
            dst[halo + q:halo + q + 8] = jnp.swapaxes(own[:, field, q:q + 8], 0, 1)
    first_face = place[1] - halo
    face_end = place[2]
    level = lax.broadcasted_iota(jnp.int32, (levels, own.shape[-1]), 0)
    src, dst = (h0, u0, v0), (h1, u1, v1)
    for step in range(STEPS):
        h, u, v = src
        lo, hi = step, total - step

        def column_sum(j, carry):
            acc = h[j]
            span = 1
            while span < levels:
                moved = pltpu.roll(acc, levels - span, 0)
                acc = acc + jnp.where(level < levels - span, moved, 0.0)
                span *= 2
            geo[j] = gravity * acc
            inv_ref[step, j] = 1.0 / jnp.maximum(h[j], mass_floor)
            return carry

        lax.fori_loop(lo, hi, column_sum, 0, unroll=4)

        def south_flux(j):
            face = first_face + j
            scale = jnp.where((face > 0) & (face < face_end), 0.25 * time_step, 0.0)
            return scale * (v[j - 1] + v[j]) * (h[j - 1] + h[j])

        def advance(j, flux_north):
            hj, uj, vj, gj = h[j], u[j], v[j], geo[j]
            flux = south_flux(j + 1)
            east = (0.25 * time_step) * (uj + lane_roll(uj, -1)) * (hj + lane_roll(hj, -1))
            east_ref[step, j] = east
            south_ref[step, j] = flux_north
            dst[0][j] = hj - ((east - lane_roll(east, 1)) + (flux - flux_north))
            slope_x = lane_roll(gj, -1) - lane_roll(gj, 1)
            slope_y = geo[j + 1] - geo[j - 1]
            dst[1][j] = uj + time_step * (coriolis * vj - 0.5 * slope_x)
            dst[2][j] = vj - time_step * (coriolis * uj + 0.5 * slope_y)
            return flux

        last = lax.fori_loop(lo + 1, hi - 1, advance, south_flux(lo + 1), unroll=3)
        south_ref[step, hi - 1] = last
        src, dst = dst, src
    block = h_out.shape[0]
    for k in range(block):
        for r in range(rows):
            for out, field in zip((h_out, u_out, v_out), src):
                out[k, pl.ds(r, 1), :] = field[halo + r, pl.ds(place[0] * block + k, 1), :]


def tracer_kernel(place, counts, flags, mass, north, south, inv_ref, east_ref, south_ref, *rest, first, blocks):
    out_ref, cur0, cur1 = rest[-3:]
    slot = pl.program_id(0) + first
    levels, rows, _ = mass.shape[1:]
    halo = north.shape[2]
    total = rows + 2 * halo
    group = place[0]
    start = jnp.int32(0)
    for g in range(counts.shape[0]):
        start = start + jnp.where(g < group, counts[g], 0)
    live = slot < counts[group]
    flag = flags[jnp.minimum(start + slot, flags.shape[0] - 1)]

    def run(limited):
        for q in range(0, halo, 8):
            cur0[q:q + 8] = jnp.swapaxes(north[0, :, q:q + 8], 0, 1)
            cur0[halo + rows + q:halo + rows + q + 8] = jnp.swapaxes(south[0, :, q:q + 8], 0, 1)
        for q in range(0, rows, 8):
            cur0[halo + q:halo + q + 8] = jnp.swapaxes(mass[0, :, q:q + 8], 0, 1)
        src, dst = cur0, cur1
        for step in range(STEPS):
            lo, hi = 2 * (step + 1), total - 2 * (step + 1)
            size = next(b for b in range(blocks, 0, -1) if (hi - lo) % b == 0)

            def ratio(j):
                return src[j] * inv_ref[step, j]

            def south_term(j, a, b, c, d):
                return south_ref[step, j] * face_value(a, b, c, d, limited)

            near = [ratio(lo - 2), ratio(lo - 1), ratio(lo), ratio(lo + 1)]
            term = south_term(lo, *near)

            def sweep(k, carry):
                j = lo + k * size
                ratios = list(carry[:3])
                masses = [src[j + b] for b in range(size + 2)]
                ratios += [masses[b] * inv_ref[step, j + b] for b in range(2, size + 2)]
                terms = [carry[3]]
                terms += [south_term(j + b + 1, *ratios[b:b + 4]) for b in range(size)]
                done = []
                for b in range(size):
                    r = ratios[b + 1]
                    east = east_ref[step, j + b] * face_value(
                        lane_roll(r, 1), r, lane_roll(r, -1), lane_roll(r, -2), limited)
                    done.append(masses[b] - ((east - lane_roll(east, 1)) + (terms[b + 1] - terms[b])))
                for b in range(size):
                    dst[j + b] = done[b]
                return (*ratios[size:size + 3], terms[size])

            lax.fori_loop(0, (hi - lo) // size, sweep, (*near[1:], term))
            src, dst = dst, src
        for q in range(0, rows, 8):
            out_ref[0, :, q:q + 8] = jnp.swapaxes(src[halo + q:halo + q + 8], 0, 1)

    @pl.when(live & (flag > 0))
    def _():
        run(True)

    @pl.when(live & (flag <= 0))
    def _():
        run(False)

    @pl.when(jnp.logical_not(live))
    def _():
        out_ref[...] = jnp.zeros_like(out_ref)


def whole_block(shape):
    return pl.BlockSpec(shape, lambda *_: (0,) * len(shape))


def run_dynamics(place, own, north, south, level_block):
    levels, _, rows, columns = own.shape
    total = rows + 2 * HALO
    flux = jax.ShapeDtypeStruct((STEPS, total, levels, columns), jnp.float32)
    state = jax.ShapeDtypeStruct((level_block, rows, columns), jnp.float32)
    return pl.pallas_call(
        dynamics_kernel,
        grid_spec=pltpu.PrefetchScalarGridSpec(
            num_scalar_prefetch=1,
            grid=(1,),
            in_specs=[whole_block(own.shape), whole_block(north.shape), whole_block(south.shape)],
            out_specs=[whole_block(flux.shape)] * 3 + [whole_block(state.shape)] * 3,
            scratch_shapes=[pltpu.VMEM((total, levels, columns), jnp.float32)] * 7,
        ),
        out_shape=[flux] * 3 + [state] * 3,
        compiler_params=pltpu.CompilerParams(vmem_limit_bytes=48 << 20),
        name="dynamics",
    )(place, own, north, south)


def run_tracers(place, counts, flags, mass, north, south, fluxes, first, count, earlier):
    slots, levels, rows, columns = mass.shape
    total = rows + 2 * HALO

    def slot_block(height, shift):
        return pl.BlockSpec((1, levels, height, columns), lambda i, *_: (i + shift, 0, 0, 0))

    in_specs = [slot_block(rows, first), slot_block(HALO, 0), slot_block(HALO, 0)]
    in_specs += [whole_block(f.shape) for f in fluxes]
    operands = [mass, north, south, *fluxes]
    aliases = {}
    if earlier is not None:
        aliases = {3 + len(operands): 0}
        in_specs.append(pl.BlockSpec(memory_space=pl.ANY))
        operands.append(earlier)
    return pl.pallas_call(
        functools.partial(tracer_kernel, first=first, blocks=7),
        grid_spec=pltpu.PrefetchScalarGridSpec(
            num_scalar_prefetch=3,
            grid=(count,),
            in_specs=in_specs,
            out_specs=slot_block(rows, first),
            scratch_shapes=[pltpu.VMEM((total, levels, columns), jnp.float32)] * 2,
        ),
        out_shape=jax.ShapeDtypeStruct(mass.shape, jnp.float32),
        input_output_aliases=aliases,
        compiler_params=pltpu.CompilerParams(vmem_limit_bytes=48 << 20),
        name="tracers",
    )(place, counts, flags, *operands)


def on_device(tracer_mass, layer_mass, zonal_wind, merid_wind, group_counts, limiter_flags):
    n_comp = lax.axis_size("comp")
    n_band = lax.axis_size("band")
    slots, levels, rows, columns = tracer_mass.shape
    level_block = layer_mass.shape[0]
    place = jnp.stack([
        lax.axis_index("comp"), lax.axis_index("band") * rows, jnp.int32(rows * n_band)
    ]).astype(jnp.int32)
    chunk = slots // 2
    halos = []
    for first in range(0, slots, chunk):
        part = tracer_mass[first:first + chunk]
        halos.append((
            band_shift(part[:, :, rows - HALO:], 1),
            band_shift(part[:, :, :HALO], -1),
        ))
    state = jnp.stack([layer_mass, zonal_wind, merid_wind], 1)
    copies = jnp.broadcast_to(state[None], (n_comp, *state.shape)).reshape(n_comp * level_block, *state.shape[1:])
    gathered = lax.all_to_all(copies, "comp", 0, 0, tiled=True)
    from_north = band_shift(gathered[:, :, rows - HALO:], 1)
    from_south = band_shift(gathered[:, :, :HALO], -1)
    *fluxes, height, zonal, merid = run_dynamics(place, gathered, from_north, from_south, level_block)
    tracers = None
    for index, (north, south) in enumerate(halos):
        tracers = run_tracers(place, group_counts, limiter_flags, tracer_mass, north, south,
                              fluxes, index * chunk, chunk, tracers)
    return tracers, height, zonal, merid


def solution(mesh):
    placed = (
        P("comp", None, "band", None),
        P("comp", "band", None),
        P("comp", "band", None),
        P("comp", "band", None),
        P(),
        P(),
    )
    return jax.shard_map(
        on_device,
        mesh=mesh,
        in_specs=placed,
        out_specs=placed[:4],
        check_vma=False,
    )
```

profile of v0, /device:TPU:6, one launch (start us, length us, event | category | flops | bytes accessed | tf_op | source)
XLA Modules:
  0.0 176.6 jit_solution(11124182853209357092)
XLA Ops:
  0.6 0.8 maximum_bitcast_fusion
  1.4 1.0 reshape.14
  2.4 6.3 %all-to-all-start = ((f32[8,3,16,512]{3,2,1,0:T(8,128)}), f32[8,3,16,512]{3,2,1,0:T(8,128)S(1)}, u32[]{:S(2)}, u32[]{:S(2)}) async-start(f32[8,3,16,512]{3,2,1,0:T(8,128)} %reshape.14), calls=%async_computation | async-start | bytes 1572864 | tf_op jit(solution)/shard_map/all_to_all | solution.py:239
  8.8 6.0 %fusion = (f32[12,8,8,512]{3,2,1,0:T(8,128)}, f32[12,8,8,512]{3,2,1,0:T(8,128)}, f32[12,8,8,512]{3,2,1,0:T(8,128)}, f32[12,8,8,512]{3,2,1,0:T(8,128)}) fusion(f32[24,8,16,512]{3,2,1,0:T(8,128)} %mass.3), kind=kLoop, calls=%fused_computation.2 | loop fusion | bytes 12582912 | tf_op jit(solution)/shard_map/slice | solution.py:235
  14.7 1.9 %collective-permute-start.5 = (f32[12,8,8,512]{3,2,1,0:T(8,128)}, f32[12,8,8,512]{3,2,1,0:T(8,128)}, u32[]{:S(2)}, u32[]{:S(2)}) collective-permute-start(f32[12,8,8,512]{3,2,1,0:T(8,128)} %get-tuple-element.16), channel_id=1, source_target_pairs={{8,0},{16,8},{24,16},{9,1},{17,9},{25,17},{10,2},{18,10},{26,18},{... | collective-permute-start | bytes 4718600 | tf_op jit(solution)/shard_map/ppermute | solution.py:26
  16.7 3.6 %collective-permute-start.4 = (f32[12,8,8,512]{3,2,1,0:T(8,128)}, f32[12,8,8,512]{3,2,1,0:T(8,128)}, u32[]{:S(2)}, u32[]{:S(2)}) collective-permute-start(f32[12,8,8,512]{3,2,1,0:T(8,128)} %get-tuple-element.17), channel_id=1, source_target_pairs={{0,8},{8,16},{16,24},{1,9},{9,17},{17,25},{2,10},{10,18},{18,26},{... | collective-permute-start | bytes 4718600 | tf_op jit(solution)/shard_map/ppermute | solution.py:26
  20.3 1.9 %collective-permute-start.1 = (f32[12,8,8,512]{3,2,1,0:T(8,128)}, f32[12,8,8,512]{3,2,1,0:T(8,128)S(1)}, u32[]{:S(2)}, u32[]{:S(2)}) collective-permute-start(f32[12,8,8,512]{3,2,1,0:T(8,128)} %get-tuple-element.18), channel_id=1, source_target_pairs={{8,0},{16,8},{24,16},{9,1},{17,9},{25,17},{10,2},{18,10},{26,18},{... | collective-permute-start | bytes 4718600 | tf_op jit(solution)/shard_map/ppermute | solution.py:26
  22.2 0.0 copy-start.1
  22.2 0.0 copy-start.2
  22.3 2.5 %collective-permute-start = (f32[12,8,8,512]{3,2,1,0:T(8,128)}, f32[12,8,8,512]{3,2,1,0:T(8,128)}, u32[]{:S(2)}, u32[]{:S(2)}) collective-permute-start(f32[12,8,8,512]{3,2,1,0:T(8,128)} %get-tuple-element.19), channel_id=1, source_target_pairs={{0,8},{8,16},{16,24},{1,9},{9,17},{17,25},{2,10},{10,18},{18,26},{... | collective-permute-start | bytes 4718600 | tf_op jit(solution)/shard_map/ppermute | solution.py:26
  24.8 3.6 %all-to-all-done.own = f32[8,3,16,512]{3,2,1,0:T(8,128)S(1)} async-done(((f32[8,3,16,512]{3,2,1,0:T(8,128)}), f32[8,3,16,512]{3,2,1,0:T(8,128)S(1)}, u32[]{:S(2)}, u32[]{:S(2)}) %all-to-all-start) | async-done | bytes 786464 | tf_op jit(solution)/shard_map/all_to_all | solution.py:239
  28.3 0.1 fusion.1
  28.4 1.9 %collective-permute-start.3 = (f32[8,3,8,512]{3,2,1,0:T(8,128)S(1)}, f32[8,3,8,512]{3,2,1,0:T(8,128)S(1)}, u32[]{:S(2)}, u32[]{:S(2)}) collective-permute-start(f32[8,3,8,512]{3,2,1,0:T(8,128)S(1)} %get-tuple-element.20), channel_id=1, source_target_pairs={{8,0},{16,8},{24,16},{9,1},{17,9},{25,17},{10,2},{18,10},{26,18},{... | collective-permute-start | bytes 1179656 | tf_op jit(solution)/shard_map/ppermute | solution.py:26
  30.3 25.6 %collective-permute-done.3.south = f32[8,3,8,512]{3,2,1,0:T(8,128)S(1)} collective-permute-done((f32[8,3,8,512]{3,2,1,0:T(8,128)S(1)}, f32[8,3,8,512]{3,2,1,0:T(8,128)S(1)}, u32[]{:S(2)}, u32[]{:S(2)}) %collective-permute-start.3) | collective-permute-done | bytes 393248 | tf_op jit(solution)/shard_map/ppermute | solution.py:26
  55.8 1.9 %collective-permute-start.2 = (f32[8,3,8,512]{3,2,1,0:T(8,128)S(1)}, f32[8,3,8,512]{3,2,1,0:T(8,128)S(1)}, u32[]{:S(2)}, u32[]{:S(2)}) collective-permute-start(f32[8,3,8,512]{3,2,1,0:T(8,128)S(1)} %get-tuple-element.21), channel_id=1, source_target_pairs={{0,8},{8,16},{16,24},{1,9},{9,17},{17,25},{2,10},{10,18},{18,26},{... | collective-permute-start | bytes 1179656 | tf_op jit(solution)/shard_map/ppermute | solution.py:26
  57.8 0.1 pad_add_fusion.place
  57.8 7.3 %collective-permute-done.2.north = f32[8,3,8,512]{3,2,1,0:T(8,128)S(1)} collective-permute-done((f32[8,3,8,512]{3,2,1,0:T(8,128)S(1)}, f32[8,3,8,512]{3,2,1,0:T(8,128)S(1)}, u32[]{:S(2)}, u32[]{:S(2)}) %collective-permute-start.2) | collective-permute-done | bytes 393248 | tf_op jit(solution)/shard_map/ppermute | solution.py:26
  65.1 9.4 %dynamics.1 = (f32[4,32,8,512]{3,2,1,0:T(8,128)S(1)}, f32[4,32,8,512]{3,2,1,0:T(8,128)S(1)}, f32[4,32,8,512]{3,2,1,0:T(8,128)}, f32[1,16,512]{2,1,0:T(8,128)}, f...) custom-call(s32[3]{0:T(128)S(1)} %pad_add_fusion.place, f32[8,3,16,512]{3,2,1,0:T(8,128)S(1)} %all-to-all-done.own, ...), custom_call_target="tpu_custom_call" | custom-call | tf_op jit(solution)/shard_map/dynamics/pallas_call | solution.py:175
  74.5 0.0 copy-start
  74.5 1.3 copy-done
  75.8 0.0 collective-permute-done.5.south
  75.8 0.0 collective-permute-done.4.north
  75.8 0.0 copy-done.1
  75.8 0.0 copy-done.2
  75.8 50.5 %tracers.2.rest_0_ = f32[24,8,16,512]{3,2,1,0:T(8,128)} custom-call(s32[3]{0:T(128)S(1)} %pad_add_fusion.place, s32[8]{0:T(128)S(1)} %copy-done.1, s32[96]{0:T(128)S(1)} %copy-done.2, f32[24,8,16,512]{3,2,1,0:T(8,128)} %mass.3, f32[12,8,8,512]{3,2,1,0:T(8,128)} %collective-permute-done.4.north, f32[12,8,8,512]{3,2,1,0:T(8,128)} %collective-permute-done.5.south, ...), custom_call_target="tpu_custom_call" | custom-call | tf_op jit(solution)/shard_map/tracers/pallas_call | solution.py:205
  126.4 0.0 collective-permute-done.1.south
  126.4 0.0 collective-permute-done.north
  126.4 50.2 %tracers.3 = f32[24,8,16,512]{3,2,1,0:T(8,128)} custom-call(s32[3]{0:T(128)S(1)} %pad_add_fusion.place, s32[8]{0:T(128)S(1)} %copy-done.1, s32[96]{0:T(128)S(1)} %copy-done.2, f32[24,8,16,512]{3,2,1,0:T(8,128)} %mass.3, f32[12,8,8,512]{3,2,1,0:T(8,128)} %collective-permute-done.north, ...), custom_call_target="tpu_custom_call", output_to_operand_aliasing={{}: (9, {})} | custom-call | tf_op jit(solution)/shard_map/tracers/pallas_call | solution.py:205
Async XLA Ops:
  2.4 25.9 %all-to-all-start = ((f32[8,3,16,512]{3,2,1,0:T(8,128)}), f32[8,3,16,512]{3,2,1,0:T(8,128)S(1)}, u32[]{:S(2)}, u32[]{:S(2)}) async-start(f32[8,3,16,512]{3,2,1,0:T(8,128)} %reshape.14), calls=%async_computation | async-start | bytes 1572864 | tf_op jit(solution)/shard_map/all_to_all | solution.py:239
  14.7 61.1 %collective-permute-start.5 = (f32[12,8,8,512]{3,2,1,0:T(8,128)}, f32[12,8,8,512]{3,2,1,0:T(8,128)}, u32[]{:S(2)}, u32[]{:S(2)}) collective-permute-start(f32[12,8,8,512]{3,2,1,0:T(8,128)} %get-tuple-element.16), channel_id=1, source_target_pairs={{8,0},{16,8},{24,16},{9,1},{17,9},{25,17},{10,2},{18,10},{26,18},{... | collective-permute-start | bytes 4718600 | tf_op jit(solution)/shard_map/ppermute | solution.py:26
  16.7 59.2 %collective-permute-start.4 = (f32[12,8,8,512]{3,2,1,0:T(8,128)}, f32[12,8,8,512]{3,2,1,0:T(8,128)}, u32[]{:S(2)}, u32[]{:S(2)}) collective-permute-start(f32[12,8,8,512]{3,2,1,0:T(8,128)} %get-tuple-element.17), channel_id=1, source_target_pairs={{0,8},{8,16},{16,24},{1,9},{9,17},{17,25},{2,10},{10,18},{18,26},{... | collective-permute-start | bytes 4718600 | tf_op jit(solution)/shard_map/ppermute | solution.py:26
  20.3 106.1 %collective-permute-start.1 = (f32[12,8,8,512]{3,2,1,0:T(8,128)}, f32[12,8,8,512]{3,2,1,0:T(8,128)S(1)}, u32[]{:S(2)}, u32[]{:S(2)}) collective-permute-start(f32[12,8,8,512]{3,2,1,0:T(8,128)} %get-tuple-element.18), channel_id=1, source_target_pairs={{8,0},{16,8},{24,16},{9,1},{17,9},{25,17},{10,2},{18,10},{26,18},{... | collective-permute-start | bytes 4718600 | tf_op jit(solution)/shard_map/ppermute | solution.py:26
  22.2 53.6 %copy-start.1 = (s32[8]{0:T(128)S(1)}, s32[8]{0:T(128)}, u32[]{:S(2)}) copy-start(s32[8]{0:T(128)} %counts.3) | copy-start | bytes 100
  22.2 53.6 %copy-start.2 = (s32[96]{0:T(128)S(1)}, s32[96]{0:T(128)}, u32[]{:S(2)}) copy-start(s32[96]{0:T(128)} %flags.3) | copy-start | bytes 1156
  22.3 104.1 %collective-permute-start = (f32[12,8,8,512]{3,2,1,0:T(8,128)}, f32[12,8,8,512]{3,2,1,0:T(8,128)}, u32[]{:S(2)}, u32[]{:S(2)}) collective-permute-start(f32[12,8,8,512]{3,2,1,0:T(8,128)} %get-tuple-element.19), channel_id=1, source_target_pairs={{0,8},{8,16},{16,24},{1,9},{9,17},{17,25},{2,10},{10,18},{18,26},{... | collective-permute-start | bytes 4718600 | tf_op jit(solution)/shard_map/ppermute | solution.py:26
  28.4 27.5 %collective-permute-start.3 = (f32[8,3,8,512]{3,2,1,0:T(8,128)S(1)}, f32[8,3,8,512]{3,2,1,0:T(8,128)S(1)}, u32[]{:S(2)}, u32[]{:S(2)}) collective-permute-start(f32[8,3,8,512]{3,2,1,0:T(8,128)S(1)} %get-tuple-element.20), channel_id=1, source_target_pairs={{8,0},{16,8},{24,16},{9,1},{17,9},{25,17},{10,2},{18,10},{26,18},{... | collective-permute-start | bytes 1179656 | tf_op jit(solution)/shard_map/ppermute | solution.py:26
  55.8 9.3 %collective-permute-start.2 = (f32[8,3,8,512]{3,2,1,0:T(8,128)S(1)}, f32[8,3,8,512]{3,2,1,0:T(8,128)S(1)}, u32[]{:S(2)}, u32[]{:S(2)}) collective-permute-start(f32[8,3,8,512]{3,2,1,0:T(8,128)S(1)} %get-tuple-element.21), channel_id=1, source_target_pairs={{0,8},{8,16},{16,24},{1,9},{9,17},{17,25},{2,10},{10,18},{18,26},{... | collective-permute-start | bytes 1179656 | tf_op jit(solution)/shard_map/ppermute | solution.py:26
  74.5 1.3 copy-start
where the time goes:
time: 177 us
  Pallas kernels  110 us (62%)
  waiting for transfers between devices  36.4 us (21%)
  starting transfers between devices  20.1 us (11%)
  local copies, waits for them, and re-layouts  8.34 us (5%)
    pallas_call x2, Pallas kernels, run_tracers(): pl.pallas_call(functools.partial(tracer_kernel, first=first, blocks=7), g...  101 us
    ppermute x6, waiting for transfers between devices, band_shift(): return lax.ppermute(block, 'band', pairs)  32.8 us
    ppermute x6, starting transfers between devices, band_shift(): return lax.ppermute(block, 'band', pairs)  13.8 us
    pallas_call x1, Pallas kernels, run_dynamics(): pl.pallas_call(dynamics_kernel, grid_spec=pltpu.PrefetchScalarGridSpec(nu...  9.4 us
    all_to_all x1, starting transfers between devices, on_device(): gathered = lax.all_to_all(copies, 'comp', 0, 0, tiled=True)  6.34 us
    slice x1, local copies, waits for them, and re-layouts, on_device(): part[:, :, :HALO]  5.98 us
    all_to_all x1, waiting for transfers between devices, on_device(): gathered = lax.all_to_all(copies, 'comp', 0, 0, tiled=True)  3.55 us
  transfers between devices with their start and end apart: 7, of which 3 were waited for; matrix products, arithmetic and copies ran while one was open for 3% of the time, Pallas kernels for 34%

commit v1 on v0

v1 whole, which is shorter than its diff:
```python
import functools

import jax
import jax.numpy as jnp
from jax import lax
from jax.experimental import pallas as pl
from jax.experimental.pallas import tpu as pltpu
from jax.sharding import PartitionSpec as P

STEPS = 4
HALO = 2 * STEPS

time_step = 0.1
gravity = 0.25
coriolis = 0.5
mass_floor = 0.5


LANES = 128


def band_shift(block, offset):
    count = lax.axis_size("band")
    pairs = [(i, i + offset) for i in range(count) if 0 <= i + offset < count]
    return lax.ppermute(block, "band", pairs)


def lane_index(shape):
    return lax.broadcasted_iota(jnp.int32, shape, len(shape) - 1)


def swap_bits(tiles):
    tiles = list(tiles)
    lane = lane_index(tiles[0].shape)
    bit = 1
    while bit < len(tiles):
        keep = (lane & bit) == 0
        for a in range(len(tiles)):
            if not a & bit:
                b = a | bit
                first, second = tiles[a], tiles[b]
                axis = first.ndim - 1
                tiles[a] = jnp.where(keep, first, pltpu.roll(second, bit, axis))
                tiles[b] = jnp.where(keep, pltpu.roll(first, LANES - bit, axis), second)
        bit *= 2
    return tiles


def neighbour_lanes(shape, parts, offset):
    lane = lane_index(shape)
    run = LANES // parts
    place = run * (lane % parts) + lane // parts
    place = (place + offset + LANES) % LANES
    return (place % run) * parts + place // run


def take_lanes(tile, index):
    return jnp.take_along_axis(tile, index, axis=1, mode="promise_in_bounds")


def split_row(row):
    return [row[..., p * LANES:(p + 1) * LANES] for p in range(row.shape[-1] // LANES)]


def arrange_kernel(mass, top, bottom):
    rows = mass.shape[2]
    half = rows // 2
    for out, base in ((top, 0), (bottom, half)):
        for q in range(0, half, 8):
            block = jnp.swapaxes(mass[0, :, base + q:base + q + 8], 0, 1)
            tiles = swap_bits(split_row(block))
            for p, tile in enumerate(tiles):
                out[0, q:q + 8, p] = tile


def dynamics_kernel(place, own, north, south, inv_ref, east_ref, south_ref,
                    h_out, u_out, v_out, h0, u0, v0, h1, u1, v1, geo):
    levels, _, rows, columns = own.shape
    parts = columns // LANES
    halo = north.shape[2]
    total = rows + 2 * halo
    for field, dst in enumerate((h0, u0, v0)):
        for source, base in ((north, 0), (own, halo), (south, halo + rows)):
            for q in range(0, source.shape[2], 8):
                block = jnp.swapaxes(source[:, field, q:q + 8], 0, 1)
                for p, tile in enumerate(swap_bits(split_row(block))):
                    dst[base + q:base + q + 8, p] = tile
    first_face = place[1] - halo
    face_end = place[2]
    shape = (levels, LANES)
    ahead = neighbour_lanes(shape, parts, 1)
    behind = neighbour_lanes(shape, parts, -1)
    level = lax.broadcasted_iota(jnp.int32, shape, 0)
    src, dst = (h0, u0, v0), (h1, u1, v1)
    for step in range(STEPS):
        h, u, v = src
        lo, hi = step, total - step

        def column_sum(j, carry):
            for p in range(parts):
                hp = h[j, p]
                acc = hp
                span = 1
                while span < levels:
                    moved = pltpu.roll(acc, levels - span, 0)
                    acc = acc + jnp.where(level < levels - span, moved, 0.0)
                    span *= 2
                geo[j, p] = gravity * acc
                inv_ref[step, j, p] = (1.0 / 12.0) / jnp.maximum(hp, mass_floor)
            return carry

        lax.fori_loop(lo, hi, column_sum, 0, unroll=2)

        def south_flux(j):
            face = first_face + j
            scale = jnp.where((face > 0) & (face < face_end), 0.25 * time_step, 0.0)
            return [scale * (v[j - 1, p] + v[j, p]) * (h[j - 1, p] + h[j, p]) for p in range(parts)]

        def advance(j, flux_north):
            hj, uj, vj, gj = ([f[j, p] for p in range(parts)] for f in (h, u, v, geo))
            hj.append(take_lanes(hj[0], ahead))
            uj.append(take_lanes(uj[0], ahead))
            gj = [take_lanes(gj[-1], behind), *gj, take_lanes(gj[0], ahead)]
            flux = south_flux(j + 1)
            east = [(0.25 * time_step) * (uj[p] + uj[p + 1]) * (hj[p] + hj[p + 1]) for p in range(parts)]
            east = [take_lanes(east[-1], behind), *east]
            for p in range(parts):
                east_ref[step, j, p] = east[p + 1]
                south_ref[step, j, p] = flux_north[p]
                dst[0][j, p] = hj[p] - ((east[p + 1] - east[p]) + (flux[p] - flux_north[p]))
                slope_x = gj[p + 2] - gj[p]
                slope_y = geo[j + 1, p] - geo[j - 1, p]
                dst[1][j, p] = uj[p] + time_step * (coriolis * vj[p] - 0.5 * slope_x)
                dst[2][j, p] = vj[p] - time_step * (coriolis * uj[p] + 0.5 * slope_y)
            return flux

        last = lax.fori_loop(lo + 1, hi - 1, advance, south_flux(lo + 1), unroll=2)
        for p in range(parts):
            south_ref[step, hi - 1, p] = last[p]
        src, dst = dst, src
    block = h_out.shape[0]
    for out, field in zip((h_out, u_out, v_out), src):
        for k in range(block):
            mine = pl.ds(place[0] * block + k, 1)
            for r in range(rows):
                tiles = swap_bits([field[halo + r, p, mine, :] for p in range(parts)])
                for p, tile in enumerate(tiles):
                    out[k, r:r + 1, p * LANES:(p + 1) * LANES] = tile


def tracer_kernel(place, counts, flags, north, top, bottom, south, inv_ref, east_ref, south_ref, *rest, first, size):
    out_ref, cur, even, odd = rest[-4:]
    slot = pl.program_id(0) + first
    parts = north.shape[2]
    levels = north.shape[3]
    halo = north.shape[1]
    half = top.shape[1]
    rows = 2 * half
    total = rows + 2 * halo
    group = place[0]
    start = jnp.int32(0)
    for g in range(counts.shape[0]):
        start = start + jnp.where(g < group, counts[g], 0)
    live = slot < counts[group]
    flag = flags[jnp.minimum(start + slot, flags.shape[0] - 1)]
    shape = (levels, LANES)

    def run(limited):
        ahead = neighbour_lanes(shape, parts, 1)
        behind = neighbour_lanes(shape, parts, -1)

        def spread(buffer, j, tiles):
            for p in range(parts):
                buffer[j, p + 1] = tiles[p]
            buffer[j, 0] = take_lanes(tiles[-1], behind)
            buffer[j, parts + 1] = take_lanes(tiles[0], ahead)
            buffer[j, parts + 2] = take_lanes(tiles[1], ahead)

        for source, base in ((north, 0), (top, halo), (bottom, halo + half), (south, halo + rows)):
            def enter(r, carry):
                tiles = [source[0, r, p] for p in range(parts)]
                for p in range(parts):
                    cur[size + base + r, p] = tiles[p]
                spread(even, size + base + r, [tiles[p] * inv_ref[0, base + r, p] for p in range(parts)])
                return carry
            lax.fori_loop(0, source.shape[1], enter, 0, unroll=True)

        def face(a2, a, b, b2, bounds):
            raw = 7.0 * (a + b) - (a2 + b2)
            if limited:
                raw = jnp.minimum(jnp.maximum(raw, jnp.minimum(*bounds)), jnp.maximum(*bounds))
            return raw

        def scaled(tiles):
            return [12.0 * t for t in tiles] if limited else [None] * len(tiles)

        src, dst = even, odd
        for step in range(STEPS):
            lo, hi = 2 * (step + 1), total - 2 * (step + 1)
            onward = step + 1 < STEPS

            def south_terms(j, near, bounds):
                return [south_ref[step, j, p] * face(*(t[p] for t in near), tuple(t[p] for t in bounds))
                        for p in range(parts)]

            near = [[src[size + lo - 2 + b, p + 1] for p in range(parts)] for b in range(4)]
            term = south_terms(lo, near, [scaled(near[1]), scaled(near[2])])

            def finish(j, partial, moved):
                for b in range(size):
                    at = size + j - size + b
                    tiles = [partial[b] + moved[b]]
                    cur[at, 0] = tiles[0]
                    if onward:
                        tiles += [cur[at, p] for p in range(1, parts)]
                        factor = [inv_ref[step + 1, jnp.maximum(j - size + b, 0), p] for p in range(parts)]
                        spread(dst, at, [t * f for t, f in zip(tiles, factor)])

            def sweep(k, carry):
                term, partial, moved = carry
                j = lo + k * size
                table = [[src[size + j - 1 + b, p + 1] for p in range(parts)] for b in range(size + 3)]
                bounds = [None] + [scaled(t) for t in table[1:size + 2]]
                masses = [[cur[size + j + b, p] for p in range(parts)] for b in range(size)]
                next_partial, next_moved, stores = [], [], []
                for b in range(size):
                    at = size + j + b
                    wide = [src[at, 0], *table[b + 1], src[at, parts + 1], src[at, parts + 2]]
                    limit = bounds[b + 1] + scaled([wide[parts + 1]])
                    east = [east_ref[step, j + b, p] * face(*wide[p:p + 4], (limit[p], limit[p + 1]))
                            for p in range(parts)]
                    next_moved.append(take_lanes(east[-1], behind))
                    following = south_terms(j + b + 1, table[b:b + 4], bounds[b + 1:b + 3])
                    next_partial.append(masses[b][0] - (east[0] + (following[0] - term[0])))
                    stores.append([masses[b][p] - ((east[p] - east[p - 1]) + (following[p] - term[p]))
                                   for p in range(1, parts)])
                    term = following
                finish(j, partial, moved)
                for b in range(size):
                    for p in range(1, parts):
                        cur[size + j + b, p] = stores[b][p - 1]
                return term, next_partial, next_moved

            zeros = [jnp.zeros(shape, jnp.float32)] * size
            count = (hi - lo) // size
            term, partial, moved = lax.fori_loop(0, count, sweep, (term, zeros, zeros))
            finish(hi, partial, moved)
            src, dst = dst, src
        for q in range(0, rows, 8):
            base = size + halo + q
            tiles = swap_bits([cur[base:base + 8, p] for p in range(parts)])
            for p, tile in enumerate(tiles):
                out_ref[0, :, q:q + 8, p * LANES:(p + 1) * LANES] = jnp.swapaxes(tile, 0, 1)

    @pl.when(live & (flag > 0))
    def _():
        run(True)

    @pl.when(live & (flag <= 0))
    def _():
        run(False)

    @pl.when(jnp.logical_not(live))
    def _():
        out_ref[...] = jnp.zeros_like(out_ref)


def whole_block(shape):
    return pl.BlockSpec(shape, lambda *_: (0,) * len(shape))


def run_arrange(mass, first, count):
    _, levels, rows, columns = mass.shape
    half = jax.ShapeDtypeStruct((count, rows // 2, columns // LANES, levels, LANES), jnp.float32)
    return pl.pallas_call(
        arrange_kernel,
        grid=(count,),
        in_specs=[pl.BlockSpec((1, levels, rows, columns), lambda i: (i + first, 0, 0, 0))],
        out_specs=[pl.BlockSpec((1, *half.shape[1:]), lambda i: (i, 0, 0, 0, 0))] * 2,
        out_shape=[half] * 2,
        name="arrange",
    )(mass)


def run_dynamics(place, own, north, south, level_block):
    levels, _, rows, columns = own.shape
    total = rows + 2 * HALO
    tiles = (total, columns // LANES, levels, LANES)
    flux = jax.ShapeDtypeStruct((STEPS, *tiles), jnp.float32)
    state = jax.ShapeDtypeStruct((level_block, rows, columns), jnp.float32)
    return pl.pallas_call(
        dynamics_kernel,
        grid_spec=pltpu.PrefetchScalarGridSpec(
            num_scalar_prefetch=1,
            grid=(1,),
            in_specs=[whole_block(own.shape), whole_block(north.shape), whole_block(south.shape)],
            out_specs=[whole_block(flux.shape)] * 3 + [whole_block(state.shape)] * 3,
            scratch_shapes=[pltpu.VMEM(tiles, jnp.float32)] * 7,
        ),
        out_shape=[flux] * 3 + [state] * 3,
        compiler_params=pltpu.CompilerParams(vmem_limit_bytes=48 << 20),
        name="dynamics",
    )(place, own, north, south)


def run_tracers(place, counts, flags, blocks, fluxes, first, out_shape, earlier, size=4):
    count, half, parts, levels, lanes = blocks[0].shape
    total = 2 * half + 2 * HALO
    in_specs = [pl.BlockSpec((1, *b.shape[1:]), lambda i, *_: (i, 0, 0, 0, 0)) for b in blocks]
    in_specs += [whole_block(f.shape) for f in fluxes]
    operands = [*blocks, *fluxes]
    aliases = {}
    if earlier is not None:
        aliases = {3 + len(operands): 0}
        in_specs.append(pl.BlockSpec(memory_space=pl.ANY))
        operands.append(earlier)
    wide = pltpu.VMEM((total + size, parts + 3, levels, lanes), jnp.float32)
    return pl.pallas_call(
        functools.partial(tracer_kernel, first=first, size=size),
        grid_spec=pltpu.PrefetchScalarGridSpec(
            num_scalar_prefetch=3,
            grid=(count,),
            in_specs=in_specs,
            out_specs=pl.BlockSpec((1, *out_shape[1:]), lambda i, *_: (i + first, 0, 0, 0)),
            scratch_shapes=[pltpu.VMEM((total + size, parts, levels, lanes), jnp.float32), wide, wide],
        ),
        out_shape=jax.ShapeDtypeStruct(out_shape, jnp.float32),
        input_output_aliases=aliases,
        compiler_params=pltpu.CompilerParams(vmem_limit_bytes=48 << 20),
        name="tracers",
    )(place, counts, flags, *operands)


def on_device(tracer_mass, layer_mass, zonal_wind, merid_wind, group_counts, limiter_flags):
    n_comp = lax.axis_size("comp")
    n_band = lax.axis_size("band")
    slots, levels, rows, columns = tracer_mass.shape
    level_block = layer_mass.shape[0]
    assert rows == 2 * HALO and levels == 8
    place = jnp.stack([
        lax.axis_index("comp"), lax.axis_index("band") * rows, jnp.int32(rows * n_band)
    ]).astype(jnp.int32)
    state = jnp.stack([layer_mass, zonal_wind, merid_wind], 1)
    copies = jnp.broadcast_to(state[None], (n_comp, *state.shape)).reshape(n_comp * level_block, *state.shape[1:])
    gathered = lax.all_to_all(copies, "comp", 0, 0, tiled=True)
    chunk = slots // 2
    halves = [run_arrange(tracer_mass, first, chunk) for first in range(0, slots, chunk)]

    def exchange(top, bottom):
        return (band_shift(bottom, 1), top, bottom, band_shift(top, -1))

    blocks = [exchange(*halves[0])]
    from_north = band_shift(gathered[:, :, rows - HALO:], 1)
    from_south = band_shift(gathered[:, :, :HALO], -1)
    top, bottom, from_north, from_south = lax.optimization_barrier((*halves[1], from_north, from_south))
    blocks.append(exchange(top, bottom))
    *fluxes, height, zonal, merid = run_dynamics(place, gathered, from_north, from_south, level_block)
    tracers = None
    for index, block in enumerate(blocks):
        tracers = run_tracers(place, group_counts, limiter_flags, block, fluxes, index * chunk,
                              tracer_mass.shape, tracers)
    return tracers, height, zonal, merid


def solution(mesh):
    placed = (
        P("comp", None, "band", None),
        P("comp", "band", None),
        P("comp", "band", None),
        P("comp", "band", None),
        P(),
        P(),
    )
    return jax.shard_map(
        on_device,
        mesh=mesh,
        in_specs=placed,
        out_specs=placed[:4],
        check_vma=False,
    )
```

time: 177 us -> 170 us (0.960)
  the two profiles are of different devices: /device:TPU:6 before, /device:TPU:11 now
where the time goes in v1:
time: 170 us; the launch traced here: 167 us
  Pallas kernels  120 us (71%)
  blocking collectives  22.6 us (13%)
  starting transfers between devices  18 us (11%)
  local copies, waits for them, and re-layouts  4.98 us (3%)
    pallas_call x2, Pallas kernels, run_tracers(): pl.pallas_call(functools.partial(tracer_kernel, first=first, size=size),...  87.2 us
    all_to_all x1, blocking collectives, on_device(): gathered = lax.all_to_all(copies, 'comp', 0, 0, tiled=True)  22.6 us
    pallas_call x2, Pallas kernels, run_arrange(): pl.pallas_call(arrange_kernel, grid=(count,), in_specs=[pl.BlockSpec((1,...  18.3 us
    ppermute x6, starting transfers between devices, band_shift(): return lax.ppermute(block, 'band', pairs)  18 us
    pallas_call x1, Pallas kernels, run_dynamics(): pl.pallas_call(dynamics_kernel, grid_spec=pltpu.PrefetchScalarGridSpec(nu...  14.4 us
    unnamed x16, local copies, waits for them, and re-layouts  4.09 us
  transfers between devices with their start and end apart: 6, of which 0 were waited for; matrix products, arithmetic and copies ran while one was open for 0% of the time, Pallas kernels for 46%

profile of v1, /device:TPU:11, one launch (start us, length us, event | category | flops | bytes accessed | tf_op | source)
XLA Modules:
  0.0 167.2 jit_solution(14723568049220753804)
XLA Ops:
  0.6 0.8 maximum_bitcast_fusion
  1.4 0.1 reshape.14
  1.5 22.6 %all_to_all.5.own = f32[8,3,16,512]{3,2,1,0:T(8,128)S(1)} all-to-all(f32[8,3,16,512]{3,2,1,0:T(8,128)S(1)} %reshape.14), channel_id=1, replica_groups=mesh['band'=4,'comp'=8] {'comp'}, dimensions={0} | all-to-all | bytes 1572864 | tf_op jit(solution)/shard_map/all_to_all | solution.py:345
  24.1 0.8 fusion
  25.0 3.9 %collective-permute-start.1 = (f32[8,3,8,512]{3,2,1,0:T(8,128)}, f32[8,3,8,512]{3,2,1,0:T(8,128)S(1)}, u32[]{:S(2)}, u32[]{:S(2)}) collective-permute-start(f32[8,3,8,512]{3,2,1,0:T(8,128)} %get-tuple-element.32), channel_id=1, source_target_pairs={{8,0},{16,8},{24,16},{9,1},{17,9},{25,17},{10,2},{18,10},{26,18},{... | collective-permute-start | bytes 1179656 | tf_op jit(solution)/shard_map/ppermute | solution.py:25
  28.9 3.0 %collective-permute-start = (f32[8,3,8,512]{3,2,1,0:T(8,128)S(1)}, f32[8,3,8,512]{3,2,1,0:T(8,128)S(1)}, u32[]{:S(2)}, u32[]{:S(2)}) collective-permute-start(f32[8,3,8,512]{3,2,1,0:T(8,128)S(1)} %get-tuple-element.33), channel_id=1, source_target_pairs={{0,8},{8,16},{16,24},{1,9},{9,17},{17,25},{2,10},{10,18},{18,26},{... | collective-permute-start | bytes 1179656 | tf_op jit(solution)/shard_map/ppermute | solution.py:25
  31.9 9.2 %arrange.3 = (f32[12,8,4,8,128]{4,3,2,1,0:T(8,128)}, f32[12,8,4,8,128]{4,3,2,1,0:T(8,128)}) custom-call(f32[24,8,16,512]{3,2,1,0:T(8,128)} %mass.3), custom_call_target="tpu_custom_call" | custom-call | tf_op jit(solution)/shard_map/arrange/pallas_call | solution.py:275
  41.1 2.4 %collective-permute-start.4 = (f32[12,8,4,8,128]{4,3,2,1,0:T(8,128)}, f32[12,8,4,8,128]{4,3,2,1,0:T(8,128)}, u32[]{:S(2)}, u32[]{:S(2)}) collective-permute-start(f32[12,8,4,8,128]{4,3,2,1,0:T(8,128)} %get-tuple-element.27.bottom), channel_id=1, source_target_pairs={{0,8},{8,16},{16,24},{1,9},{9,17},{17,25},{2,10},{10,18},{18,26},{... | collective-permute-start | bytes 4718600 | tf_op jit(solution)/shard_map/ppermute | solution.py:25
  43.5 3.1 %collective-permute-start.5 = (f32[12,8,4,8,128]{4,3,2,1,0:T(8,128)}, f32[12,8,4,8,128]{4,3,2,1,0:T(8,128)}, u32[]{:S(2)}, u32[]{:S(2)}) collective-permute-start(f32[12,8,4,8,128]{4,3,2,1,0:T(8,128)} %get-tuple-element.28.top), channel_id=1, source_target_pairs={{8,0},{16,8},{24,16},{9,1},{17,9},{25,17},{10,2},{18,10},{26,18},{... | collective-permute-start | bytes 4718600 | tf_op jit(solution)/shard_map/ppermute | solution.py:25
  46.6 9.2 %arrange.2 = (f32[12,8,4,8,128]{4,3,2,1,0:T(8,128)}, f32[12,8,4,8,128]{4,3,2,1,0:T(8,128)}) custom-call(f32[24,8,16,512]{3,2,1,0:T(8,128)} %mass.3), custom_call_target="tpu_custom_call" | custom-call | tf_op jit(solution)/shard_map/arrange/pallas_call | solution.py:275
  55.7 0.0 copy-start.2
  55.7 0.0 copy-start.6
  55.7 0.0 copy-start.7
  55.7 0.0 collective-permute-done.1.south
  55.7 0.0 collective-permute-done.north
  55.7 2.6 %collective-permute-start.2 = (f32[12,8,4,8,128]{4,3,2,1,0:T(8,128)}, f32[12,8,4,8,128]{4,3,2,1,0:T(8,128)}, u32[]{:S(2)}, u32[]{:S(2)}) collective-permute-start(f32[12,8,4,8,128]{4,3,2,1,0:T(8,128)} %get-tuple-element.20.bottom), channel_id=1, source_target_pairs={{0,8},{8,16},{16,24},{1,9},{9,17},{17,25},{2,10},{10,18},{18,26},{... | collective-permute-start | bytes 4718600 | tf_op jit(solution)/shard_map/ppermute | solution.py:25
  58.4 3.0 %collective-permute-start.3 = (f32[12,8,4,8,128]{4,3,2,1,0:T(8,128)}, f32[12,8,4,8,128]{4,3,2,1,0:T(8,128)}, u32[]{:S(2)}, u32[]{:S(2)}) collective-permute-start(f32[12,8,4,8,128]{4,3,2,1,0:T(8,128)} %get-tuple-element.21.top), channel_id=1, source_target_pairs={{8,0},{16,8},{24,16},{9,1},{17,9},{25,17},{10,2},{18,10},{26,18},{... | collective-permute-start | bytes 4718600 | tf_op jit(solution)/shard_map/ppermute | solution.py:25
  61.4 0.1 pad_add_fusion.place
  61.4 14.4 %dynamics.1 = (f32[4,32,4,8,128]{4,3,2,1,0:T(8,128)S(1)}, f32[4,32,4,8,128]{4,3,2,1,0:T(8,128)S(1)}, f32[4,32,4,8,128]{4,3,2,1,0:T(8,128)}, f32[1,16,512]{2,1,0:...) custom-call(s32[3]{0:T(128)S(1)} %pad_add_fusion.place, f32[8,3,16,512]{3,2,1,0:T(8,128)S(1)} %all_to_all.5.own, ...), custom_call_target="tpu_custom_call" | custom-call | tf_op jit(solution)/shard_map/dynamics/pallas_call | solution.py:291
  75.8 0.0 copy-start
  75.8 1.3 copy-done
  77.2 0.0 copy-start.1
  77.2 1.3 copy-done.1
  78.5 0.0 collective-permute-done.4.north
  78.5 0.0 collective-permute-done.5.south
  78.5 0.0 copy-done.2
  78.5 0.0 copy-done.6
  78.5 0.0 copy-done.7
  78.5 0.0 copy-start.3
  78.5 1.4 copy-done.3
  79.9 0.0 copy-start.4
  80.0 0.0 copy-start.5
  80.0 43.7 %tracers.2.rest_0_ = f32[24,8,16,512]{3,2,1,0:T(8,128)} custom-call(s32[3]{0:T(128)S(1)} %pad_add_fusion.place, s32[8]{0:T(128)S(1)} %copy-done.6, s32[96]{0:T(128)S(1)} %copy-done.7, f32[12,8,4,8,128]{4,3,2,1,0:T(8,128)} %collective-permute-done.4.north, f32[12,8,4,8,128]{4,3,2,1,0:T(8,128)S(1)} %copy-done.2, f32[12,8,4,8,128]{4,3,2,1,0:T(8,128)S(1)} %copy-done.3, ...), custom_call_target="tpu_custom_call" | custom-call | tf_op jit(solution)/shard_map/tracers/pallas_call | solution.py:318
  123.7 0.0 collective-permute-done.2.north
  123.7 0.0 collective-permute-done.3.south
  123.7 0.0 copy-done.4
  123.7 0.0 copy-done.5
  123.7 43.5 %tracers.3 = f32[24,8,16,512]{3,2,1,0:T(8,128)} custom-call(s32[3]{0:T(128)S(1)} %pad_add_fusion.place, s32[8]{0:T(128)S(1)} %copy-done.6, s32[96]{0:T(128)S(1)} %copy-done.7, f32[12,8,4,8,128]{4,3,2,1,0:T(8,128)} %collective-permute-done.2.north, f32[12,8,4,8,128]{4,3,2,1,0:T(8,128)S(1)} %copy-done.4, ...), custom_call_target="tpu_custom_call", output_to_operand_aliasing={{}: (10, {})} | custom-call | tf_op jit(solution)/shard_map/tracers/pallas_call | solution.py:318
Async XLA Ops:
  25.0 30.8 %collective-permute-start.1 = (f32[8,3,8,512]{3,2,1,0:T(8,128)}, f32[8,3,8,512]{3,2,1,0:T(8,128)S(1)}, u32[]{:S(2)}, u32[]{:S(2)}) collective-permute-start(f32[8,3,8,512]{3,2,1,0:T(8,128)} %get-tuple-element.32), channel_id=1, source_target_pairs={{8,0},{16,8},{24,16},{9,1},{17,9},{25,17},{10,2},{18,10},{26,18},{... | collective-permute-start | bytes 1179656 | tf_op jit(solution)/shard_map/ppermute | solution.py:25
  28.9 26.9 %collective-permute-start = (f32[8,3,8,512]{3,2,1,0:T(8,128)S(1)}, f32[8,3,8,512]{3,2,1,0:T(8,128)S(1)}, u32[]{:S(2)}, u32[]{:S(2)}) collective-permute-start(f32[8,3,8,512]{3,2,1,0:T(8,128)S(1)} %get-tuple-element.33), channel_id=1, source_target_pairs={{0,8},{8,16},{16,24},{1,9},{9,17},{17,25},{2,10},{10,18},{18,26},{... | collective-permute-start | bytes 1179656 | tf_op jit(solution)/shard_map/ppermute | solution.py:25
  41.1 37.4 %collective-permute-start.4 = (f32[12,8,4,8,128]{4,3,2,1,0:T(8,128)}, f32[12,8,4,8,128]{4,3,2,1,0:T(8,128)}, u32[]{:S(2)}, u32[]{:S(2)}) collective-permute-start(f32[12,8,4,8,128]{4,3,2,1,0:T(8,128)} %get-tuple-element.27.bottom), channel_id=1, source_target_pairs={{0,8},{8,16},{16,24},{1,9},{9,17},{17,25},{2,10},{10,18},{18,26},{... | collective-permute-start | bytes 4718600 | tf_op jit(solution)/shard_map/ppermute | solution.py:25
  43.5 35.0 %collective-permute-start.5 = (f32[12,8,4,8,128]{4,3,2,1,0:T(8,128)}, f32[12,8,4,8,128]{4,3,2,1,0:T(8,128)}, u32[]{:S(2)}, u32[]{:S(2)}) collective-permute-start(f32[12,8,4,8,128]{4,3,2,1,0:T(8,128)} %get-tuple-element.28.top), channel_id=1, source_target_pairs={{8,0},{16,8},{24,16},{9,1},{17,9},{25,17},{10,2},{18,10},{26,18},{... | collective-permute-start | bytes 4718600 | tf_op jit(solution)/shard_map/ppermute | solution.py:25
  55.7 22.8 %copy-start.2 = (f32[12,8,4,8,128]{4,3,2,1,0:T(8,128)S(1)}, f32[12,8,4,8,128]{4,3,2,1,0:T(8,128)}, u32[]{:S(2)}) copy-start(f32[12,8,4,8,128]{4,3,2,1,0:T(8,128)} %get-tuple-element.28.top) | copy-start | bytes 4718596
  55.7 22.8 %copy-start.6 = (s32[8]{0:T(128)S(1)}, s32[8]{0:T(128)}, u32[]{:S(2)}) copy-start(s32[8]{0:T(128)} %counts.3) | copy-start | bytes 100
  55.7 22.8 %copy-start.7 = (s32[96]{0:T(128)S(1)}, s32[96]{0:T(128)}, u32[]{:S(2)}) copy-start(s32[96]{0:T(128)} %flags.3) | copy-start | bytes 1156
  55.7 67.9 %collective-permute-start.2 = (f32[12,8,4,8,128]{4,3,2,1,0:T(8,128)}, f32[12,8,4,8,128]{4,3,2,1,0:T(8,128)}, u32[]{:S(2)}, u32[]{:S(2)}) collective-permute-start(f32[12,8,4,8,128]{4,3,2,1,0:T(8,128)} %get-tuple-element.20.bottom), channel_id=1, source_target_pairs={{0,8},{8,16},{16,24},{1,9},{9,17},{17,25},{2,10},{10,18},{18,26},{... | collective-permute-start | bytes 4718600 | tf_op jit(solution)/shard_map/ppermute | solution.py:25
  58.4 65.3 %collective-permute-start.3 = (f32[12,8,4,8,128]{4,3,2,1,0:T(8,128)}, f32[12,8,4,8,128]{4,3,2,1,0:T(8,128)}, u32[]{:S(2)}, u32[]{:S(2)}) collective-permute-start(f32[12,8,4,8,128]{4,3,2,1,0:T(8,128)} %get-tuple-element.21.top), channel_id=1, source_target_pairs={{8,0},{16,8},{24,16},{9,1},{17,9},{25,17},{10,2},{18,10},{26,18},{... | collective-permute-start | bytes 4718600 | tf_op jit(solution)/shard_map/ppermute | solution.py:25
  75.8 1.3 copy-start
  77.2 1.4 copy-start.1
  78.5 1.4 copy-start.3
  79.9 43.7 %copy-start.4 = (f32[12,8,4,8,128]{4,3,2,1,0:T(8,128)S(1)}, f32[12,8,4,8,128]{4,3,2,1,0:T(8,128)}, u32[]{:S(2)}) copy-start(f32[12,8,4,8,128]{4,3,2,1,0:T(8,128)} %get-tuple-element.21.top) | copy-start | bytes 4718596
  80.0 43.7 %copy-start.5 = (f32[12,8,4,8,128]{4,3,2,1,0:T(8,128)S(1)}, f32[12,8,4,8,128]{4,3,2,1,0:T(8,128)}, u32[]{:S(2)}) copy-start(f32[12,8,4,8,128]{4,3,2,1,0:T(8,128)} %get-tuple-element.20.bottom) | copy-start | bytes 4718596

commit v2 on v1

v2 whole, which is shorter than its diff:
```python
import functools
import math

import jax
import jax.numpy as jnp
from jax import lax
from jax.experimental import pallas as pl
from jax.experimental.pallas import tpu as pltpu
from jax.sharding import PartitionSpec as P


STEPS = 4
HALO = 2 * STEPS

time_step = 0.1
gravity = 0.25
coriolis = 0.5
mass_floor = 0.5


LANES = 128
DELAY = 3


def band_shift(block, offset):
    count = lax.axis_size("band")
    pairs = [(i, i + offset) for i in range(count) if 0 <= i + offset < count]
    return lax.ppermute(block, "band", pairs)


def lane_index(shape):
    return lax.broadcasted_iota(jnp.int32, shape, len(shape) - 1)


def swap_bits(tiles):
    tiles = list(tiles)
    lane = lane_index(tiles[0].shape)
    bit = 1
    while bit < len(tiles):
        keep = (lane & bit) == 0
        for a in range(len(tiles)):
            if not a & bit:
                b = a | bit
                first, second = tiles[a], tiles[b]
                axis = first.ndim - 1
                tiles[a] = jnp.where(keep, first, pltpu.roll(second, bit, axis))
                tiles[b] = jnp.where(keep, pltpu.roll(first, LANES - bit, axis), second)
        bit *= 2
    return tiles


def lane_order(shape, parts, inverse):
    lane = lane_index(shape)
    few, many = (parts, LANES // parts) if inverse else (LANES // parts, parts)
    return (lane & (few - 1)) * many + (lane >> (few.bit_length() - 1))


def take_lanes(tile, index):
    return jnp.take_along_axis(tile, index, axis=1, mode="promise_in_bounds")


def interleave(tiles):
    order = lane_order(tiles[0].shape[-2:], len(tiles), False)
    return [take_each(t, order) for t in swap_bits(tiles)]


def restore(tiles):
    order = lane_order(tiles[0].shape[-2:], len(tiles), True)
    return swap_bits([take_each(t, order) for t in tiles])


def take_each(tile, order):
    if tile.ndim == 2:
        return take_lanes(tile, order)
    return jnp.stack([take_lanes(tile[i], order) for i in range(tile.shape[0])])


def after(tile):
    return pltpu.roll(tile, LANES - 1, 1)


def before(tile):
    return pltpu.roll(tile, 1, 1)


def plane_order(levels):
    majors = levels // 2
    swapped = [(field, d, flip) for flip in range(2) for d in range(majors) for field in (1, 2)]
    return swapped + [(0, d, flip) for d in range(majors) for flip in range(2)]


def source_level(comp, levels, major, flip):
    majors = levels // 2
    at = (comp >> 1) - major
    return jnp.where(at < 0, at + majors, at) * 2 + ((comp & 1) ^ flip)


def split_row(row):
    return [row[..., p * LANES:(p + 1) * LANES] for p in range(row.shape[-1] // LANES)]


def arrange_kernel(mass, top, bottom):
    rows = mass.shape[2]
    half = rows // 2

    def one(t, carry):
        for out, base in ((top, 0), (bottom, half)):
            for q in range(0, half, 8):
                block = jnp.swapaxes(mass[t, :, base + q:base + q + 8], 0, 1)
                for p, tile in enumerate(interleave(split_row(block))):
                    out[t, q:q + 8, p] = tile
        return carry

    lax.fori_loop(0, mass.shape[0], one, 0)


def dynamics_kernel(place, own, north, south, inv_ref, east_ref, south_ref,
                    h_out, u_out, v_out, h0, u0, v0, h1, u1, v1, geo, stage):
    planes, rows, columns = own.shape
    parts = columns // LANES
    halo = north.shape[1]
    total = rows + 2 * halo
    levels = planes // 3
    for plane, (field, major, flip) in enumerate(plane_order(levels)):
        level = source_level(place[0], levels, major, flip)
        for source, base in ((north, 0), (own, halo), (south, halo + rows)):
            stage[field, level, base:base + source.shape[1]] = source[plane]
    for field, dst in enumerate((h0, u0, v0)):
        for q in range(0, total, 8):
            block = jnp.swapaxes(stage[field, :, q:q + 8], 0, 1)
            for p, tile in enumerate(interleave(split_row(block))):
                dst[q:q + 8, p] = tile
    first_face = place[1] - halo
    scales = [jnp.where((first_face + j > 0) & (first_face + j < place[2]), 0.25 * time_step, 0.0)
              for j in range(total)]
    level = lax.broadcasted_iota(jnp.int32, (levels, LANES), 0)
    src, dst = (h0, u0, v0), (h1, u1, v1)
    for step in range(STEPS):
        h, u, v = src
        lo, hi = step, total - step
        for j in range(lo, hi):
            for p in range(parts):
                hp = h[j, p]
                acc = hp
                span = 1
                while span < levels:
                    moved = pltpu.roll(acc, levels - span, 0)
                    acc = acc + jnp.where(level < levels - span, moved, 0.0)
                    span *= 2
                geo[j, p] = gravity * acc
                inv_ref[step, j, p] = (1.0 / 12.0) / jnp.maximum(hp, mass_floor)

        def south_flux(j):
            return [scales[j] * (v[j - 1, p] + v[j, p]) * (h[j - 1, p] + h[j, p]) for p in range(parts)]

        def finish(j, tiles, moved):
            dst[0][j, 0] = tiles[0] + moved
            for p in range(1, parts):
                dst[0][j, p] = tiles[p]

        flux_north = south_flux(lo + 1)
        pending = []
        for j in range(lo + 1, hi - 1):
            hj, uj, vj, gj = ([f[j, p] for p in range(parts)] for f in (h, u, v, geo))
            hj.append(after(hj[0]))
            uj.append(after(uj[0]))
            gj = [before(gj[-1]), *gj, after(gj[0])]
            flux = south_flux(j + 1)
            east = [(0.25 * time_step) * (uj[p] + uj[p + 1]) * (hj[p] + hj[p + 1]) for p in range(parts)]
            tiles = [hj[0] - (east[0] + (flux[0] - flux_north[0]))]
            tiles += [hj[p] - ((east[p] - east[p - 1]) + (flux[p] - flux_north[p])) for p in range(1, parts)]
            pending.append((j, tiles, before(east[-1])))
            for p in range(parts):
                east_ref[step, j, p] = east[p]
                south_ref[step, j, p] = flux_north[p]
                slope_x = gj[p + 2] - gj[p]
                slope_y = geo[j + 1, p] - geo[j - 1, p]
                dst[1][j, p] = uj[p] + time_step * (coriolis * vj[p] - 0.5 * slope_x)
                dst[2][j, p] = vj[p] - time_step * (coriolis * uj[p] + 0.5 * slope_y)
            flux_north = flux
            if len(pending) > DELAY:
                finish(*pending.pop(0))
        for one in pending:
            finish(*one)
        for p in range(parts):
            south_ref[step, hi - 1, p] = flux_north[p]
        src, dst = dst, src
    block = h_out.shape[0]
    for out, field in zip((h_out, u_out, v_out), src):
        for k in range(block):
            mine = pl.ds(place[0] * block + k, 1)
            for q in range(0, rows, 8):
                tiles = restore([
                    jnp.concatenate([field[halo + q + i, p, mine, :] for i in range(8)], 0) for p in range(parts)])
                for p, tile in enumerate(tiles):
                    out[k, q:q + 8, p * LANES:(p + 1) * LANES] = tile


def tracer_kernel(place, counts, flags, north, top, bottom, south, inv_ref, east_ref, south_ref, *rest, first):
    out_ref, cur, even, odd = rest[-4:]
    slot = pl.program_id(0) + first
    parts = north.shape[2]
    halo = north.shape[1]
    half = top.shape[1]
    rows = 2 * half
    total = rows + 2 * halo
    group = place[0]
    start = jnp.int32(0)
    for g in range(counts.shape[0]):
        start = start + jnp.where(g < group, counts[g], 0)
    live = slot < counts[group]
    flag = flags[jnp.minimum(start + slot, flags.shape[0] - 1)]

    def entry(j):
        for source, base in ((south, halo + rows), (bottom, halo + half), (top, halo), (north, 0)):
            if j >= base:
                return [source[0, j - base, p] for p in range(parts)]

    def run(limited):
        def spread(buffer, j, tiles):
            for p in range(parts):
                buffer[j, p + 1] = tiles[p]
            buffer[j, 0] = before(tiles[-1])
            buffer[j, parts + 1] = after(tiles[0])
            buffer[j, parts + 2] = after(tiles[1])

        for j in range(total):
            spread(even, j, [t * inv_ref[0, j, p] for p, t in enumerate(entry(j))])

        def face(a2, a, b, b2, bounds):
            raw = 7.0 * (a + b) - (a2 + b2)
            if limited:
                raw = jnp.minimum(jnp.maximum(raw, jnp.minimum(*bounds)), jnp.maximum(*bounds))
            return raw

        def scaled(tiles):
            return [12.0 * t for t in tiles] if limited else [None] * len(tiles)

        src, dst = even, odd
        for step in range(STEPS):
            lo, hi = 2 * (step + 1), total - 2 * (step + 1)

            def south_terms(j, near, bounds):
                return [south_ref[step, j, p] * face(*(t[p] for t in near), tuple(t[p] for t in bounds))
                        for p in range(parts)]

            def load(j):
                return [src[j, p + 1] for p in range(parts)]

            def finish(j, tiles, moved):
                tiles = [tiles[0] + moved, *tiles[1:]]
                for p in range(parts):
                    cur[j, p] = tiles[p]
                if step + 1 < STEPS:
                    spread(dst, j, [t * inv_ref[step + 1, j, p] for p, t in enumerate(tiles)])

            near = [load(lo - 2 + b) for b in range(4)]
            bound = [scaled(near[1]), scaled(near[2])]
            term = south_terms(lo, near, bound)
            pending = []
            for j in range(lo, hi):
                near = [*near[1:], load(j + 2)]
                bound = [bound[1], scaled(near[2])]
                wide = [src[j, 0], *near[1], src[j, parts + 1], src[j, parts + 2]]
                limit = bound[0] + scaled([wide[parts + 1]])
                east = [east_ref[step, j, p] * face(*wide[p:p + 4], (limit[p], limit[p + 1]))
                        for p in range(parts)]
                moved = before(east[-1])
                following = south_terms(j + 1, near, bound)
                mass = entry(j) if step == 0 else [cur[j, p] for p in range(parts)]
                tiles = [mass[0] - (east[0] + (following[0] - term[0]))]
                tiles += [mass[p] - ((east[p] - east[p - 1]) + (following[p] - term[p])) for p in range(1, parts)]
                term = following
                pending.append((j, tiles, moved))
                if len(pending) > DELAY:
                    finish(*pending.pop(0))
            for one in pending:
                finish(*one)
            src, dst = dst, src
        for q in range(0, rows, 8):
            base = halo + q
            tiles = restore([cur[base:base + 8, p] for p in range(parts)])
            for p, tile in enumerate(tiles):
                out_ref[0, :, q:q + 8, p * LANES:(p + 1) * LANES] = jnp.swapaxes(tile, 0, 1)

    @pl.when(live & (flag > 0))
    def _():
        run(True)

    @pl.when(live & (flag <= 0))
    def _():
        run(False)

    @pl.when(jnp.logical_not(live))
    def _():
        out_ref[...] = jnp.zeros_like(out_ref)


def whole_block(shape):
    return pl.BlockSpec(shape, lambda *_: (0,) * len(shape))


def run_arrange(mass, first, count):
    _, levels, rows, columns = mass.shape
    batch = math.gcd(4, count, first)
    half = jax.ShapeDtypeStruct((count, rows // 2, columns // LANES, levels, LANES), jnp.float32)
    return pl.pallas_call(
        arrange_kernel,
        grid=(count // batch,),
        in_specs=[pl.BlockSpec((batch, levels, rows, columns), lambda i: (i + first // batch, 0, 0, 0))],
        out_specs=[pl.BlockSpec((batch, *half.shape[1:]), lambda i: (i, 0, 0, 0, 0))] * 2,
        out_shape=[half] * 2,
        name="arrange",
    )(mass)


def run_dynamics(place, own, north, south, level_block):
    planes, rows, columns = own.shape
    levels = planes // 3
    total = rows + 2 * HALO
    tiles = (total, columns // LANES, levels, LANES)
    flux = jax.ShapeDtypeStruct((STEPS, *tiles), jnp.float32)
    state = jax.ShapeDtypeStruct((level_block, rows, columns), jnp.float32)
    return pl.pallas_call(
        dynamics_kernel,
        grid_spec=pltpu.PrefetchScalarGridSpec(
            num_scalar_prefetch=1,
            grid=(1,),
            in_specs=[whole_block(own.shape), whole_block(north.shape), whole_block(south.shape)],
            out_specs=[pl.BlockSpec(memory_space=pltpu.VMEM)] * 3 + [whole_block(state.shape)] * 3,
            scratch_shapes=[pltpu.VMEM(tiles, jnp.float32)] * 7 + [pltpu.VMEM((3, levels, total, columns), jnp.float32)],
        ),
        out_shape=[flux] * 3 + [state] * 3,
        compiler_params=pltpu.CompilerParams(vmem_limit_bytes=48 << 20),
        name="dynamics",
    )(place, own, north, south)


def run_tracers(place, counts, flags, blocks, fluxes, first, out_shape, earlier):
    count, half, parts, levels, lanes = blocks[0].shape
    total = 2 * half + 2 * HALO
    in_specs = [pl.BlockSpec((1, *b.shape[1:]), lambda i, *_: (i, 0, 0, 0, 0)) for b in blocks]
    in_specs += [pl.BlockSpec(memory_space=pltpu.VMEM)] * len(fluxes)
    operands = [*blocks, *fluxes]
    aliases = {}
    if earlier is not None:
        aliases = {3 + len(operands): 0}
        in_specs.append(pl.BlockSpec(memory_space=pl.ANY))
        operands.append(earlier)
    wide = pltpu.VMEM((total, parts + 3, levels, lanes), jnp.float32)
    return pl.pallas_call(
        functools.partial(tracer_kernel, first=first),
        grid_spec=pltpu.PrefetchScalarGridSpec(
            num_scalar_prefetch=3,
            grid=(count,),
            in_specs=in_specs,
            out_specs=pl.BlockSpec((1, *out_shape[1:]), lambda i, *_: (i + first, 0, 0, 0)),
            scratch_shapes=[pltpu.VMEM((total, parts, levels, lanes), jnp.float32), wide, wide],
        ),
        out_shape=jax.ShapeDtypeStruct(out_shape, jnp.float32),
        input_output_aliases=aliases,
        compiler_params=pltpu.CompilerParams(vmem_limit_bytes=48 << 20),
        name="tracers",
    )(place, counts, flags, *operands)


def on_device(tracer_mass, layer_mass, zonal_wind, merid_wind, group_counts, limiter_flags):
    n_comp = lax.axis_size("comp")
    n_band = lax.axis_size("band")
    slots, levels, rows, _ = tracer_mass.shape
    level_block = layer_mass.shape[0]
    assert rows == 2 * HALO and levels == 8
    place = jnp.stack([
        lax.axis_index("comp"), lax.axis_index("band") * rows, jnp.int32(rows * n_band)
    ]).astype(jnp.int32)
    majors = n_comp // 2
    assert level_block == 1 and n_comp == levels and levels % 2 == 0

    def swap_minor(block):
        return lax.ppermute(block, "comp", [(i, i ^ 1) for i in range(n_comp)])

    def over_major(block):
        received = []
        for d in range(1, majors):
            received.append(lax.ppermute(block, "comp", [(i, (i + 2 * d) % n_comp) for i in range(n_comp)]))
        return lax.optimization_barrier(jnp.concatenate([block, *received], 0))

    chunk = slots // 2
    other_height = swap_minor(layer_mass)
    winds = over_major(jnp.concatenate([zonal_wind, merid_wind], 0))
    pair = lax.optimization_barrier(jnp.concatenate([layer_mass, other_height], 0))
    heights = over_major(pair)
    other_winds = swap_minor(winds)
    gathered = jnp.concatenate([winds, other_winds, heights], 0)
    from_north = band_shift(gathered[:, rows - HALO:], 1)
    from_south = band_shift(gathered[:, :HALO], -1)
    blocks = []
    for first in (0, chunk):
        top, bottom = run_arrange(tracer_mass, first, chunk)
        north = band_shift(bottom, 1)
        south = band_shift(top, -1)
        blocks.append((north, top, bottom, south))
    *fluxes, height, zonal, merid = run_dynamics(place, gathered, from_north, from_south, level_block)
    tracers = None
    for index, block in enumerate(blocks):
        tracers = run_tracers(place, group_counts, limiter_flags, block, fluxes, index * chunk,
                              tracer_mass.shape, tracers)
    return tracers, height, zonal, merid


def solution(mesh):
    placed = (
        P("comp", None, "band", None),
        P("comp", "band", None),
        P("comp", "band", None),
        P("comp", "band", None),
        P(),
        P(),
    )
    return jax.shard_map(
        on_device,
        mesh=mesh,
        in_specs=placed,
        out_specs=placed[:4],
        check_vma=False,
    )
```

time: 170 us -> 135 us (0.79)
  the two profiles are of different devices: /device:TPU:11 before, /device:TPU:14 now
where the time goes in v2:
time: 135 us
  Pallas kernels  69.7 us (52%)
  waiting for transfers between devices  33.5 us (25%)
  starting transfers between devices  26.1 us (19%)
  local copies, waits for them, and re-layouts  4.29 us (3%)
    pallas_call x2, Pallas kernels, run_tracers(): pl.pallas_call(functools.partial(tracer_kernel, first=first), grid_spec=p...  44.3 us
    ppermute x6, waiting for transfers between devices, band_shift(): return lax.ppermute(block, 'band', pairs)  20.8 us
    ppermute x6, starting transfers between devices, band_shift(): return lax.ppermute(block, 'band', pairs)  15.1 us
    pallas_call x2, Pallas kernels, run_arrange(): pl.pallas_call(arrange_kernel, grid=(count // batch,), in_specs=[pl.Block...  14.4 us
    pallas_call x1, Pallas kernels, run_dynamics(): pl.pallas_call(dynamics_kernel, grid_spec=pltpu.PrefetchScalarGridSpec(nu...  10.9 us
    ppermute x6, starting transfers between devices, over_major(): lax.ppermute(block, 'comp', [(i, (i + 2 * d) % n_comp) for i in range(n_c...  8.97 us
    ppermute x6, waiting for transfers between devices, over_major(): lax.ppermute(block, 'comp', [(i, (i + 2 * d) % n_comp) for i in range(n_c...  6.72 us
    ppermute x2, waiting for transfers between devices, swap_minor(): return lax.ppermute(block, 'comp', [(i, i ^ 1) for i in range(n_comp)])  5.95 us
  transfers between devices with their start and end apart: 14, of which 5 were waited for; matrix products, arithmetic and copies ran while one was open for 1% of the time, Pallas kernels for 35%

profile of v2, /device:TPU:14, one launch (start us, length us, event | category | flops | bytes accessed | tf_op | source)
XLA Modules:
  0.0 134.6 jit_solution(153115339442613902)
XLA Ops:
  0.6 0.6 collective-permute-start.6
  1.2 0.8 constant_dynamic-update-slice_fusion.1
  2.0 0.8 constant_dynamic-update-slice_fusion
  2.8 0.4 collective-permute-start.4
  3.2 2.6 %collective-permute-start.3 = (f32[2,16,512]{2,1,0:T(8,128)S(1)}, f32[2,16,512]{2,1,0:T(8,128)S(1)}, u32[]{:S(2)}, u32[]{:S(2)}) collective-permute-start(f32[2,16,512]{2,1,0:T(8,128)S(1)} %get-tuple-element.26), channel_id=1, source_target_pairs={{0,4},{1,5},{2,6},{3,7},{4,0},{5,1},{6,2},{7,3},{8,12},{9,13},{10,... | collective-permute-start | bytes 196616 | tf_op jit(solution)/shard_map/ppermute | solution.py:385
  5.8 2.5 %collective-permute-start.2 = (f32[2,16,512]{2,1,0:T(8,128)S(1)}, f32[2,16,512]{2,1,0:T(8,128)S(1)}, u32[]{:S(2)}, u32[]{:S(2)}) collective-permute-start(f32[2,16,512]{2,1,0:T(8,128)S(1)} %get-tuple-element.26), channel_id=1, source_target_pairs={{0,2},{1,3},{2,4},{3,5},{4,6},{5,7},{6,0},{7,1},{8,10},{9,11},{10,... | collective-permute-start | bytes 196616 | tf_op jit(solution)/shard_map/ppermute | solution.py:385
  8.3 7.2 %arrange.3 = (f32[12,8,4,8,128]{4,3,2,1,0:T(8,128)}, f32[12,8,4,8,128]{4,3,2,1,0:T(8,128)}) custom-call(f32[24,8,16,512]{3,2,1,0:T(8,128)} %mass.3), custom_call_target="tpu_custom_call" | custom-call | tf_op jit(solution)/shard_map/arrange/pallas_call | solution.py:307
  15.5 0.0 copy-start.4
  15.5 0.0 copy-start.8
  15.5 2.0 %collective-permute-start.12 = (f32[12,8,4,8,128]{4,3,2,1,0:T(8,128)}, f32[12,8,4,8,128]{4,3,2,1,0:T(8,128)}, u32[]{:S(2)}, u32[]{:S(2)}) collective-permute-start(f32[12,8,4,8,128]{4,3,2,1,0:T(8,128)} %get-tuple-element.19.bottom), channel_id=1, source_target_pairs={{0,8},{8,16},{16,24},{1,9},{9,17},{17,25},{2,10},{10,18},{18,26},{... | collective-permute-start | bytes 4718600 | tf_op jit(solution)/shard_map/ppermute | solution.py:28
  17.5 7.2 %arrange.2 = (f32[12,8,4,8,128]{4,3,2,1,0:T(8,128)}, f32[12,8,4,8,128]{4,3,2,1,0:T(8,128)}) custom-call(f32[24,8,16,512]{3,2,1,0:T(8,128)} %mass.3), custom_call_target="tpu_custom_call" | custom-call | tf_op jit(solution)/shard_map/arrange/pallas_call | solution.py:307
  24.8 0.0 collective-permute-done.6
  24.8 0.0 copy-done.4
  24.8 3.6 %collective-permute-start.13 = (f32[12,8,4,8,128]{4,3,2,1,0:T(8,128)S(1)}, f32[12,8,4,8,128]{4,3,2,1,0:T(8,128)}, u32[]{:S(2)}, u32[]{:S(2)}) collective-permute-start(f32[12,8,4,8,128]{4,3,2,1,0:T(8,128)S(1)} %copy-done.4), channel_id=1, source_target_pairs={{8,0},{16,8},{24,16},{9,1},{17,9},{25,17},{10,2},{18,10},{26,18},{... | collective-permute-start | bytes 4718600 | tf_op jit(solution)/shard_map/ppermute | solution.py:28
  28.4 0.0 copy-done.8
  28.4 0.0 collective-permute-done.2
  28.5 0.1 collective-permute-start.9
  28.5 0.0 collective-permute-done.4
  28.5 1.9 %collective-permute-start = (f32[12,8,4,8,128]{4,3,2,1,0:T(8,128)}, f32[12,8,4,8,128]{4,3,2,1,0:T(8,128)}, u32[]{:S(2)}, u32[]{:S(2)}) collective-permute-start(f32[12,8,4,8,128]{4,3,2,1,0:T(8,128)} %get-tuple-element.14.bottom), channel_id=1, source_target_pairs={{0,8},{8,16},{16,24},{1,9},{9,17},{17,25},{2,10},{10,18},{18,26},{... | collective-permute-start | bytes 4718600 | tf_op jit(solution)/shard_map/ppermute | solution.py:28
  30.5 0.0 collective-permute-done.3
  30.5 3.6 %collective-permute-start.1 = (f32[12,8,4,8,128]{4,3,2,1,0:T(8,128)}, f32[12,8,4,8,128]{4,3,2,1,0:T(8,128)}, u32[]{:S(2)}, u32[]{:S(2)}) collective-permute-start(f32[12,8,4,8,128]{4,3,2,1,0:T(8,128)} %get-tuple-element.15.top), channel_id=1, source_target_pairs={{8,0},{16,8},{24,16},{9,1},{17,9},{25,17},{10,2},{18,10},{26,18},{... | collective-permute-start | bytes 4718600 | tf_op jit(solution)/shard_map/ppermute | solution.py:28
  34.1 0.0 collective-permute-done.9
  34.1 1.5 %collective-permute-start.8 = (f32[2,16,512]{2,1,0:T(8,128)S(1)}, f32[2,16,512]{2,1,0:T(8,128)S(1)}, u32[]{:S(2)}, u32[]{:S(2)}) collective-permute-start(f32[2,16,512]{2,1,0:T(8,128)S(1)} %pad_maximum_fusion.2), channel_id=1, source_target_pairs={{0,4},{1,5},{2,6},{3,7},{4,0},{5,1},{6,2},{7,3},{8,12},{9,13},{10,... | collective-permute-start | bytes 196616 | tf_op jit(solution)/shard_map/ppermute | solution.py:385
  35.7 3.8 %collective-permute-done.8 = f32[2,16,512]{2,1,0:T(8,128)S(1)} collective-permute-done((f32[2,16,512]{2,1,0:T(8,128)S(1)}, f32[2,16,512]{2,1,0:T(8,128)S(1)}, u32[]{:S(2)}, u32[]{:S(2)}) %collective-permute-start.8) | collective-permute-done | bytes 65568 | tf_op jit(solution)/shard_map/ppermute | solution.py:385
  39.5 1.9 %collective-permute-start.7 = (f32[2,16,512]{2,1,0:T(8,128)S(1)}, f32[2,16,512]{2,1,0:T(8,128)S(1)}, u32[]{:S(2)}, u32[]{:S(2)}) collective-permute-start(f32[2,16,512]{2,1,0:T(8,128)S(1)} %pad_maximum_fusion.2), channel_id=1, source_target_pairs={{0,2},{1,3},{2,4},{3,5},{4,6},{5,7},{6,0},{7,1},{8,10},{9,11},{10,... | collective-permute-start | bytes 196616 | tf_op jit(solution)/shard_map/ppermute | solution.py:385
  41.4 2.9 %collective-permute-done.7 = f32[2,16,512]{2,1,0:T(8,128)S(1)} collective-permute-done((f32[2,16,512]{2,1,0:T(8,128)S(1)}, f32[2,16,512]{2,1,0:T(8,128)S(1)}, u32[]{:S(2)}, u32[]{:S(2)}) %collective-permute-start.7) | collective-permute-done | bytes 65568 | tf_op jit(solution)/shard_map/ppermute | solution.py:385
  44.3 1.5 %collective-permute-start.5 = (f32[8,16,512]{2,1,0:T(8,128)S(1)}, f32[8,16,512]{2,1,0:T(8,128)S(1)}, u32[]{:S(2)}, u32[]{:S(2)}) collective-permute-start(f32[8,16,512]{2,1,0:T(8,128)S(1)} %constant_dynamic-update-slice_fusion.2), channel_id=1, source_target_pairs={{0,1},{1,0},{2,3},{3,2},{4,5},{5,4},{6,7},{7,6},{8,9},{9,8},{10,11... | collective-permute-start | bytes 786440 | tf_op jit(solution)/shard_map/ppermute | solution.py:380
  45.8 6.0 %collective-permute-done.5 = f32[8,16,512]{2,1,0:T(8,128)S(1)} collective-permute-done((f32[8,16,512]{2,1,0:T(8,128)S(1)}, f32[8,16,512]{2,1,0:T(8,128)S(1)}, u32[]{:S(2)}, u32[]{:S(2)}) %collective-permute-start.5) | collective-permute-done | bytes 262176 | tf_op jit(solution)/shard_map/ppermute | solution.py:380
  51.7 0.1 pad_maximum_fusion.own
  51.8 0.0 copy-start.6
  51.8 0.0 copy-start.7
  51.8 0.1 fusion
  51.9 1.9 %collective-permute-start.11 = (f32[24,8,512]{2,1,0:T(8,128)S(1)}, f32[24,8,512]{2,1,0:T(8,128)S(1)}, u32[]{:S(2)}, u32[]{:S(2)}) collective-permute-start(f32[24,8,512]{2,1,0:T(8,128)S(1)} %get-tuple-element.24), channel_id=1, source_target_pairs={{8,0},{16,8},{24,16},{9,1},{17,9},{25,17},{10,2},{18,10},{26,18},{... | collective-permute-start | bytes 1179656 | tf_op jit(solution)/shard_map/ppermute | solution.py:28
  53.8 13.6 %collective-permute-done.11.south = f32[24,8,512]{2,1,0:T(8,128)S(1)} collective-permute-done((f32[24,8,512]{2,1,0:T(8,128)S(1)}, f32[24,8,512]{2,1,0:T(8,128)S(1)}, u32[]{:S(2)}, u32[]{:S(2)}) %collective-permute-start.11) | collective-permute-done | bytes 393248 | tf_op jit(solution)/shard_map/ppermute | solution.py:28
  67.4 1.9 %collective-permute-start.10 = (f32[24,8,512]{2,1,0:T(8,128)S(1)}, f32[24,8,512]{2,1,0:T(8,128)S(1)}, u32[]{:S(2)}, u32[]{:S(2)}) collective-permute-start(f32[24,8,512]{2,1,0:T(8,128)S(1)} %get-tuple-element.25), channel_id=1, source_target_pairs={{0,8},{8,16},{16,24},{1,9},{9,17},{17,25},{2,10},{10,18},{18,26},{... | collective-permute-start | bytes 1179656 | tf_op jit(solution)/shard_map/ppermute | solution.py:28
  69.3 0.0 copy-start.5
  69.3 0.1 pad_add_fusion.place
  69.4 7.2 %collective-permute-done.10.north = f32[24,8,512]{2,1,0:T(8,128)S(1)} collective-permute-done((f32[24,8,512]{2,1,0:T(8,128)S(1)}, f32[24,8,512]{2,1,0:T(8,128)S(1)}, u32[]{:S(2)}, u32[]{:S(2)}) %collective-permute-start.10) | collective-permute-done | bytes 393248 | tf_op jit(solution)/shard_map/ppermute | solution.py:28
  76.7 10.9 %dynamics.1 = (f32[4,32,4,8,128]{4,3,2,1,0:T(8,128)S(1)}, f32[4,32,4,8,128]{4,3,2,1,0:T(8,128)S(1)}, f32[4,32,4,8,128]{4,3,2,1,0:T(8,128)}, f32[1,16,512]{2,1,0:...) custom-call(s32[3]{0:T(128)S(1)} %pad_add_fusion.place, f32[24,16,512]{2,1,0:T(8,128)S(1)} %pad_maximum_fusion.own, ...), custom_call_target="tpu_custom_call" | custom-call | tf_op jit(solution)/shard_map/dynamics/pallas_call | solution.py:324
  87.5 0.0 copy-start
  87.5 1.3 copy-done
  88.9 0.0 copy-start.1
  88.9 1.3 %copy-done.1 = f32[4,32,4,8,128]{4,3,2,1,0:T(8,128)} copy-done((f32[4,32,4,8,128]{4,3,2,1,0:T(8,128)}, f32[4,32,4,8,128]{4,3,2,1,0:T(8,128)S(1)}, u32[]{:S(2)}) %copy-start.1) | copy-done | bytes 2097176
  90.2 0.0 collective-permute-done.12.north
  90.2 0.0 collective-permute-done.13.south
  90.2 0.0 copy-done.6
  90.2 0.0 copy-done.7
  90.2 0.0 copy-done.5
  90.2 0.0 copy-start.2
  90.2 0.0 copy-start.3
  90.3 22.3 %tracers.2.rest_0_ = f32[24,8,16,512]{3,2,1,0:T(8,128)} custom-call(s32[3]{0:T(128)S(1)} %pad_add_fusion.place, s32[8]{0:T(128)S(1)} %copy-done.6, s32[96]{0:T(128)S(1)} %copy-done.7, f32[12,8,4,8,128]{4,3,2,1,0:T(8,128)} %collective-permute-done.12.north, f32[12,8,4,8,128]{4,3,2,1,0:T(8,128)S(1)} %copy-done.4, f32[12,8,4,8,128]{4,3,2,1,0:T(8,128)S(1)} %copy-done.5, ...), custom_call_target="tpu_custom_call" | custom-call | tf_op jit(solution)/shard_map/tracers/pallas_call | solution.py:351
  112.6 0.0 collective-permute-done.north
  112.6 0.0 collective-permute-done.1.south
  112.6 0.0 copy-done.2
  112.6 0.0 copy-done.3
  112.6 22.0 %tracers.3 = f32[24,8,16,512]{3,2,1,0:T(8,128)} custom-call(s32[3]{0:T(128)S(1)} %pad_add_fusion.place, s32[8]{0:T(128)S(1)} %copy-done.6, s32[96]{0:T(128)S(1)} %copy-done.7, f32[12,8,4,8,128]{4,3,2,1,0:T(8,128)} %collective-permute-done.north, f32[12,8,4,8,128]{4,3,2,1,0:T(8,128)S(1)} %copy-done.2, ...), custom_call_target="tpu_custom_call", output_to_operand_aliasing={{}: (10, {})} | custom-call | tf_op jit(solution)/shard_map/tracers/pallas_call | solution.py:351
  (5 shorter events, 0.0 us)
Async XLA Ops:
  0.6 24.1 %collective-permute-start.6 = (f32[1,16,512]{2,1,0:T(8,128)}, f32[1,16,512]{2,1,0:T(8,128)S(1)}, u32[]{:S(2)}, u32[]{:S(2)}) collective-permute-start(f32[1,16,512]{2,1,0:T(8,128)} %param.7), channel_id=1, source_target_pairs={{0,1},{1,0},{2,3},{3,2},{4,5},{5,4},{6,7},{7,6},{8,9},{9,8},{10,11... | collective-permute-start | bytes 98312 | tf_op jit(solution)/shard_map/ppermute | solution.py:380
  2.8 25.8 %collective-permute-start.4 = (f32[2,16,512]{2,1,0:T(8,128)S(1)}, f32[2,16,512]{2,1,0:T(8,128)S(1)}, u32[]{:S(2)}, u32[]{:S(2)}) collective-permute-start(f32[2,16,512]{2,1,0:T(8,128)S(1)} %get-tuple-element.26), channel_id=1, source_target_pairs={{0,6},{1,7},{2,0},{3,1},{4,2},{5,3},{6,4},{7,5},{8,14},{9,15},{10,... | collective-permute-start | bytes 196616 | tf_op jit(solution)/shard_map/ppermute | solution.py:385
  3.2 27.3 %collective-permute-start.3 = (f32[2,16,512]{2,1,0:T(8,128)S(1)}, f32[2,16,512]{2,1,0:T(8,128)S(1)}, u32[]{:S(2)}, u32[]{:S(2)}) collective-permute-start(f32[2,16,512]{2,1,0:T(8,128)S(1)} %get-tuple-element.26), channel_id=1, source_target_pairs={{0,4},{1,5},{2,6},{3,7},{4,0},{5,1},{6,2},{7,3},{8,12},{9,13},{10,... | collective-permute-start | bytes 196616 | tf_op jit(solution)/shard_map/ppermute | solution.py:385
  5.8 22.6 %collective-permute-start.2 = (f32[2,16,512]{2,1,0:T(8,128)S(1)}, f32[2,16,512]{2,1,0:T(8,128)S(1)}, u32[]{:S(2)}, u32[]{:S(2)}) collective-permute-start(f32[2,16,512]{2,1,0:T(8,128)S(1)} %get-tuple-element.26), channel_id=1, source_target_pairs={{0,2},{1,3},{2,4},{3,5},{4,6},{5,7},{6,0},{7,1},{8,10},{9,11},{10,... | collective-permute-start | bytes 196616 | tf_op jit(solution)/shard_map/ppermute | solution.py:385
  15.5 9.3 %copy-start.4 = (f32[12,8,4,8,128]{4,3,2,1,0:T(8,128)S(1)}, f32[12,8,4,8,128]{4,3,2,1,0:T(8,128)}, u32[]{:S(2)}) copy-start(f32[12,8,4,8,128]{4,3,2,1,0:T(8,128)} %get-tuple-element.20.top) | copy-start | bytes 4718596
  15.5 12.9 %copy-start.8 = (f32[1,16,512]{2,1,0:T(8,128)S(1)}, f32[1,16,512]{2,1,0:T(8,128)}, u32[]{:S(2)}) copy-start(f32[1,16,512]{2,1,0:T(8,128)} %param.7) | copy-start | bytes 98308
  15.5 74.7 %collective-permute-start.12 = (f32[12,8,4,8,128]{4,3,2,1,0:T(8,128)}, f32[12,8,4,8,128]{4,3,2,1,0:T(8,128)}, u32[]{:S(2)}, u32[]{:S(2)}) collective-permute-start(f32[12,8,4,8,128]{4,3,2,1,0:T(8,128)} %get-tuple-element.19.bottom), channel_id=1, source_target_pairs={{0,8},{8,16},{16,24},{1,9},{9,17},{17,25},{2,10},{10,18},{18,26},{... | collective-permute-start | bytes 4718600 | tf_op jit(solution)/shard_map/ppermute | solution.py:28
  24.8 65.4 %collective-permute-start.13 = (f32[12,8,4,8,128]{4,3,2,1,0:T(8,128)S(1)}, f32[12,8,4,8,128]{4,3,2,1,0:T(8,128)}, u32[]{:S(2)}, u32[]{:S(2)}) collective-permute-start(f32[12,8,4,8,128]{4,3,2,1,0:T(8,128)S(1)} %copy-done.4), channel_id=1, source_target_pairs={{8,0},{16,8},{24,16},{9,1},{17,9},{25,17},{10,2},{18,10},{26,18},{... | collective-permute-start | bytes 4718600 | tf_op jit(solution)/shard_map/ppermute | solution.py:28
  28.5 5.7 %collective-permute-start.9 = (f32[2,16,512]{2,1,0:T(8,128)S(1)}, f32[2,16,512]{2,1,0:T(8,128)S(1)}, u32[]{:S(2)}, u32[]{:S(2)}) collective-permute-start(f32[2,16,512]{2,1,0:T(8,128)S(1)} %pad_maximum_fusion.2), channel_id=1, source_target_pairs={{0,6},{1,7},{2,0},{3,1},{4,2},{5,3},{6,4},{7,5},{8,14},{9,15},{10,... | collective-permute-start | bytes 196616 | tf_op jit(solution)/shard_map/ppermute | solution.py:385
  28.5 84.1 %collective-permute-start = (f32[12,8,4,8,128]{4,3,2,1,0:T(8,128)}, f32[12,8,4,8,128]{4,3,2,1,0:T(8,128)}, u32[]{:S(2)}, u32[]{:S(2)}) collective-permute-start(f32[12,8,4,8,128]{4,3,2,1,0:T(8,128)} %get-tuple-element.14.bottom), channel_id=1, source_target_pairs={{0,8},{8,16},{16,24},{1,9},{9,17},{17,25},{2,10},{10,18},{18,26},{... | collective-permute-start | bytes 4718600 | tf_op jit(solution)/shard_map/ppermute | solution.py:28
  30.5 82.1 %collective-permute-start.1 = (f32[12,8,4,8,128]{4,3,2,1,0:T(8,128)}, f32[12,8,4,8,128]{4,3,2,1,0:T(8,128)}, u32[]{:S(2)}, u32[]{:S(2)}) collective-permute-start(f32[12,8,4,8,128]{4,3,2,1,0:T(8,128)} %get-tuple-element.15.top), channel_id=1, source_target_pairs={{8,0},{16,8},{24,16},{9,1},{17,9},{25,17},{10,2},{18,10},{26,18},{... | collective-permute-start | bytes 4718600 | tf_op jit(solution)/shard_map/ppermute | solution.py:28
  34.1 5.3 %collective-permute-start.8 = (f32[2,16,512]{2,1,0:T(8,128)S(1)}, f32[2,16,512]{2,1,0:T(8,128)S(1)}, u32[]{:S(2)}, u32[]{:S(2)}) collective-permute-start(f32[2,16,512]{2,1,0:T(8,128)S(1)} %pad_maximum_fusion.2), channel_id=1, source_target_pairs={{0,4},{1,5},{2,6},{3,7},{4,0},{5,1},{6,2},{7,3},{8,12},{9,13},{10,... | collective-permute-start | bytes 196616 | tf_op jit(solution)/shard_map/ppermute | solution.py:385
  39.5 4.8 %collective-permute-start.7 = (f32[2,16,512]{2,1,0:T(8,128)S(1)}, f32[2,16,512]{2,1,0:T(8,128)S(1)}, u32[]{:S(2)}, u32[]{:S(2)}) collective-permute-start(f32[2,16,512]{2,1,0:T(8,128)S(1)} %pad_maximum_fusion.2), channel_id=1, source_target_pairs={{0,2},{1,3},{2,4},{3,5},{4,6},{5,7},{6,0},{7,1},{8,10},{9,11},{10,... | collective-permute-start | bytes 196616 | tf_op jit(solution)/shard_map/ppermute | solution.py:385
  44.3 7.5 %collective-permute-start.5 = (f32[8,16,512]{2,1,0:T(8,128)S(1)}, f32[8,16,512]{2,1,0:T(8,128)S(1)}, u32[]{:S(2)}, u32[]{:S(2)}) collective-permute-start(f32[8,16,512]{2,1,0:T(8,128)S(1)} %constant_dynamic-update-slice_fusion.2), channel_id=1, source_target_pairs={{0,1},{1,0},{2,3},{3,2},{4,5},{5,4},{6,7},{7,6},{8,9},{9,8},{10,11... | collective-permute-start | bytes 786440 | tf_op jit(solution)/shard_map/ppermute | solution.py:380
  51.8 38.4 %copy-start.6 = (s32[8]{0:T(128)S(1)}, s32[8]{0:T(128)}, u32[]{:S(2)}) copy-start(s32[8]{0:T(128)} %counts.3) | copy-start | bytes 100
  51.8 38.4 %copy-start.7 = (s32[96]{0:T(128)S(1)}, s32[96]{0:T(128)}, u32[]{:S(2)}) copy-start(s32[96]{0:T(128)} %flags.3) | copy-start | bytes 1156
  51.9 15.5 %collective-permute-start.11 = (f32[24,8,512]{2,1,0:T(8,128)S(1)}, f32[24,8,512]{2,1,0:T(8,128)S(1)}, u32[]{:S(2)}, u32[]{:S(2)}) collective-permute-start(f32[24,8,512]{2,1,0:T(8,128)S(1)} %get-tuple-element.24), channel_id=1, source_target_pairs={{8,0},{16,8},{24,16},{9,1},{17,9},{25,17},{10,2},{18,10},{26,18},{... | collective-permute-start | bytes 1179656 | tf_op jit(solution)/shard_map/ppermute | solution.py:28
  67.4 9.3 %collective-permute-start.10 = (f32[24,8,512]{2,1,0:T(8,128)S(1)}, f32[24,8,512]{2,1,0:T(8,128)S(1)}, u32[]{:S(2)}, u32[]{:S(2)}) collective-permute-start(f32[24,8,512]{2,1,0:T(8,128)S(1)} %get-tuple-element.25), channel_id=1, source_target_pairs={{0,8},{8,16},{16,24},{1,9},{9,17},{17,25},{2,10},{10,18},{18,26},{... | collective-permute-start | bytes 1179656 | tf_op jit(solution)/shard_map/ppermute | solution.py:28
  69.3 20.9 %copy-start.5 = (f32[12,8,4,8,128]{4,3,2,1,0:T(8,128)S(1)}, f32[12,8,4,8,128]{4,3,2,1,0:T(8,128)}, u32[]{:S(2)}) copy-start(f32[12,8,4,8,128]{4,3,2,1,0:T(8,128)} %get-tuple-element.19.bottom) | copy-start | bytes 4718596
  87.5 1.3 copy-start
  88.9 1.4 %copy-start.1 = (f32[4,32,4,8,128]{4,3,2,1,0:T(8,128)}, f32[4,32,4,8,128]{4,3,2,1,0:T(8,128)S(1)}, u32[]{:S(2)}) copy-start(f32[4,32,4,8,128]{4,3,2,1,0:T(8,128)S(1)} %get-tuple-element.17.east_ref) | copy-start | bytes 6291460
  90.2 22.4 %copy-start.2 = (f32[12,8,4,8,128]{4,3,2,1,0:T(8,128)S(1)}, f32[12,8,4,8,128]{4,3,2,1,0:T(8,128)}, u32[]{:S(2)}) copy-start(f32[12,8,4,8,128]{4,3,2,1,0:T(8,128)} %get-tuple-element.15.top) | copy-start | bytes 4718596
  90.2 22.4 %copy-start.3 = (f32[12,8,4,8,128]{4,3,2,1,0:T(8,128)S(1)}, f32[12,8,4,8,128]{4,3,2,1,0:T(8,128)}, u32[]{:S(2)}) copy-start(f32[12,8,4,8,128]{4,3,2,1,0:T(8,128)} %get-tuple-element.14.bottom) | copy-start | bytes 4718596

commit v3 on v2

--- a/solution.py
+++ b/solution.py
@@ -103,19 +103,16 @@
     rows = mass.shape[2]
     half = rows // 2
 
-    def one(t, carry):
+    for t in range(mass.shape[0]):
         for out, base in ((top, 0), (bottom, half)):
             for q in range(0, half, 8):
                 block = jnp.swapaxes(mass[t, :, base + q:base + q + 8], 0, 1)
                 for p, tile in enumerate(interleave(split_row(block))):
                     out[t, q:q + 8, p] = tile
-        return carry
-
-    lax.fori_loop(0, mass.shape[0], one, 0)
-
-
-def dynamics_kernel(place, own, north, south, inv_ref, east_ref, south_ref,
-                    h_out, u_out, v_out, h0, u0, v0, h1, u1, v1, geo, stage):
+
+
+def run_dynamics(place, own, north, south, h_out, u_out, v_out, inv_ref, east_ref, south_ref,
+                 h0, u0, v0, h1, u1, v1, geo, stage):
     planes, rows, columns = own.shape
     parts = columns // LANES
     halo = north.shape[1]
@@ -137,8 +134,9 @@
     src, dst = (h0, u0, v0), (h1, u1, v1)
     for step in range(STEPS):
         h, u, v = src
-        lo, hi = step, total - step
-        for j in range(lo, hi):
+        lo, hi = 2 * (step + 1), total - 2 * (step + 1)
+
+        def column(j):
             for p in range(parts):
                 hp = h[j, p]
                 acc = hp
@@ -158,9 +156,12 @@
             for p in range(1, parts):
                 dst[0][j, p] = tiles[p]
 
-        flux_north = south_flux(lo + 1)
+        for j in range(lo - 2, lo + 1):
+            column(j)
+        flux_north = south_flux(lo)
         pending = []
-        for j in range(lo + 1, hi - 1):
+        for j in range(lo, hi):
+            column(j + 1)
             hj, uj, vj, gj = ([f[j, p] for p in range(parts)] for f in (h, u, v, geo))
             hj.append(after(hj[0]))
             uj.append(after(uj[0]))
@@ -183,7 +184,8 @@
         for one in pending:
             finish(*one)
         for p in range(parts):
-            south_ref[step, hi - 1, p] = flux_north[p]
+            south_ref[step, hi, p] = flux_north[p]
+        column(hi + 1)
         src, dst = dst, src
     block = h_out.shape[0]
     for out, field in zip((h_out, u_out, v_out), src):
@@ -196,9 +198,29 @@
                     out[k, q:q + 8, p * LANES:(p + 1) * LANES] = tile
 
 
-def tracer_kernel(place, counts, flags, north, top, bottom, south, inv_ref, east_ref, south_ref, *rest, first):
-    out_ref, cur, even, odd = rest[-4:]
-    slot = pl.program_id(0) + first
+def tracer_kernel(place, counts, flags, *refs, first, lead):
+    step_id = pl.program_id(0)
+    if lead:
+        planes, (north, top, bottom, south, out_ref), refs = refs[:3], refs[3:8], refs[8:]
+        states, kept, refs = refs[:3], refs[3:6], refs[6:]
+    else:
+        kept, (north, top, bottom, south, _, out_ref), refs = refs[:3], refs[3:9], refs[9:]
+    (cur, even, odd), fluxes, done, work = refs[:3], refs[3:6], refs[6], refs[7:]
+    pairs = zip(fluxes, kept) if lead else zip(kept, fluxes)
+    copies = [pltpu.make_async_copy(a, b, done.at[i]) for i, (a, b) in enumerate(pairs)]
+
+    @pl.when(step_id == 0)
+    def _():
+        if lead:
+            run_dynamics(place, *planes, *states, *fluxes, *work)
+        for copy in copies:
+            copy.start()
+        if not lead:
+            for copy in copies:
+                copy.wait()
+
+    inv_ref, east_ref, south_ref = fluxes
+    slot = step_id + first
     parts = north.shape[2]
     halo = north.shape[1]
     half = top.shape[1]
@@ -295,6 +317,12 @@
     def _():
         out_ref[...] = jnp.zeros_like(out_ref)
 
+    if lead:
+        @pl.when(step_id == pl.num_programs(0) - 1)
+        def _():
+            for copy in copies:
+                copy.wait()
+
 
 def whole_block(shape):
     return pl.BlockSpec(shape, lambda *_: (0,) * len(shape))
@@ -314,52 +342,45 @@
     )(mass)
 
 
-def run_dynamics(place, own, north, south, level_block):
-    planes, rows, columns = own.shape
-    levels = planes // 3
+def run_tracers(place, counts, flags, blocks, planes, kept, earlier, first, out_shape):
+    lead = planes is not None
+    count, half, parts, levels, lanes = blocks[0].shape
+    rows, columns = 2 * half, parts * lanes
     total = rows + 2 * HALO
-    tiles = (total, columns // LANES, levels, LANES)
-    flux = jax.ShapeDtypeStruct((STEPS, *tiles), jnp.float32)
-    state = jax.ShapeDtypeStruct((level_block, rows, columns), jnp.float32)
+    tiles = (total, parts, levels, lanes)
+    wide = (total, parts + 3, levels, lanes)
+    anywhere = pl.BlockSpec(memory_space=pl.ANY)
+    block_specs = [pl.BlockSpec((1, *b.shape[1:]), lambda i, *_: (i, 0, 0, 0, 0)) for b in blocks]
+    out_specs = [pl.BlockSpec((1, *out_shape[1:]), lambda i, *_: (i + first, 0, 0, 0))]
+    out_types = [jax.ShapeDtypeStruct(out_shape, jnp.float32)]
+    scratch = [tiles, wide, wide] + [(STEPS, *tiles)] * 3
+    scratch = [pltpu.VMEM(s, jnp.float32) for s in scratch] + [pltpu.SemaphoreType.DMA((3,))]
+    aliases = {}
+    if lead:
+        state = (1, rows, columns)
+        operands = [*planes, *blocks]
+        in_specs = [whole_block(p.shape) for p in planes] + block_specs
+        out_specs += [whole_block(state)] * 3 + [anywhere] * 3
+        out_types += [jax.ShapeDtypeStruct(state, jnp.float32)] * 3
+        out_types += [jax.ShapeDtypeStruct((STEPS, *tiles), jnp.float32)] * 3
+        work = [tiles] * 7 + [(3, levels, total, columns)]
+        scratch += [pltpu.VMEM(s, jnp.float32) for s in work]
+    else:
+        operands = [*kept, *blocks, earlier]
+        in_specs = [anywhere] * 3 + block_specs + [anywhere]
+        aliases = {2 + len(operands): 0}
     return pl.pallas_call(
-        dynamics_kernel,
-        grid_spec=pltpu.PrefetchScalarGridSpec(
-            num_scalar_prefetch=1,
-            grid=(1,),
-            in_specs=[whole_block(own.shape), whole_block(north.shape), whole_block(south.shape)],
-            out_specs=[pl.BlockSpec(memory_space=pltpu.VMEM)] * 3 + [whole_block(state.shape)] * 3,
-            scratch_shapes=[pltpu.VMEM(tiles, jnp.float32)] * 7 + [pltpu.VMEM((3, levels, total, columns), jnp.float32)],
-        ),
-        out_shape=[flux] * 3 + [state] * 3,
-        compiler_params=pltpu.CompilerParams(vmem_limit_bytes=48 << 20),
-        name="dynamics",
-    )(place, own, north, south)
-
-
-def run_tracers(place, counts, flags, blocks, fluxes, first, out_shape, earlier):
-    count, half, parts, levels, lanes = blocks[0].shape
-    total = 2 * half + 2 * HALO
-    in_specs = [pl.BlockSpec((1, *b.shape[1:]), lambda i, *_: (i, 0, 0, 0, 0)) for b in blocks]
-    in_specs += [pl.BlockSpec(memory_space=pltpu.VMEM)] * len(fluxes)
-    operands = [*blocks, *fluxes]
-    aliases = {}
-    if earlier is not None:
-        aliases = {3 + len(operands): 0}
-        in_specs.append(pl.BlockSpec(memory_space=pl.ANY))
-        operands.append(earlier)
-    wide = pltpu.VMEM((total, parts + 3, levels, lanes), jnp.float32)
-    return pl.pallas_call(
-        functools.partial(tracer_kernel, first=first),
+        functools.partial(tracer_kernel, first=first, lead=lead),
         grid_spec=pltpu.PrefetchScalarGridSpec(
             num_scalar_prefetch=3,
             grid=(count,),
             in_specs=in_specs,
-            out_specs=pl.BlockSpec((1, *out_shape[1:]), lambda i, *_: (i + first, 0, 0, 0)),
-            scratch_shapes=[pltpu.VMEM((total, parts, levels, lanes), jnp.float32), wide, wide],
+            out_specs=out_specs,
+            scratch_shapes=scratch,
         ),
-        out_shape=jax.ShapeDtypeStruct(out_shape, jnp.float32),
+        out_shape=out_types,
         input_output_aliases=aliases,
-        compiler_params=pltpu.CompilerParams(vmem_limit_bytes=48 << 20),
+        compiler_params=pltpu.CompilerParams(vmem_limit_bytes=52 << 20),
         name="tracers",
     )(place, counts, flags, *operands)
 
@@ -400,11 +421,11 @@
         north = band_shift(bottom, 1)
         south = band_shift(top, -1)
         blocks.append((north, top, bottom, south))
-    *fluxes, height, zonal, merid = run_dynamics(place, gathered, from_north, from_south, level_block)
-    tracers = None
-    for index, block in enumerate(blocks):
-        tracers = run_tracers(place, group_counts, limiter_flags, block, fluxes, index * chunk,
-                              tracer_mass.shape, tracers)
+    planes = (gathered, from_north, from_south)
+    earlier, height, zonal, merid, *kept = run_tracers(
+        place, group_counts, limiter_flags, blocks[0], planes, None, None, 0, tracer_mass.shape)
+    tracers, = run_tracers(
+        place, group_counts, limiter_flags, blocks[1], None, kept, earlier, chunk, tracer_mass.shape)
     return tracers, height, zonal, merid
 
 

time: 135 us -> 119 us (0.88)
  the two profiles are of different devices: /device:TPU:14 before, /device:TPU:11 now
where the time goes in v3:
time: 119 us; the launch traced here: 118 us
  Pallas kernels  64 us (54%)
  starting transfers between devices  29.2 us (25%)
  waiting for transfers between devices  22.5 us (19%)
  local copies, waits for them, and re-layouts  1.61 us (1%)
    pallas_call x2, Pallas kernels, run_tracers(): pl.pallas_call(functools.partial(tracer_kernel, first=first, lead=lead),...  50.3 us
    ppermute x6, starting transfers between devices, band_shift(): return lax.ppermute(block, 'band', pairs)  19.2 us
    pallas_call x2, Pallas kernels, run_arrange(): pl.pallas_call(arrange_kernel, grid=(count // batch,), in_specs=[pl.Block...  13.7 us
    ppermute x6, waiting for transfers between devices, band_shift(): return lax.ppermute(block, 'band', pairs)  12.4 us
    ppermute x6, starting transfers between devices, over_major(): lax.ppermute(block, 'comp', [(i, (i + 2 * d) % n_comp) for i in range(n_c...  8.44 us
    ppermute x2, waiting for transfers between devices, swap_minor(): return lax.ppermute(block, 'comp', [(i, i ^ 1) for i in range(n_comp)])  6.5 us
    ppermute x6, waiting for transfers between devices, over_major(): lax.ppermute(block, 'comp', [(i, (i + 2 * d) % n_comp) for i in range(n_c...  3.54 us
  transfers between devices with their start and end apart: 14, of which 5 were waited for; matrix products, arithmetic and copies ran while one was open for 1% of the time, Pallas kernels for 35%

profile of v3, /device:TPU:11, one launch (start us, length us, event | category | flops | bytes accessed | tf_op | source)
XLA Modules:
  0.0 118.4 jit_solution(10793196830804588915)
XLA Ops:
  0.6 0.3 collective-permute-start.4
  1.0 0.8 constant_dynamic-update-slice_fusion.1
  1.7 0.8 constant_dynamic-update-slice_fusion
  2.5 1.3 %collective-permute-start = (f32[2,16,512]{2,1,0:T(8,128)S(1)}, f32[2,16,512]{2,1,0:T(8,128)S(1)}, u32[]{:S(2)}, u32[]{:S(2)}) collective-permute-start(f32[2,16,512]{2,1,0:T(8,128)S(1)} %get-tuple-element.28), channel_id=1, source_target_pairs={{0,2},{1,3},{2,4},{3,5},{4,6},{5,7},{6,0},{7,1},{8,10},{9,11},{10,... | collective-permute-start | bytes 196616 | tf_op jit(solution)/shard_map/ppermute | solution.py:406
  3.8 1.1 collective-permute-start.1
  4.8 1.4 %collective-permute-start.2 = (f32[2,16,512]{2,1,0:T(8,128)S(1)}, f32[2,16,512]{2,1,0:T(8,128)S(1)}, u32[]{:S(2)}, u32[]{:S(2)}) collective-permute-start(f32[2,16,512]{2,1,0:T(8,128)S(1)} %get-tuple-element.28), channel_id=1, source_target_pairs={{0,6},{1,7},{2,0},{3,1},{4,2},{5,3},{6,4},{7,5},{8,14},{9,15},{10,... | collective-permute-start | bytes 196616 | tf_op jit(solution)/shard_map/ppermute | solution.py:406
  6.3 6.8 %arrange.2 = (f32[12,8,4,8,128]{4,3,2,1,0:T(8,128)}, f32[12,8,4,8,128]{4,3,2,1,0:T(8,128)}) custom-call(f32[24,8,16,512]{3,2,1,0:T(8,128)} %mass.3), custom_call_target="tpu_custom_call" | custom-call | tf_op jit(solution)/shard_map/arrange/pallas_call | solution.py:335
  13.1 0.0 copy-start.2
  13.1 4.9 %collective-permute-start.10 = (f32[12,8,4,8,128]{4,3,2,1,0:T(8,128)}, f32[12,8,4,8,128]{4,3,2,1,0:T(8,128)}, u32[]{:S(2)}, u32[]{:S(2)}) collective-permute-start(f32[12,8,4,8,128]{4,3,2,1,0:T(8,128)} %get-tuple-element.15.refs_5_), channel_id=1, source_target_pairs={{0,8},{8,16},{16,24},{1,9},{9,17},{17,25},{2,10},{10,18},{18,26},{... | collective-permute-start | bytes 4718600 | tf_op jit(solution)/shard_map/ppermute | solution.py:28
  18.0 6.8 %arrange.3 = (f32[12,8,4,8,128]{4,3,2,1,0:T(8,128)}, f32[12,8,4,8,128]{4,3,2,1,0:T(8,128)}) custom-call(f32[24,8,16,512]{3,2,1,0:T(8,128)} %mass.3), custom_call_target="tpu_custom_call" | custom-call | tf_op jit(solution)/shard_map/arrange/pallas_call | solution.py:335
  24.9 0.0 collective-permute-done.4
  24.9 1.9 %collective-permute-start.11 = (f32[12,8,4,8,128]{4,3,2,1,0:T(8,128)}, f32[12,8,4,8,128]{4,3,2,1,0:T(8,128)}, u32[]{:S(2)}, u32[]{:S(2)}) collective-permute-start(f32[12,8,4,8,128]{4,3,2,1,0:T(8,128)} %get-tuple-element.16.refs_4_), channel_id=1, source_target_pairs={{8,0},{16,8},{24,16},{9,1},{17,9},{25,17},{10,2},{18,10},{26,18},{... | collective-permute-start | bytes 4718600 | tf_op jit(solution)/shard_map/ppermute | solution.py:28
  26.8 0.0 copy-done.2
  26.8 0.0 collective-permute-done
  26.8 0.1 collective-permute-start.5
  26.9 0.0 collective-permute-done.1
  26.9 3.8 %collective-permute-start.12 = (f32[12,8,4,8,128]{4,3,2,1,0:T(8,128)}, f32[12,8,4,8,128]{4,3,2,1,0:T(8,128)S(1)}, u32[]{:S(2)}, u32[]{:S(2)}) collective-permute-start(f32[12,8,4,8,128]{4,3,2,1,0:T(8,128)} %get-tuple-element.20.refs_5_), channel_id=1, source_target_pairs={{0,8},{8,16},{16,24},{1,9},{9,17},{17,25},{2,10},{10,18},{18,26},{... | collective-permute-start | bytes 4718600 | tf_op jit(solution)/shard_map/ppermute | solution.py:28
  30.8 0.0 collective-permute-done.2
  30.8 1.9 %collective-permute-start.13 = (f32[12,8,4,8,128]{4,3,2,1,0:T(8,128)}, f32[12,8,4,8,128]{4,3,2,1,0:T(8,128)}, u32[]{:S(2)}, u32[]{:S(2)}) collective-permute-start(f32[12,8,4,8,128]{4,3,2,1,0:T(8,128)} %get-tuple-element.21.refs_4_), channel_id=1, source_target_pairs={{8,0},{16,8},{24,16},{9,1},{17,9},{25,17},{10,2},{18,10},{26,18},{... | collective-permute-start | bytes 4718600 | tf_op jit(solution)/shard_map/ppermute | solution.py:28
  32.7 0.0 collective-permute-done.5
  32.7 3.3 %collective-permute-start.6 = (f32[2,16,512]{2,1,0:T(8,128)S(1)}, f32[2,16,512]{2,1,0:T(8,128)S(1)}, u32[]{:S(2)}, u32[]{:S(2)}) collective-permute-start(f32[2,16,512]{2,1,0:T(8,128)S(1)} %pad_maximum_fusion.2), channel_id=1, source_target_pairs={{0,4},{1,5},{2,6},{3,7},{4,0},{5,1},{6,2},{7,3},{8,12},{9,13},{10,... | collective-permute-start | bytes 196616 | tf_op jit(solution)/shard_map/ppermute | solution.py:406
  36.0 1.8 %collective-permute-done.6 = f32[2,16,512]{2,1,0:T(8,128)S(1)} collective-permute-done((f32[2,16,512]{2,1,0:T(8,128)S(1)}, f32[2,16,512]{2,1,0:T(8,128)S(1)}, u32[]{:S(2)}, u32[]{:S(2)}) %collective-permute-start.6) | collective-permute-done | bytes 65568 | tf_op jit(solution)/shard_map/ppermute | solution.py:406
  37.7 1.3 %collective-permute-start.7 = (f32[2,16,512]{2,1,0:T(8,128)S(1)}, f32[2,16,512]{2,1,0:T(8,128)S(1)}, u32[]{:S(2)}, u32[]{:S(2)}) collective-permute-start(f32[2,16,512]{2,1,0:T(8,128)S(1)} %pad_maximum_fusion.2), channel_id=1, source_target_pairs={{0,6},{1,7},{2,0},{3,1},{4,2},{5,3},{6,4},{7,5},{8,14},{9,15},{10,... | collective-permute-start | bytes 196616 | tf_op jit(solution)/shard_map/ppermute | solution.py:406
  39.1 1.8 %collective-permute-done.7 = f32[2,16,512]{2,1,0:T(8,128)S(1)} collective-permute-done((f32[2,16,512]{2,1,0:T(8,128)S(1)}, f32[2,16,512]{2,1,0:T(8,128)S(1)}, u32[]{:S(2)}, u32[]{:S(2)}) %collective-permute-start.7) | collective-permute-done | bytes 65568 | tf_op jit(solution)/shard_map/ppermute | solution.py:406
  40.9 1.2 %collective-permute-start.3 = (f32[8,16,512]{2,1,0:T(8,128)S(1)}, f32[8,16,512]{2,1,0:T(8,128)S(1)}, u32[]{:S(2)}, u32[]{:S(2)}) collective-permute-start(f32[8,16,512]{2,1,0:T(8,128)S(1)} %constant_dynamic-update-slice_fusion.2), channel_id=1, source_target_pairs={{0,1},{1,0},{2,3},{3,2},{4,5},{5,4},{6,7},{7,6},{8,9},{9,8},{10,11... | collective-permute-start | bytes 786440 | tf_op jit(solution)/shard_map/ppermute | solution.py:401
  42.1 0.0 copy-start
  42.1 0.0 copy-start.1
  42.1 6.5 %collective-permute-done.3 = f32[8,16,512]{2,1,0:T(8,128)S(1)} collective-permute-done((f32[8,16,512]{2,1,0:T(8,128)S(1)}, f32[8,16,512]{2,1,0:T(8,128)S(1)}, u32[]{:S(2)}, u32[]{:S(2)}) %collective-permute-start.3) | collective-permute-done | bytes 262176 | tf_op jit(solution)/shard_map/ppermute | solution.py:401
  48.6 0.1 pad_maximum_fusion.refs_0_
  48.7 0.1 fusion
  48.7 4.5 %collective-permute-start.8 = (f32[24,8,512]{2,1,0:T(8,128)S(1)}, f32[24,8,512]{2,1,0:T(8,128)S(1)}, u32[]{:S(2)}, u32[]{:S(2)}) collective-permute-start(f32[24,8,512]{2,1,0:T(8,128)S(1)} %get-tuple-element.27), channel_id=1, source_target_pairs={{0,8},{8,16},{16,24},{1,9},{9,17},{17,25},{2,10},{10,18},{18,26},{... | collective-permute-start | bytes 1179656 | tf_op jit(solution)/shard_map/ppermute | solution.py:28
  53.3 4.7 %collective-permute-done.8.refs_1_ = f32[24,8,512]{2,1,0:T(8,128)S(1)} collective-permute-done((f32[24,8,512]{2,1,0:T(8,128)S(1)}, f32[24,8,512]{2,1,0:T(8,128)S(1)}, u32[]{:S(2)}, u32[]{:S(2)}) %collective-permute-start.8) | collective-permute-done | bytes 393248 | tf_op jit(solution)/shard_map/ppermute | solution.py:28
  58.0 2.1 %collective-permute-start.9 = (f32[24,8,512]{2,1,0:T(8,128)S(1)}, f32[24,8,512]{2,1,0:T(8,128)S(1)}, u32[]{:S(2)}, u32[]{:S(2)}) collective-permute-start(f32[24,8,512]{2,1,0:T(8,128)S(1)} %get-tuple-element.26), channel_id=1, source_target_pairs={{8,0},{16,8},{24,16},{9,1},{17,9},{25,17},{10,2},{18,10},{26,18},{... | collective-permute-start | bytes 1179656 | tf_op jit(solution)/shard_map/ppermute | solution.py:28
  60.1 0.1 pad_add_fusion.place
  60.2 7.7 %collective-permute-done.9.refs_2_ = f32[24,8,512]{2,1,0:T(8,128)S(1)} collective-permute-done((f32[24,8,512]{2,1,0:T(8,128)S(1)}, f32[24,8,512]{2,1,0:T(8,128)S(1)}, u32[]{:S(2)}, u32[]{:S(2)}) %collective-permute-start.9) | collective-permute-done | bytes 393248 | tf_op jit(solution)/shard_map/ppermute | solution.py:28
  67.9 0.0 collective-permute-done.10.refs_3_
  67.9 0.0 collective-permute-done.11.refs_6_
  67.9 0.0 copy-done
  67.9 0.0 copy-done.1
  67.9 27.3 %tracers.2 = (f32[24,8,16,512]{3,2,1,0:T(8,128)}, f32[1,16,512]{2,1,0:T(8,128)}, f32[1,16,512]{2,1,0:T(8,128)}, f32[1,16,512]{2,1,0:T(8,128)}, f32[4,32,4,8,128]...) custom-call(s32[3]{0:T(128)S(1)} %pad_add_fusion.place, s32[8]{0:T(128)S(1)} %copy-done, ...), custom_call_target="tpu_custom_call" | custom-call | tf_op jit(solution)/shard_map/tracers/pallas_call | solution.py:372
  95.2 0.0 collective-permute-done.12.refs_3_
  95.2 0.0 collective-permute-done.13.refs_6_
  95.2 23.0 %tracers.3 = f32[24,8,16,512]{3,2,1,0:T(8,128)} custom-call(s32[3]{0:T(128)S(1)} %pad_add_fusion.place, s32[8]{0:T(128)S(1)} %copy-done, s32[96]{0:T(128)S(1)} %copy-done.1, f32[4,32,4,8,128]{4,3,2,1,0:T(8,128)} %get-tuple-element.17.refs_0_, f32[4,32,4,8,128]{4,3,2,1,0:T(8,128)} %get-tuple-element.18.refs_1_, ...), custom_call_target="tpu_custom_call", output_to_operand_aliasing={{}: (10, {})} | custom-call | tf_op jit(solution)/shard_map/tracers/pallas_call | solution.py:372
  (5 shorter events, 0.0 us)
Async XLA Ops:
  0.6 24.2 %collective-permute-start.4 = (f32[1,16,512]{2,1,0:T(8,128)}, f32[1,16,512]{2,1,0:T(8,128)S(1)}, u32[]{:S(2)}, u32[]{:S(2)}) collective-permute-start(f32[1,16,512]{2,1,0:T(8,128)} %param.7), channel_id=1, source_target_pairs={{0,1},{1,0},{2,3},{3,2},{4,5},{5,4},{6,7},{7,6},{8,9},{9,8},{10,11... | collective-permute-start | bytes 98312 | tf_op jit(solution)/shard_map/ppermute | solution.py:401
  2.5 24.3 %collective-permute-start = (f32[2,16,512]{2,1,0:T(8,128)S(1)}, f32[2,16,512]{2,1,0:T(8,128)S(1)}, u32[]{:S(2)}, u32[]{:S(2)}) collective-permute-start(f32[2,16,512]{2,1,0:T(8,128)S(1)} %get-tuple-element.28), channel_id=1, source_target_pairs={{0,2},{1,3},{2,4},{3,5},{4,6},{5,7},{6,0},{7,1},{8,10},{9,11},{10,... | collective-permute-start | bytes 196616 | tf_op jit(solution)/shard_map/ppermute | solution.py:406
  3.8 23.1 %collective-permute-start.1 = (f32[2,16,512]{2,1,0:T(8,128)S(1)}, f32[2,16,512]{2,1,0:T(8,128)S(1)}, u32[]{:S(2)}, u32[]{:S(2)}) collective-permute-start(f32[2,16,512]{2,1,0:T(8,128)S(1)} %get-tuple-element.28), channel_id=1, source_target_pairs={{0,4},{1,5},{2,6},{3,7},{4,0},{5,1},{6,2},{7,3},{8,12},{9,13},{10,... | collective-permute-start | bytes 196616 | tf_op jit(solution)/shard_map/ppermute | solution.py:406
  4.8 25.9 %collective-permute-start.2 = (f32[2,16,512]{2,1,0:T(8,128)S(1)}, f32[2,16,512]{2,1,0:T(8,128)S(1)}, u32[]{:S(2)}, u32[]{:S(2)}) collective-permute-start(f32[2,16,512]{2,1,0:T(8,128)S(1)} %get-tuple-element.28), channel_id=1, source_target_pairs={{0,6},{1,7},{2,0},{3,1},{4,2},{5,3},{6,4},{7,5},{8,14},{9,15},{10,... | collective-permute-start | bytes 196616 | tf_op jit(solution)/shard_map/ppermute | solution.py:406
  13.1 13.7 %copy-start.2 = (f32[1,16,512]{2,1,0:T(8,128)S(1)}, f32[1,16,512]{2,1,0:T(8,128)}, u32[]{:S(2)}) copy-start(f32[1,16,512]{2,1,0:T(8,128)} %param.7) | copy-start | bytes 98308
  13.1 54.8 %collective-permute-start.10 = (f32[12,8,4,8,128]{4,3,2,1,0:T(8,128)}, f32[12,8,4,8,128]{4,3,2,1,0:T(8,128)}, u32[]{:S(2)}, u32[]{:S(2)}) collective-permute-start(f32[12,8,4,8,128]{4,3,2,1,0:T(8,128)} %get-tuple-element.15.refs_5_), channel_id=1, source_target_pairs={{0,8},{8,16},{16,24},{1,9},{9,17},{17,25},{2,10},{10,18},{18,26},{... | collective-permute-start | bytes 4718600 | tf_op jit(solution)/shard_map/ppermute | solution.py:28
  24.9 43.0 %collective-permute-start.11 = (f32[12,8,4,8,128]{4,3,2,1,0:T(8,128)}, f32[12,8,4,8,128]{4,3,2,1,0:T(8,128)}, u32[]{:S(2)}, u32[]{:S(2)}) collective-permute-start(f32[12,8,4,8,128]{4,3,2,1,0:T(8,128)} %get-tuple-element.16.refs_4_), channel_id=1, source_target_pairs={{8,0},{16,8},{24,16},{9,1},{17,9},{25,17},{10,2},{18,10},{26,18},{... | collective-permute-start | bytes 4718600 | tf_op jit(solution)/shard_map/ppermute | solution.py:28
  26.8 5.9 %collective-permute-start.5 = (f32[2,16,512]{2,1,0:T(8,128)S(1)}, f32[2,16,512]{2,1,0:T(8,128)S(1)}, u32[]{:S(2)}, u32[]{:S(2)}) collective-permute-start(f32[2,16,512]{2,1,0:T(8,128)S(1)} %pad_maximum_fusion.2), channel_id=1, source_target_pairs={{0,2},{1,3},{2,4},{3,5},{4,6},{5,7},{6,0},{7,1},{8,10},{9,11},{10,... | collective-permute-start | bytes 196616 | tf_op jit(solution)/shard_map/ppermute | solution.py:406
  26.9 68.3 %collective-permute-start.12 = (f32[12,8,4,8,128]{4,3,2,1,0:T(8,128)}, f32[12,8,4,8,128]{4,3,2,1,0:T(8,128)S(1)}, u32[]{:S(2)}, u32[]{:S(2)}) collective-permute-start(f32[12,8,4,8,128]{4,3,2,1,0:T(8,128)} %get-tuple-element.20.refs_5_), channel_id=1, source_target_pairs={{0,8},{8,16},{16,24},{1,9},{9,17},{17,25},{2,10},{10,18},{18,26},{... | collective-permute-start | bytes 4718600 | tf_op jit(solution)/shard_map/ppermute | solution.py:28
  30.8 64.5 %collective-permute-start.13 = (f32[12,8,4,8,128]{4,3,2,1,0:T(8,128)}, f32[12,8,4,8,128]{4,3,2,1,0:T(8,128)}, u32[]{:S(2)}, u32[]{:S(2)}) collective-permute-start(f32[12,8,4,8,128]{4,3,2,1,0:T(8,128)} %get-tuple-element.21.refs_4_), channel_id=1, source_target_pairs={{8,0},{16,8},{24,16},{9,1},{17,9},{25,17},{10,2},{18,10},{26,18},{... | collective-permute-start | bytes 4718600 | tf_op jit(solution)/shard_map/ppermute | solution.py:28
  32.7 5.0 %collective-permute-start.6 = (f32[2,16,512]{2,1,0:T(8,128)S(1)}, f32[2,16,512]{2,1,0:T(8,128)S(1)}, u32[]{:S(2)}, u32[]{:S(2)}) collective-permute-start(f32[2,16,512]{2,1,0:T(8,128)S(1)} %pad_maximum_fusion.2), channel_id=1, source_target_pairs={{0,4},{1,5},{2,6},{3,7},{4,0},{5,1},{6,2},{7,3},{8,12},{9,13},{10,... | collective-permute-start | bytes 196616 | tf_op jit(solution)/shard_map/ppermute | solution.py:406
  37.7 3.1 %collective-permute-start.7 = (f32[2,16,512]{2,1,0:T(8,128)S(1)}, f32[2,16,512]{2,1,0:T(8,128)S(1)}, u32[]{:S(2)}, u32[]{:S(2)}) collective-permute-start(f32[2,16,512]{2,1,0:T(8,128)S(1)} %pad_maximum_fusion.2), channel_id=1, source_target_pairs={{0,6},{1,7},{2,0},{3,1},{4,2},{5,3},{6,4},{7,5},{8,14},{9,15},{10,... | collective-permute-start | bytes 196616 | tf_op jit(solution)/shard_map/ppermute | solution.py:406
  40.9 7.8 %collective-permute-start.3 = (f32[8,16,512]{2,1,0:T(8,128)S(1)}, f32[8,16,512]{2,1,0:T(8,128)S(1)}, u32[]{:S(2)}, u32[]{:S(2)}) collective-permute-start(f32[8,16,512]{2,1,0:T(8,128)S(1)} %constant_dynamic-update-slice_fusion.2), channel_id=1, source_target_pairs={{0,1},{1,0},{2,3},{3,2},{4,5},{5,4},{6,7},{7,6},{8,9},{9,8},{10,11... | collective-permute-start | bytes 786440 | tf_op jit(solution)/shard_map/ppermute | solution.py:401
  42.1 25.8 %copy-start = (s32[8]{0:T(128)S(1)}, s32[8]{0:T(128)}, u32[]{:S(2)}) copy-start(s32[8]{0:T(128)} %counts.3) | copy-start | bytes 100
  42.1 25.8 %copy-start.1 = (s32[96]{0:T(128)S(1)}, s32[96]{0:T(128)}, u32[]{:S(2)}) copy-start(s32[96]{0:T(128)} %flags.3) | copy-start | bytes 1156
  48.7 9.2 %collective-permute-start.8 = (f32[24,8,512]{2,1,0:T(8,128)S(1)}, f32[24,8,512]{2,1,0:T(8,128)S(1)}, u32[]{:S(2)}, u32[]{:S(2)}) collective-permute-start(f32[24,8,512]{2,1,0:T(8,128)S(1)} %get-tuple-element.27), channel_id=1, source_target_pairs={{0,8},{8,16},{16,24},{1,9},{9,17},{17,25},{2,10},{10,18},{18,26},{... | collective-permute-start | bytes 1179656 | tf_op jit(solution)/shard_map/ppermute | solution.py:28
  58.0 9.9 %collective-permute-start.9 = (f32[24,8,512]{2,1,0:T(8,128)S(1)}, f32[24,8,512]{2,1,0:T(8,128)S(1)}, u32[]{:S(2)}, u32[]{:S(2)}) collective-permute-start(f32[24,8,512]{2,1,0:T(8,128)S(1)} %get-tuple-element.26), channel_id=1, source_target_pairs={{8,0},{16,8},{24,16},{9,1},{17,9},{25,17},{10,2},{18,10},{26,18},{... | collective-permute-start | bytes 1179656 | tf_op jit(solution)/shard_map/ppermute | solution.py:28

commit v4 on v3

--- a/solution.py
+++ b/solution.py
@@ -84,9 +84,7 @@
 
 
 def plane_order(levels):
-    majors = levels // 2
-    swapped = [(field, d, flip) for flip in range(2) for d in range(majors) for field in (1, 2)]
-    return swapped + [(0, d, flip) for d in range(majors) for flip in range(2)]
+    return [(field, d, flip) for flip in range(2) for d in range(levels // 2) for field in range(3)]
 
 
 def source_level(comp, levels, major, flip):
@@ -406,18 +404,15 @@
             received.append(lax.ppermute(block, "comp", [(i, (i + 2 * d) % n_comp) for i in range(n_comp)]))
         return lax.optimization_barrier(jnp.concatenate([block, *received], 0))
 
-    chunk = slots // 2
-    other_height = swap_minor(layer_mass)
-    winds = over_major(jnp.concatenate([zonal_wind, merid_wind], 0))
-    pair = lax.optimization_barrier(jnp.concatenate([layer_mass, other_height], 0))
-    heights = over_major(pair)
-    other_winds = swap_minor(winds)
-    gathered = jnp.concatenate([winds, other_winds, heights], 0)
+    chunk = slots // 3
+    near = over_major(jnp.concatenate([layer_mass, zonal_wind, merid_wind], 0))
+    far = swap_minor(near)
+    gathered = jnp.concatenate([near, far], 0)
     from_north = band_shift(gathered[:, rows - HALO:], 1)
     from_south = band_shift(gathered[:, :HALO], -1)
     blocks = []
-    for first in (0, chunk):
-        top, bottom = run_arrange(tracer_mass, first, chunk)
+    for first, count in ((0, chunk), (chunk, slots - chunk)):
+        top, bottom = run_arrange(tracer_mass, first, count)
         north = band_shift(bottom, 1)
         south = band_shift(top, -1)
         blocks.append((north, top, bottom, south))

time: 119 us -> 116 us (0.975)
  the two profiles are of different devices: /device:TPU:11 before, /device:TPU:14 now
where the time goes in v4:
time: 116 us; the launch traced here: 115 us
  Pallas kernels  64 us (55%)
  waiting for transfers between devices  26.3 us (23%)
  starting transfers between devices  20.5 us (18%)
  other arithmetic  2.03 us (2%)
  local copies, waits for them, and re-layouts  1.38 us (1%)
    pallas_call x2, Pallas kernels, run_tracers(): pl.pallas_call(functools.partial(tracer_kernel, first=first, lead=lead),...  50.4 us
    ppermute x6, waiting for transfers between devices, band_shift(): return lax.ppermute(block, 'band', pairs)  20.7 us
    ppermute x6, starting transfers between devices, band_shift(): return lax.ppermute(block, 'band', pairs)  15.2 us
    pallas_call x2, Pallas kernels, run_arrange(): pl.pallas_call(arrange_kernel, grid=(count // batch,), in_specs=[pl.Block...  13.6 us
    ppermute x3, waiting for transfers between devices, over_major(): lax.ppermute(block, 'comp', [(i, (i + 2 * d) % n_comp) for i in range(n_c...  5.59 us
    ppermute x3, starting transfers between devices, over_major(): lax.ppermute(block, 'comp', [(i, (i + 2 * d) % n_comp) for i in range(n_c...  4.67 us
  transfers between devices with their start and end apart: 10, of which 4 were waited for; matrix products, arithmetic and copies ran while one was open for 2% of the time, Pallas kernels for 23%

profile of v4, /device:TPU:14, one launch (start us, length us, event | category | flops | bytes accessed | tf_op | source)
XLA Modules:
  0.0 115.2 jit_solution(17104313196682696937)
XLA Ops:
  0.6 0.0 copy-start.4
  0.6 0.0 copy-start.5
  0.7 0.0 copy-start.6
  0.7 8.4 %arrange.3 = (f32[16,8,4,8,128]{4,3,2,1,0:T(8,128)}, f32[16,8,4,8,128]{4,3,2,1,0:T(8,128)}) custom-call(f32[24,8,16,512]{3,2,1,0:T(8,128)} %mass.3), custom_call_target="tpu_custom_call" | custom-call | tf_op jit(solution)/shard_map/arrange/pallas_call | solution.py:333
  9.1 1.9 %collective-permute-start.8 = (f32[16,8,4,8,128]{4,3,2,1,0:T(8,128)}, f32[16,8,4,8,128]{4,3,2,1,0:T(8,128)S(1)}, u32[]{:S(2)}, u32[]{:S(2)}) collective-permute-start(f32[16,8,4,8,128]{4,3,2,1,0:T(8,128)} %get-tuple-element.20.refs_5_), channel_id=1, source_target_pairs={{0,8},{8,16},{16,24},{1,9},{9,17},{17,25},{2,10},{10,18},{18,26},{... | collective-permute-start | bytes 6291464 | tf_op jit(solution)/shard_map/ppermute | solution.py:28
  11.0 3.6 %collective-permute-start.9 = (f32[16,8,4,8,128]{4,3,2,1,0:T(8,128)}, f32[16,8,4,8,128]{4,3,2,1,0:T(8,128)}, u32[]{:S(2)}, u32[]{:S(2)}) collective-permute-start(f32[16,8,4,8,128]{4,3,2,1,0:T(8,128)} %get-tuple-element.21.refs_4_), channel_id=1, source_target_pairs={{8,0},{16,8},{24,16},{9,1},{17,9},{25,17},{10,2},{18,10},{26,18},{... | collective-permute-start | bytes 6291464 | tf_op jit(solution)/shard_map/ppermute | solution.py:28
  14.6 0.0 copy-done.4
  14.7 0.0 copy-done.5
  14.7 0.0 copy-done.6
  14.7 1.6 %collective-permute-start = (f32[3,16,512]{2,1,0:T(8,128)S(1)}, f32[3,16,512]{2,1,0:T(8,128)S(1)}, u32[]{:S(2)}, u32[]{:S(2)}) collective-permute-start(f32[3,16,512]{2,1,0:T(8,128)S(1)} %get-tuple-element.28), channel_id=1, source_target_pairs={{0,2},{1,3},{2,4},{3,5},{4,6},{5,7},{6,0},{7,1},{8,10},{9,11},{10,... | collective-permute-start | bytes 294920 | tf_op jit(solution)/shard_map/ppermute | solution.py:404
  16.3 0.4 collective-permute-start.2
  16.8 2.6 %collective-permute-start.1 = (f32[3,16,512]{2,1,0:T(8,128)S(1)}, f32[3,16,512]{2,1,0:T(8,128)S(1)}, u32[]{:S(2)}, u32[]{:S(2)}) collective-permute-start(f32[3,16,512]{2,1,0:T(8,128)S(1)} %get-tuple-element.28), channel_id=1, source_target_pairs={{0,4},{1,5},{2,6},{3,7},{4,0},{5,1},{6,2},{7,3},{8,12},{9,13},{10,... | collective-permute-start | bytes 294920 | tf_op jit(solution)/shard_map/ppermute | solution.py:404
  19.4 0.2 collective-permute-done
  19.6 5.4 %collective-permute-done.1 = f32[3,16,512]{2,1,0:T(8,128)S(1)} collective-permute-done((f32[3,16,512]{2,1,0:T(8,128)S(1)}, f32[3,16,512]{2,1,0:T(8,128)S(1)}, u32[]{:S(2)}, u32[]{:S(2)}) %collective-permute-start.1) | collective-permute-done | bytes 98336 | tf_op jit(solution)/shard_map/ppermute | solution.py:404
  25.0 0.0 collective-permute-done.2
  25.0 0.6 collective-permute-start.3
  25.6 5.2 %arrange.2 = (f32[8,8,4,8,128]{4,3,2,1,0:T(8,128)}, f32[8,8,4,8,128]{4,3,2,1,0:T(8,128)}) custom-call(f32[24,8,16,512]{3,2,1,0:T(8,128)} %mass.3), custom_call_target="tpu_custom_call" | custom-call | tf_op jit(solution)/shard_map/arrange/pallas_call | solution.py:333
  30.8 0.0 copy-start
  30.8 0.0 copy-start.1
  30.8 2.0 %collective-permute-start.6 = (f32[8,8,4,8,128]{4,3,2,1,0:T(8,128)}, f32[8,8,4,8,128]{4,3,2,1,0:T(8,128)}, u32[]{:S(2)}, u32[]{:S(2)}) collective-permute-start(f32[8,8,4,8,128]{4,3,2,1,0:T(8,128)} %get-tuple-element.15.refs_5_), channel_id=1, source_target_pairs={{0,8},{8,16},{16,24},{1,9},{9,17},{17,25},{2,10},{10,18},{18,26},{... | collective-permute-start | bytes 3145736 | tf_op jit(solution)/shard_map/ppermute | solution.py:28
  32.9 3.6 %collective-permute-start.7 = (f32[8,8,4,8,128]{4,3,2,1,0:T(8,128)}, f32[8,8,4,8,128]{4,3,2,1,0:T(8,128)}, u32[]{:S(2)}, u32[]{:S(2)}) collective-permute-start(f32[8,8,4,8,128]{4,3,2,1,0:T(8,128)} %get-tuple-element.16.refs_4_), channel_id=1, source_target_pairs={{8,0},{16,8},{24,16},{9,1},{17,9},{25,17},{10,2},{18,10},{26,18},{... | collective-permute-start | bytes 3145736 | tf_op jit(solution)/shard_map/ppermute | solution.py:28
  36.5 0.0 collective-permute-done.3
  36.6 0.0 copy-start.3
  36.6 0.9 fusion.1
  37.4 0.0 copy-done.3
  37.4 1.9 %collective-permute-start.5 = (f32[24,8,512]{2,1,0:T(8,128)S(1)}, f32[24,8,512]{2,1,0:T(8,128)S(1)}, u32[]{:S(2)}, u32[]{:S(2)}) collective-permute-start(f32[24,8,512]{2,1,0:T(8,128)S(1)} %get-tuple-element.26), channel_id=1, source_target_pairs={{8,0},{16,8},{24,16},{9,1},{17,9},{25,17},{10,2},{18,10},{26,18},{... | collective-permute-start | bytes 1179656 | tf_op jit(solution)/shard_map/ppermute | solution.py:28
  39.4 14.5 %collective-permute-done.5.refs_2_ = f32[24,8,512]{2,1,0:T(8,128)S(1)} collective-permute-done((f32[24,8,512]{2,1,0:T(8,128)S(1)}, f32[24,8,512]{2,1,0:T(8,128)S(1)}, u32[]{:S(2)}, u32[]{:S(2)}) %collective-permute-start.5) | collective-permute-done | bytes 393248 | tf_op jit(solution)/shard_map/ppermute | solution.py:28
  53.8 2.1 %collective-permute-start.4 = (f32[24,8,512]{2,1,0:T(8,128)}, f32[24,8,512]{2,1,0:T(8,128)S(1)}, u32[]{:S(2)}, u32[]{:S(2)}) collective-permute-start(f32[24,8,512]{2,1,0:T(8,128)} %get-tuple-element.27), channel_id=1, source_target_pairs={{0,8},{8,16},{16,24},{1,9},{9,17},{17,25},{2,10},{10,18},{18,26},{... | collective-permute-start | bytes 1179656 | tf_op jit(solution)/shard_map/ppermute | solution.py:28
  55.9 0.1 pad_add_fusion.place
  56.0 1.1 pad_maximum_fusion.refs_0_
  57.1 6.2 %collective-permute-done.4.refs_1_ = f32[24,8,512]{2,1,0:T(8,128)S(1)} collective-permute-done((f32[24,8,512]{2,1,0:T(8,128)}, f32[24,8,512]{2,1,0:T(8,128)S(1)}, u32[]{:S(2)}, u32[]{:S(2)}) %collective-permute-start.4) | collective-permute-done | bytes 393248 | tf_op jit(solution)/shard_map/ppermute | solution.py:28
  63.3 0.0 collective-permute-done.6.refs_3_
  63.3 0.0 collective-permute-done.7.refs_6_
  63.3 0.0 copy-done
  63.3 0.0 copy-done.1
  63.3 21.3 %tracers.2 = (f32[24,8,16,512]{3,2,1,0:T(8,128)}, f32[1,16,512]{2,1,0:T(8,128)}, f32[1,16,512]{2,1,0:T(8,128)}, f32[1,16,512]{2,1,0:T(8,128)}, f32[4,32,4,8,128]...) custom-call(s32[3]{0:T(128)S(1)} %pad_add_fusion.place, s32[8]{0:T(128)S(1)} %copy-done, ...), custom_call_target="tpu_custom_call" | custom-call | tf_op jit(solution)/shard_map/tracers/pallas_call | solution.py:370
  84.6 0.0 collective-permute-done.8.refs_3_
  84.7 0.0 copy-start.2
  84.7 0.0 collective-permute-done.9.refs_6_
  84.7 1.3 %copy-done.2 = f32[16,8,4,8,128]{4,3,2,1,0:T(8,128)} copy-done((f32[16,8,4,8,128]{4,3,2,1,0:T(8,128)}, f32[16,8,4,8,128]{4,3,2,1,0:T(8,128)S(1)}, u32[]{:S(2)}) %copy-start.2) | copy-done | bytes 2097176
  86.0 29.1 %tracers.3 = f32[24,8,16,512]{3,2,1,0:T(8,128)} custom-call(s32[3]{0:T(128)S(1)} %pad_add_fusion.place, s32[8]{0:T(128)S(1)} %copy-done, s32[96]{0:T(128)S(1)} %copy-done.1, f32[4,32,4,8,128]{4,3,2,1,0:T(8,128)} %get-tuple-element.17.refs_0_, f32[4,32,4,8,128]{4,3,2,1,0:T(8,128)} %get-tuple-element.18.refs_1_, ...), custom_call_target="tpu_custom_call", output_to_operand_aliasing={{}: (10, {})} | custom-call | tf_op jit(solution)/shard_map/tracers/pallas_call | solution.py:370
  (6 shorter events, 0.0 us)
Async XLA Ops:
  0.6 14.0 %copy-start.4 = (f32[1,16,512]{2,1,0:T(8,128)S(1)}, f32[1,16,512]{2,1,0:T(8,128)}, u32[]{:S(2)}) copy-start(f32[1,16,512]{2,1,0:T(8,128)} %param.7) | copy-start | bytes 98308
  0.6 14.0 %copy-start.5 = (f32[1,16,512]{2,1,0:T(8,128)S(1)}, f32[1,16,512]{2,1,0:T(8,128)}, u32[]{:S(2)}) copy-start(f32[1,16,512]{2,1,0:T(8,128)} %param.8) | copy-start | bytes 98308
  0.7 14.0 %copy-start.6 = (f32[1,16,512]{2,1,0:T(8,128)S(1)}, f32[1,16,512]{2,1,0:T(8,128)}, u32[]{:S(2)}) copy-start(f32[1,16,512]{2,1,0:T(8,128)} %param.9) | copy-start | bytes 98308
  9.1 75.6 %collective-permute-start.8 = (f32[16,8,4,8,128]{4,3,2,1,0:T(8,128)}, f32[16,8,4,8,128]{4,3,2,1,0:T(8,128)S(1)}, u32[]{:S(2)}, u32[]{:S(2)}) collective-permute-start(f32[16,8,4,8,128]{4,3,2,1,0:T(8,128)} %get-tuple-element.20.refs_5_), channel_id=1, source_target_pairs={{0,8},{8,16},{16,24},{1,9},{9,17},{17,25},{2,10},{10,18},{18,26},{... | collective-permute-start | bytes 6291464 | tf_op jit(solution)/shard_map/ppermute | solution.py:28
  11.0 73.7 %collective-permute-start.9 = (f32[16,8,4,8,128]{4,3,2,1,0:T(8,128)}, f32[16,8,4,8,128]{4,3,2,1,0:T(8,128)}, u32[]{:S(2)}, u32[]{:S(2)}) collective-permute-start(f32[16,8,4,8,128]{4,3,2,1,0:T(8,128)} %get-tuple-element.21.refs_4_), channel_id=1, source_target_pairs={{8,0},{16,8},{24,16},{9,1},{17,9},{25,17},{10,2},{18,10},{26,18},{... | collective-permute-start | bytes 6291464 | tf_op jit(solution)/shard_map/ppermute | solution.py:28
  14.7 4.9 %collective-permute-start = (f32[3,16,512]{2,1,0:T(8,128)S(1)}, f32[3,16,512]{2,1,0:T(8,128)S(1)}, u32[]{:S(2)}, u32[]{:S(2)}) collective-permute-start(f32[3,16,512]{2,1,0:T(8,128)S(1)} %get-tuple-element.28), channel_id=1, source_target_pairs={{0,2},{1,3},{2,4},{3,5},{4,6},{5,7},{6,0},{7,1},{8,10},{9,11},{10,... | collective-permute-start | bytes 294920 | tf_op jit(solution)/shard_map/ppermute | solution.py:404
  16.3 8.7 %collective-permute-start.2 = (f32[3,16,512]{2,1,0:T(8,128)S(1)}, f32[3,16,512]{2,1,0:T(8,128)S(1)}, u32[]{:S(2)}, u32[]{:S(2)}) collective-permute-start(f32[3,16,512]{2,1,0:T(8,128)S(1)} %get-tuple-element.28), channel_id=1, source_target_pairs={{0,6},{1,7},{2,0},{3,1},{4,2},{5,3},{6,4},{7,5},{8,14},{9,15},{10,... | collective-permute-start | bytes 294920 | tf_op jit(solution)/shard_map/ppermute | solution.py:404
  16.8 8.2 %collective-permute-start.1 = (f32[3,16,512]{2,1,0:T(8,128)S(1)}, f32[3,16,512]{2,1,0:T(8,128)S(1)}, u32[]{:S(2)}, u32[]{:S(2)}) collective-permute-start(f32[3,16,512]{2,1,0:T(8,128)S(1)} %get-tuple-element.28), channel_id=1, source_target_pairs={{0,4},{1,5},{2,6},{3,7},{4,0},{5,1},{6,2},{7,3},{8,12},{9,13},{10,... | collective-permute-start | bytes 294920 | tf_op jit(solution)/shard_map/ppermute | solution.py:404
  25.0 11.5 %collective-permute-start.3 = (f32[12,16,512]{2,1,0:T(8,128)S(1)}, f32[12,16,512]{2,1,0:T(8,128)S(1)}, u32[]{:S(2)}, u32[]{:S(2)}) collective-permute-start(f32[12,16,512]{2,1,0:T(8,128)S(1)} %constant_dynamic-update-slice_fusion.3), channel_id=1, source_target_pairs={{0,1},{1,0},{2,3},{3,2},{4,5},{5,4},{6,7},{7,6},{8,9},{9,8},{10,11... | collective-permute-start | bytes 1179656 | tf_op jit(solution)/shard_map/ppermute | solution.py:399
  30.8 32.5 %copy-start = (s32[8]{0:T(128)S(1)}, s32[8]{0:T(128)}, u32[]{:S(2)}) copy-start(s32[8]{0:T(128)} %counts.3) | copy-start | bytes 100
  30.8 32.5 %copy-start.1 = (s32[96]{0:T(128)S(1)}, s32[96]{0:T(128)}, u32[]{:S(2)}) copy-start(s32[96]{0:T(128)} %flags.3) | copy-start | bytes 1156
  30.8 32.5 %collective-permute-start.6 = (f32[8,8,4,8,128]{4,3,2,1,0:T(8,128)}, f32[8,8,4,8,128]{4,3,2,1,0:T(8,128)}, u32[]{:S(2)}, u32[]{:S(2)}) collective-permute-start(f32[8,8,4,8,128]{4,3,2,1,0:T(8,128)} %get-tuple-element.15.refs_5_), channel_id=1, source_target_pairs={{0,8},{8,16},{16,24},{1,9},{9,17},{17,25},{2,10},{10,18},{18,26},{... | collective-permute-start | bytes 3145736 | tf_op jit(solution)/shard_map/ppermute | solution.py:28
  32.9 30.4 %collective-permute-start.7 = (f32[8,8,4,8,128]{4,3,2,1,0:T(8,128)}, f32[8,8,4,8,128]{4,3,2,1,0:T(8,128)}, u32[]{:S(2)}, u32[]{:S(2)}) collective-permute-start(f32[8,8,4,8,128]{4,3,2,1,0:T(8,128)} %get-tuple-element.16.refs_4_), channel_id=1, source_target_pairs={{8,0},{16,8},{24,16},{9,1},{17,9},{25,17},{10,2},{18,10},{26,18},{... | collective-permute-start | bytes 3145736 | tf_op jit(solution)/shard_map/ppermute | solution.py:28
  36.6 0.9 copy-start.3
  37.4 16.4 %collective-permute-start.5 = (f32[24,8,512]{2,1,0:T(8,128)S(1)}, f32[24,8,512]{2,1,0:T(8,128)S(1)}, u32[]{:S(2)}, u32[]{:S(2)}) collective-permute-start(f32[24,8,512]{2,1,0:T(8,128)S(1)} %get-tuple-element.26), channel_id=1, source_target_pairs={{8,0},{16,8},{24,16},{9,1},{17,9},{25,17},{10,2},{18,10},{26,18},{... | collective-permute-start | bytes 1179656 | tf_op jit(solution)/shard_map/ppermute | solution.py:28
  53.8 9.5 %collective-permute-start.4 = (f32[24,8,512]{2,1,0:T(8,128)}, f32[24,8,512]{2,1,0:T(8,128)S(1)}, u32[]{:S(2)}, u32[]{:S(2)}) collective-permute-start(f32[24,8,512]{2,1,0:T(8,128)} %get-tuple-element.27), channel_id=1, source_target_pairs={{0,8},{8,16},{16,24},{1,9},{9,17},{17,25},{2,10},{10,18},{18,26},{... | collective-permute-start | bytes 1179656 | tf_op jit(solution)/shard_map/ppermute | solution.py:28
  84.7 1.3 %copy-start.2 = (f32[16,8,4,8,128]{4,3,2,1,0:T(8,128)}, f32[16,8,4,8,128]{4,3,2,1,0:T(8,128)S(1)}, u32[]{:S(2)}) copy-start(f32[16,8,4,8,128]{4,3,2,1,0:T(8,128)S(1)} %collective-permute-done.8.refs_3_) | copy-start | bytes 6291460

commit v5 on v4

--- a/solution.py
+++ b/solution.py
@@ -19,7 +19,8 @@
 
 
 LANES = 128
-DELAY = 3
+DELAY = 6
+BATCH = 1
 
 
 def band_shift(block, offset):
@@ -109,17 +110,19 @@
                     out[t, q:q + 8, p] = tile
 
 
-def run_dynamics(place, own, north, south, h_out, u_out, v_out, inv_ref, east_ref, south_ref,
+def run_dynamics(place, state, near, far_state, far, north, south, h_out, u_out, v_out, inv_ref, east_ref, south_ref,
                  h0, u0, v0, h1, u1, v1, geo, stage):
-    planes, rows, columns = own.shape
+    planes, rows, columns = north.shape[0], *near.shape[1:]
     parts = columns // LANES
     halo = north.shape[1]
     total = rows + 2 * halo
     levels = planes // 3
+    sources = [(piece, i) for piece in (state, near, far_state, far) for i in range(piece.shape[0])]
     for plane, (field, major, flip) in enumerate(plane_order(levels)):
         level = source_level(place[0], levels, major, flip)
-        for source, base in ((north, 0), (own, halo), (south, halo + rows)):
-            stage[field, level, base:base + source.shape[1]] = source[plane]
+        own = sources[plane][0][sources[plane][1]]
+        for block, base in ((north[plane], 0), (own, halo), (south[plane], halo + rows)):
+            stage[field, level, base:base + block.shape[0]] = block
     for field, dst in enumerate((h0, u0, v0)):
         for q in range(0, total, 8):
             block = jnp.swapaxes(stage[field, :, q:q + 8], 0, 1)
@@ -199,7 +202,7 @@
 def tracer_kernel(place, counts, flags, *refs, first, lead):
     step_id = pl.program_id(0)
     if lead:
-        planes, (north, top, bottom, south, out_ref), refs = refs[:3], refs[3:8], refs[8:]
+        planes, (north, top, bottom, south, out_ref), refs = refs[:6], refs[6:11], refs[11:]
         states, kept, refs = refs[:3], refs[3:6], refs[6:]
     else:
         kept, (north, top, bottom, south, _, out_ref), refs = refs[:3], refs[3:9], refs[9:]
@@ -218,7 +221,7 @@
                 copy.wait()
 
     inv_ref, east_ref, south_ref = fluxes
-    slot = step_id + first
+    batch = north.shape[0]
     parts = north.shape[2]
     halo = north.shape[1]
     half = top.shape[1]
@@ -228,15 +231,13 @@
     start = jnp.int32(0)
     for g in range(counts.shape[0]):
         start = start + jnp.where(g < group, counts[g], 0)
-    live = slot < counts[group]
-    flag = flags[jnp.minimum(start + slot, flags.shape[0] - 1)]
-
-    def entry(j):
+
+    def entry(t, j):
         for source, base in ((south, halo + rows), (bottom, halo + half), (top, halo), (north, 0)):
             if j >= base:
-                return [source[0, j - base, p] for p in range(parts)]
-
-    def run(limited):
+                return [source[t, j - base, p] for p in range(parts)]
+
+    def run(t, limited):
         def spread(buffer, j, tiles):
             for p in range(parts):
                 buffer[j, p + 1] = tiles[p]
@@ -245,7 +246,7 @@
             buffer[j, parts + 2] = after(tiles[1])
 
         for j in range(total):
-            spread(even, j, [t * inv_ref[0, j, p] for p, t in enumerate(entry(j))])
+            spread(even, j, [t * inv_ref[0, j, p] for p, t in enumerate(entry(t, j))])
 
         def face(a2, a, b, b2, bounds):
             raw = 7.0 * (a + b) - (a2 + b2)
@@ -269,6 +270,8 @@
 
             def finish(j, tiles, moved):
                 tiles = [tiles[0] + moved, *tiles[1:]]
+                if step + 1 == STEPS:
+                    tiles = restore(tiles)
                 for p in range(parts):
                     cur[j, p] = tiles[p]
                 if step + 1 < STEPS:
@@ -287,7 +290,7 @@
                         for p in range(parts)]
                 moved = before(east[-1])
                 following = south_terms(j + 1, near, bound)
-                mass = entry(j) if step == 0 else [cur[j, p] for p in range(parts)]
+                mass = entry(t, j) if step == 0 else [cur[j, p] for p in range(parts)]
                 tiles = [mass[0] - (east[0] + (following[0] - term[0]))]
                 tiles += [mass[p] - ((east[p] - east[p - 1]) + (following[p] - term[p])) for p in range(1, parts)]
                 term = following
@@ -299,21 +302,29 @@
             src, dst = dst, src
         for q in range(0, rows, 8):
             base = halo + q
-            tiles = restore([cur[base:base + 8, p] for p in range(parts)])
-            for p, tile in enumerate(tiles):
-                out_ref[0, :, q:q + 8, p * LANES:(p + 1) * LANES] = jnp.swapaxes(tile, 0, 1)
-
-    @pl.when(live & (flag > 0))
-    def _():
-        run(True)
-
-    @pl.when(live & (flag <= 0))
-    def _():
-        run(False)
-
-    @pl.when(jnp.logical_not(live))
-    def _():
-        out_ref[...] = jnp.zeros_like(out_ref)
+            for p in range(parts):
+                out_ref[t, :, q:q + 8, p * LANES:(p + 1) * LANES] = jnp.swapaxes(cur[base:base + 8, p], 0, 1)
+
+    def one(t, carry):
+        slot = step_id * batch + t + first
+        live = slot < counts[group]
+        flag = flags[jnp.minimum(start + slot, flags.shape[0] - 1)]
+
+        @pl.when(live & (flag > 0))
+        def _():
+            run(t, True)
+
+        @pl.when(live & (flag <= 0))
+        def _():
+            run(t, False)
+
+        @pl.when(jnp.logical_not(live))
+        def _():
+            out_ref[t] = jnp.zeros(out_ref.shape[1:], jnp.float32)
+
+        return carry
+
+    lax.fori_loop(0, batch, one, 0)
 
     if lead:
         @pl.when(step_id == pl.num_programs(0) - 1)
@@ -328,7 +339,7 @@
 
 def run_arrange(mass, first, count):
     _, levels, rows, columns = mass.shape
-    batch = math.gcd(4, count, first)
+    batch = next(b for b in range(4, 0, -1) if math.gcd(count, first) % b == 0)
     half = jax.ShapeDtypeStruct((count, rows // 2, columns // LANES, levels, LANES), jnp.float32)
     return pl.pallas_call(
         arrange_kernel,
@@ -348,8 +359,9 @@
     tiles = (total, parts, levels, lanes)
     wide = (total, parts + 3, levels, lanes)
     anywhere = pl.BlockSpec(memory_space=pl.ANY)
-    block_specs = [pl.BlockSpec((1, *b.shape[1:]), lambda i, *_: (i, 0, 0, 0, 0)) for b in blocks]
-    out_specs = [pl.BlockSpec((1, *out_shape[1:]), lambda i, *_: (i + first, 0, 0, 0))]
+    batch = math.gcd(BATCH, count, first)
+    block_specs = [pl.BlockSpec((batch, *b.shape[1:]), lambda i, *_: (i, 0, 0, 0, 0)) for b in blocks]
+    out_specs = [pl.BlockSpec((batch, *out_shape[1:]), lambda i, *_: (i + first // batch, 0, 0, 0))]
     out_types = [jax.ShapeDtypeStruct(out_shape, jnp.float32)]
     scratch = [tiles, wide, wide] + [(STEPS, *tiles)] * 3
     scratch = [pltpu.VMEM(s, jnp.float32) for s in scratch] + [pltpu.SemaphoreType.DMA((3,))]
@@ -371,7 +383,7 @@
         functools.partial(tracer_kernel, first=first, lead=lead),
         grid_spec=pltpu.PrefetchScalarGridSpec(
             num_scalar_prefetch=3,
-            grid=(count,),
+            grid=(count // batch,),
             in_specs=in_specs,
             out_specs=out_specs,
             scratch_shapes=scratch,
@@ -398,25 +410,24 @@
     def swap_minor(block):
         return lax.ppermute(block, "comp", [(i, i ^ 1) for i in range(n_comp)])
 
-    def over_major(block):
-        received = []
-        for d in range(1, majors):
-            received.append(lax.ppermute(block, "comp", [(i, (i + 2 * d) % n_comp) for i in range(n_comp)]))
-        return lax.optimization_barrier(jnp.concatenate([block, *received], 0))
-
-    chunk = slots // 3
-    near = over_major(jnp.concatenate([layer_mass, zonal_wind, merid_wind], 0))
+    state = jnp.concatenate([layer_mass, zonal_wind, merid_wind], 0)
+    received = []
+    for d in range(1, majors):
+        received.append(lax.ppermute(state, "comp", [(i, (i + 2 * d) % n_comp) for i in range(n_comp)]))
+    near = lax.optimization_barrier(jnp.concatenate(received, 0))
+    far_state = swap_minor(state)
     far = swap_minor(near)
-    gathered = jnp.concatenate([near, far], 0)
-    from_north = band_shift(gathered[:, rows - HALO:], 1)
-    from_south = band_shift(gathered[:, :HALO], -1)
+    pieces = (state, near, far_state, far)
+    from_north = band_shift(jnp.concatenate([x[:, rows - HALO:] for x in pieces], 0), 1)
+    from_south = band_shift(jnp.concatenate([x[:, :HALO] for x in pieces], 0), -1)
+    chunk = (3 * slots) // 8
     blocks = []
     for first, count in ((0, chunk), (chunk, slots - chunk)):
         top, bottom = run_arrange(tracer_mass, first, count)
         north = band_shift(bottom, 1)
         south = band_shift(top, -1)
         blocks.append((north, top, bottom, south))
-    planes = (gathered, from_north, from_south)
+    planes = (*pieces, from_north, from_south)
     earlier, height, zonal, merid, *kept = run_tracers(
         place, group_counts, limiter_flags, blocks[0], planes, None, None, 0, tracer_mass.shape)
     tracers, = run_tracers(

time: 116 us -> 111 us (0.957)
  the two profiles are of different devices: /device:TPU:14 before, /device:TPU:11 now
where the time goes in v5:
time: 111 us; the launch traced here: 110 us
  Pallas kernels  62.2 us (56%)
  starting transfers between devices  23 us (21%)
  waiting for transfers between devices  22.7 us (20%)
    pallas_call x2, Pallas kernels, run_tracers(): pl.pallas_call(functools.partial(tracer_kernel, first=first, lead=lead),...  48.6 us
    ppermute x6, waiting for transfers between devices, band_shift(): return lax.ppermute(block, 'band', pairs)  18 us
    ppermute x6, starting transfers between devices, band_shift(): return lax.ppermute(block, 'band', pairs)  16.7 us
    pallas_call x2, Pallas kernels, run_arrange(): pl.pallas_call(arrange_kernel, grid=(count // batch,), in_specs=[pl.Block...  13.6 us
    ppermute x3, starting transfers between devices, on_device(): lax.ppermute(state, 'comp', [(i, (i + 2 * d) % n_comp) for i in range(n_c...  4.73 us
    ppermute x2, waiting for transfers between devices, swap_minor(): return lax.ppermute(block, 'comp', [(i, i ^ 1) for i in range(n_comp)])  4.68 us
  transfers between devices with their start and end apart: 11, of which 3 were waited for; matrix products, arithmetic and copies ran while one was open for 1% of the time, Pallas kernels for 25%

profile of v5, /device:TPU:11, one launch (start us, length us, event | category | flops | bytes accessed | tf_op | source)
XLA Modules:
  0.0 109.8 jit_solution(3791142229327887065)
XLA Ops:
  0.6 0.0 copy-start.2
  0.6 0.0 copy-start.3
  0.7 0.0 copy-start.4
  0.7 8.0 %arrange.3 = (f32[15,8,4,8,128]{4,3,2,1,0:T(8,128)}, f32[15,8,4,8,128]{4,3,2,1,0:T(8,128)}) custom-call(f32[24,8,16,512]{3,2,1,0:T(8,128)} %mass.3), custom_call_target="tpu_custom_call" | custom-call | tf_op jit(solution)/shard_map/arrange/pallas_call | solution.py:344
  8.7 3.7 %collective-permute-start.9 = (f32[15,8,4,8,128]{4,3,2,1,0:T(8,128)}, f32[15,8,4,8,128]{4,3,2,1,0:T(8,128)S(1)}, u32[]{:S(2)}, u32[]{:S(2)}) collective-permute-start(f32[15,8,4,8,128]{4,3,2,1,0:T(8,128)} %get-tuple-element.20.refs_5_), channel_id=1, source_target_pairs={{0,8},{8,16},{16,24},{1,9},{9,17},{17,25},{2,10},{10,18},{18,26},{... | collective-permute-start | bytes 5898248 | tf_op jit(solution)/shard_map/ppermute | solution.py:29
  12.4 1.9 %collective-permute-start.10 = (f32[15,8,4,8,128]{4,3,2,1,0:T(8,128)}, f32[15,8,4,8,128]{4,3,2,1,0:T(8,128)}, u32[]{:S(2)}, u32[]{:S(2)}) collective-permute-start(f32[15,8,4,8,128]{4,3,2,1,0:T(8,128)} %get-tuple-element.21.refs_4_), channel_id=1, source_target_pairs={{8,0},{16,8},{24,16},{9,1},{17,9},{25,17},{10,2},{18,10},{26,18},{... | collective-permute-start | bytes 5898248 | tf_op jit(solution)/shard_map/ppermute | solution.py:29
  14.3 0.0 copy-done.2
  14.4 0.0 copy-done.3
  14.4 0.0 copy-done.4
  14.4 0.2 collective-permute-start.2
  14.6 2.3 %collective-permute-start.1 = (f32[3,16,512]{2,1,0:T(8,128)S(1)}, f32[3,16,512]{2,1,0:T(8,128)S(1)}, u32[]{:S(2)}, u32[]{:S(2)}) collective-permute-start(f32[3,16,512]{2,1,0:T(8,128)S(1)} %constant_dynamic-update-slice_fusion.refs_0_), channel_id=1, source_target_pairs={{0,4},{1,5},{2,6},{3,7},{4,0},{5,1},{6,2},{7,3},{8,12},{9,13},{10,... | collective-permute-start | bytes 294920 | tf_op jit(solution)/shard_map/ppermute | solution.py:416
  16.9 2.2 %collective-permute-start = (f32[3,16,512]{2,1,0:T(8,128)S(1)}, f32[3,16,512]{2,1,0:T(8,128)S(1)}, u32[]{:S(2)}, u32[]{:S(2)}) collective-permute-start(f32[3,16,512]{2,1,0:T(8,128)S(1)} %constant_dynamic-update-slice_fusion.refs_0_), channel_id=1, source_target_pairs={{0,2},{1,3},{2,4},{3,5},{4,6},{5,7},{6,0},{7,1},{8,10},{9,11},{10,... | collective-permute-start | bytes 294920 | tf_op jit(solution)/shard_map/ppermute | solution.py:416
  19.1 5.6 %arrange.2 = (f32[9,8,4,8,128]{4,3,2,1,0:T(8,128)}, f32[9,8,4,8,128]{4,3,2,1,0:T(8,128)}) custom-call(f32[24,8,16,512]{3,2,1,0:T(8,128)} %mass.3), custom_call_target="tpu_custom_call" | custom-call | tf_op jit(solution)/shard_map/arrange/pallas_call | solution.py:344
  24.7 0.0 copy-start
  24.7 0.0 copy-start.1
  24.7 0.0 collective-permute-done.2
  24.7 0.3 collective-permute-start.3
  25.0 0.0 collective-permute-done.1
  25.0 4.8 %collective-permute-start.7 = (f32[9,8,4,8,128]{4,3,2,1,0:T(8,128)}, f32[9,8,4,8,128]{4,3,2,1,0:T(8,128)}, u32[]{:S(2)}, u32[]{:S(2)}) collective-permute-start(f32[9,8,4,8,128]{4,3,2,1,0:T(8,128)} %get-tuple-element.15.refs_8_), channel_id=1, source_target_pairs={{0,8},{8,16},{16,24},{1,9},{9,17},{17,25},{2,10},{10,18},{18,26},{... | collective-permute-start | bytes 3538952 | tf_op jit(solution)/shard_map/ppermute | solution.py:29
  29.8 0.0 collective-permute-done
  29.8 1.3 %collective-permute-start.4 = (f32[9,16,512]{2,1,0:T(8,128)S(1)}, f32[9,16,512]{2,1,0:T(8,128)S(1)}, u32[]{:S(2)}, u32[]{:S(2)}) collective-permute-start(f32[9,16,512]{2,1,0:T(8,128)S(1)} %pad_maximum_fusion.2.refs_1_), channel_id=1, source_target_pairs={{0,1},{1,0},{2,3},{3,2},{4,5},{5,4},{6,7},{7,6},{8,9},{9,8},{10,11... | collective-permute-start | bytes 884744 | tf_op jit(solution)/shard_map/ppermute | solution.py:411
  31.1 0.0 collective-permute-done.3.refs_2_
  31.1 1.9 %collective-permute-start.8 = (f32[9,8,4,8,128]{4,3,2,1,0:T(8,128)}, f32[9,8,4,8,128]{4,3,2,1,0:T(8,128)}, u32[]{:S(2)}, u32[]{:S(2)}) collective-permute-start(f32[9,8,4,8,128]{4,3,2,1,0:T(8,128)} %get-tuple-element.16.refs_7_), channel_id=1, source_target_pairs={{8,0},{16,8},{24,16},{9,1},{17,9},{25,17},{10,2},{18,10},{26,18},{... | collective-permute-start | bytes 3538952 | tf_op jit(solution)/shard_map/ppermute | solution.py:29
  33.1 4.7 %collective-permute-done.4.refs_3_ = f32[9,16,512]{2,1,0:T(8,128)S(1)} collective-permute-done((f32[9,16,512]{2,1,0:T(8,128)S(1)}, f32[9,16,512]{2,1,0:T(8,128)S(1)}, u32[]{:S(2)}, u32[]{:S(2)}) %collective-permute-start.4) | collective-permute-done | bytes 294944 | tf_op jit(solution)/shard_map/ppermute | solution.py:411
  37.8 2.3 %collective-permute-start.5 = (f32[24,8,512]{2,1,0:T(8,128)S(1)}, f32[24,8,512]{2,1,0:T(8,128)S(1)}, u32[]{:S(2)}, u32[]{:S(2)}) collective-permute-start(f32[24,8,512]{2,1,0:T(8,128)S(1)} %pad_maximum_fusion), channel_id=1, source_target_pairs={{0,8},{8,16},{16,24},{1,9},{9,17},{17,25},{2,10},{10,18},{18,26},{... | collective-permute-start | bytes 1179656 | tf_op jit(solution)/shard_map/ppermute | solution.py:29
  40.1 0.8 pad_maximum_fusion.1
  40.9 10.1 %collective-permute-done.5.refs_4_ = f32[24,8,512]{2,1,0:T(8,128)S(1)} collective-permute-done((f32[24,8,512]{2,1,0:T(8,128)S(1)}, f32[24,8,512]{2,1,0:T(8,128)S(1)}, u32[]{:S(2)}, u32[]{:S(2)}) %collective-permute-start.5) | collective-permute-done | bytes 393248 | tf_op jit(solution)/shard_map/ppermute | solution.py:29
  51.0 2.1 %collective-permute-start.6 = (f32[24,8,512]{2,1,0:T(8,128)}, f32[24,8,512]{2,1,0:T(8,128)S(1)}, u32[]{:S(2)}, u32[]{:S(2)}) collective-permute-start(f32[24,8,512]{2,1,0:T(8,128)} %pad_maximum_fusion.1), channel_id=1, source_target_pairs={{8,0},{16,8},{24,16},{9,1},{17,9},{25,17},{10,2},{18,10},{26,18},{... | collective-permute-start | bytes 1179656 | tf_op jit(solution)/shard_map/ppermute | solution.py:29
  53.1 0.1 pad_add_fusion.place
  53.2 7.9 %collective-permute-done.6.refs_5_ = f32[24,8,512]{2,1,0:T(8,128)S(1)} collective-permute-done((f32[24,8,512]{2,1,0:T(8,128)}, f32[24,8,512]{2,1,0:T(8,128)S(1)}, u32[]{:S(2)}, u32[]{:S(2)}) %collective-permute-start.6) | collective-permute-done | bytes 393248 | tf_op jit(solution)/shard_map/ppermute | solution.py:29
  61.1 0.0 collective-permute-done.7.refs_6_
  61.1 0.0 collective-permute-done.8.refs_9_
  61.1 0.0 copy-done
  61.1 0.0 copy-done.1
  61.1 22.4 %tracers.2 = (f32[24,8,16,512]{3,2,1,0:T(8,128)}, f32[1,16,512]{2,1,0:T(8,128)}, f32[1,16,512]{2,1,0:T(8,128)}, f32[1,16,512]{2,1,0:T(8,128)}, f32[4,32,4,8,128]...) custom-call(s32[3]{0:T(128)S(1)} %pad_add_fusion.place, s32[8]{0:T(128)S(1)} %copy-done, ...), custom_call_target="tpu_custom_call" | custom-call | tf_op jit(solution)/shard_map/tracers/pallas_call | solution.py:382
  83.5 0.0 collective-permute-done.9.refs_3_
  83.5 0.0 collective-permute-done.10.refs_6_
  83.5 26.2 %tracers.3 = f32[24,8,16,512]{3,2,1,0:T(8,128)} custom-call(s32[3]{0:T(128)S(1)} %pad_add_fusion.place, s32[8]{0:T(128)S(1)} %copy-done, s32[96]{0:T(128)S(1)} %copy-done.1, f32[4,32,4,8,128]{4,3,2,1,0:T(8,128)} %get-tuple-element.17.refs_0_, f32[4,32,4,8,128]{4,3,2,1,0:T(8,128)} %get-tuple-element.18.refs_1_, ...), custom_call_target="tpu_custom_call", output_to_operand_aliasing={{}: (10, {})} | custom-call | tf_op jit(solution)/shard_map/tracers/pallas_call | solution.py:382
  (9 shorter events, 0.1 us)
Async XLA Ops:
  0.6 13.7 %copy-start.2 = (f32[1,16,512]{2,1,0:T(8,128)S(1)}, f32[1,16,512]{2,1,0:T(8,128)}, u32[]{:S(2)}) copy-start(f32[1,16,512]{2,1,0:T(8,128)} %param.7) | copy-start | bytes 98308
  0.6 13.7 %copy-start.3 = (f32[1,16,512]{2,1,0:T(8,128)S(1)}, f32[1,16,512]{2,1,0:T(8,128)}, u32[]{:S(2)}) copy-start(f32[1,16,512]{2,1,0:T(8,128)} %param.8) | copy-start | bytes 98308
  0.7 13.7 %copy-start.4 = (f32[1,16,512]{2,1,0:T(8,128)S(1)}, f32[1,16,512]{2,1,0:T(8,128)}, u32[]{:S(2)}) copy-start(f32[1,16,512]{2,1,0:T(8,128)} %param.9) | copy-start | bytes 98308
  8.7 74.8 %collective-permute-start.9 = (f32[15,8,4,8,128]{4,3,2,1,0:T(8,128)}, f32[15,8,4,8,128]{4,3,2,1,0:T(8,128)S(1)}, u32[]{:S(2)}, u32[]{:S(2)}) collective-permute-start(f32[15,8,4,8,128]{4,3,2,1,0:T(8,128)} %get-tuple-element.20.refs_5_), channel_id=1, source_target_pairs={{0,8},{8,16},{16,24},{1,9},{9,17},{17,25},{2,10},{10,18},{18,26},{... | collective-permute-start | bytes 5898248 | tf_op jit(solution)/shard_map/ppermute | solution.py:29
  12.4 71.1 %collective-permute-start.10 = (f32[15,8,4,8,128]{4,3,2,1,0:T(8,128)}, f32[15,8,4,8,128]{4,3,2,1,0:T(8,128)}, u32[]{:S(2)}, u32[]{:S(2)}) collective-permute-start(f32[15,8,4,8,128]{4,3,2,1,0:T(8,128)} %get-tuple-element.21.refs_4_), channel_id=1, source_target_pairs={{8,0},{16,8},{24,16},{9,1},{17,9},{25,17},{10,2},{18,10},{26,18},{... | collective-permute-start | bytes 5898248 | tf_op jit(solution)/shard_map/ppermute | solution.py:29
  14.4 10.3 %collective-permute-start.2 = (f32[3,16,512]{2,1,0:T(8,128)S(1)}, f32[3,16,512]{2,1,0:T(8,128)S(1)}, u32[]{:S(2)}, u32[]{:S(2)}) collective-permute-start(f32[3,16,512]{2,1,0:T(8,128)S(1)} %constant_dynamic-update-slice_fusion.refs_0_), channel_id=1, source_target_pairs={{0,6},{1,7},{2,0},{3,1},{4,2},{5,3},{6,4},{7,5},{8,14},{9,15},{10,... | collective-permute-start | bytes 294920 | tf_op jit(solution)/shard_map/ppermute | solution.py:416
  14.6 10.4 %collective-permute-start.1 = (f32[3,16,512]{2,1,0:T(8,128)S(1)}, f32[3,16,512]{2,1,0:T(8,128)S(1)}, u32[]{:S(2)}, u32[]{:S(2)}) collective-permute-start(f32[3,16,512]{2,1,0:T(8,128)S(1)} %constant_dynamic-update-slice_fusion.refs_0_), channel_id=1, source_target_pairs={{0,4},{1,5},{2,6},{3,7},{4,0},{5,1},{6,2},{7,3},{8,12},{9,13},{10,... | collective-permute-start | bytes 294920 | tf_op jit(solution)/shard_map/ppermute | solution.py:416
  16.9 12.9 %collective-permute-start = (f32[3,16,512]{2,1,0:T(8,128)S(1)}, f32[3,16,512]{2,1,0:T(8,128)S(1)}, u32[]{:S(2)}, u32[]{:S(2)}) collective-permute-start(f32[3,16,512]{2,1,0:T(8,128)S(1)} %constant_dynamic-update-slice_fusion.refs_0_), channel_id=1, source_target_pairs={{0,2},{1,3},{2,4},{3,5},{4,6},{5,7},{6,0},{7,1},{8,10},{9,11},{10,... | collective-permute-start | bytes 294920 | tf_op jit(solution)/shard_map/ppermute | solution.py:416
  24.7 36.4 %copy-start = (s32[8]{0:T(128)S(1)}, s32[8]{0:T(128)}, u32[]{:S(2)}) copy-start(s32[8]{0:T(128)} %counts.3) | copy-start | bytes 100
  24.7 36.4 %copy-start.1 = (s32[96]{0:T(128)S(1)}, s32[96]{0:T(128)}, u32[]{:S(2)}) copy-start(s32[96]{0:T(128)} %flags.3) | copy-start | bytes 1156
  24.7 6.4 %collective-permute-start.3 = (f32[3,16,512]{2,1,0:T(8,128)S(1)}, f32[3,16,512]{2,1,0:T(8,128)S(1)}, u32[]{:S(2)}, u32[]{:S(2)}) collective-permute-start(f32[3,16,512]{2,1,0:T(8,128)S(1)} %constant_dynamic-update-slice_fusion.refs_0_), channel_id=1, source_target_pairs={{0,1},{1,0},{2,3},{3,2},{4,5},{5,4},{6,7},{7,6},{8,9},{9,8},{10,11... | collective-permute-start | bytes 294920 | tf_op jit(solution)/shard_map/ppermute | solution.py:411
  25.0 36.0 %collective-permute-start.7 = (f32[9,8,4,8,128]{4,3,2,1,0:T(8,128)}, f32[9,8,4,8,128]{4,3,2,1,0:T(8,128)}, u32[]{:S(2)}, u32[]{:S(2)}) collective-permute-start(f32[9,8,4,8,128]{4,3,2,1,0:T(8,128)} %get-tuple-element.15.refs_8_), channel_id=1, source_target_pairs={{0,8},{8,16},{16,24},{1,9},{9,17},{17,25},{2,10},{10,18},{18,26},{... | collective-permute-start | bytes 3538952 | tf_op jit(solution)/shard_map/ppermute | solution.py:29
  29.8 7.9 %collective-permute-start.4 = (f32[9,16,512]{2,1,0:T(8,128)S(1)}, f32[9,16,512]{2,1,0:T(8,128)S(1)}, u32[]{:S(2)}, u32[]{:S(2)}) collective-permute-start(f32[9,16,512]{2,1,0:T(8,128)S(1)} %pad_maximum_fusion.2.refs_1_), channel_id=1, source_target_pairs={{0,1},{1,0},{2,3},{3,2},{4,5},{5,4},{6,7},{7,6},{8,9},{9,8},{10,11... | collective-permute-start | bytes 884744 | tf_op jit(solution)/shard_map/ppermute | solution.py:411
  31.1 29.9 %collective-permute-start.8 = (f32[9,8,4,8,128]{4,3,2,1,0:T(8,128)}, f32[9,8,4,8,128]{4,3,2,1,0:T(8,128)}, u32[]{:S(2)}, u32[]{:S(2)}) collective-permute-start(f32[9,8,4,8,128]{4,3,2,1,0:T(8,128)} %get-tuple-element.16.refs_7_), channel_id=1, source_target_pairs={{8,0},{16,8},{24,16},{9,1},{17,9},{25,17},{10,2},{18,10},{26,18},{... | collective-permute-start | bytes 3538952 | tf_op jit(solution)/shard_map/ppermute | solution.py:29
  37.8 13.2 %collective-permute-start.5 = (f32[24,8,512]{2,1,0:T(8,128)S(1)}, f32[24,8,512]{2,1,0:T(8,128)S(1)}, u32[]{:S(2)}, u32[]{:S(2)}) collective-permute-start(f32[24,8,512]{2,1,0:T(8,128)S(1)} %pad_maximum_fusion), channel_id=1, source_target_pairs={{0,8},{8,16},{16,24},{1,9},{9,17},{17,25},{2,10},{10,18},{18,26},{... | collective-permute-start | bytes 1179656 | tf_op jit(solution)/shard_map/ppermute | solution.py:29
  51.0 10.0 %collective-permute-start.6 = (f32[24,8,512]{2,1,0:T(8,128)}, f32[24,8,512]{2,1,0:T(8,128)S(1)}, u32[]{:S(2)}, u32[]{:S(2)}) collective-permute-start(f32[24,8,512]{2,1,0:T(8,128)} %pad_maximum_fusion.1), channel_id=1, source_target_pairs={{8,0},{16,8},{24,16},{9,1},{17,9},{25,17},{10,2},{18,10},{26,18},{... | collective-permute-start | bytes 1179656 | tf_op jit(solution)/shard_map/ppermute | solution.py:29

commit v6 on v5

--- a/solution.py
+++ b/solution.py
@@ -398,7 +398,7 @@
 def on_device(tracer_mass, layer_mass, zonal_wind, merid_wind, group_counts, limiter_flags):
     n_comp = lax.axis_size("comp")
     n_band = lax.axis_size("band")
-    slots, levels, rows, _ = tracer_mass.shape
+    slots, levels, rows, columns = tracer_mass.shape
     level_block = layer_mass.shape[0]
     assert rows == 2 * HALO and levels == 8
     place = jnp.stack([
@@ -410,7 +410,8 @@
     def swap_minor(block):
         return lax.ppermute(block, "comp", [(i, i ^ 1) for i in range(n_comp)])
 
-    state = jnp.concatenate([layer_mass, zonal_wind, merid_wind], 0)
+    field = lax.broadcasted_iota(jnp.int32, (3, rows, columns), 0)
+    state = jnp.where(field == 0, layer_mass, jnp.where(field == 1, zonal_wind, merid_wind))
     received = []
     for d in range(1, majors):
         received.append(lax.ppermute(state, "comp", [(i, (i + 2 * d) % n_comp) for i in range(n_comp)]))

time: 111 us -> 111 us (level)
  no operation moved by 1% of the time
where the time goes in v6:
time: 111 us; the launch traced here: 110 us
  Pallas kernels  62.1 us (56%)
  starting transfers between devices  23 us (21%)
  waiting for transfers between devices  22.6 us (20%)
    pallas_call x2, Pallas kernels, run_tracers(): pl.pallas_call(functools.partial(tracer_kernel, first=first, lead=lead),...  48.5 us
    ppermute x6, waiting for transfers between devices, band_shift(): return lax.ppermute(block, 'band', pairs)  18 us
    ppermute x6, starting transfers between devices, band_shift(): return lax.ppermute(block, 'band', pairs)  16.7 us
    pallas_call x2, Pallas kernels, run_arrange(): pl.pallas_call(arrange_kernel, grid=(count // batch,), in_specs=[pl.Block...  13.6 us
    ppermute x3, starting transfers between devices, on_device(): lax.ppermute(state, 'comp', [(i, (i + 2 * d) % n_comp) for i in range(n_c...  4.73 us
    ppermute x2, waiting for transfers between devices, swap_minor(): return lax.ppermute(block, 'comp', [(i, i ^ 1) for i in range(n_comp)])  4.68 us
  transfers between devices with their start and end apart: 11, of which 3 were waited for; matrix products, arithmetic and copies ran while one was open for 1% of the time, Pallas kernels for 25%

profile of v6, /device:TPU:11, one launch (start us, length us, event | category | flops | bytes accessed | tf_op | source)
XLA Modules:
  0.0 109.8 jit_solution(2916622047236314802)
XLA Ops:
  0.6 0.0 copy-start.2
  0.6 0.0 copy-start.3
  0.7 0.0 copy-start.4
  0.7 8.0 %arrange.3 = (f32[15,8,4,8,128]{4,3,2,1,0:T(8,128)}, f32[15,8,4,8,128]{4,3,2,1,0:T(8,128)}) custom-call(f32[24,8,16,512]{3,2,1,0:T(8,128)} %mass.3), custom_call_target="tpu_custom_call" | custom-call | tf_op jit(solution)/shard_map/arrange/pallas_call | solution.py:344
  8.7 3.7 %collective-permute-start.9 = (f32[15,8,4,8,128]{4,3,2,1,0:T(8,128)}, f32[15,8,4,8,128]{4,3,2,1,0:T(8,128)S(1)}, u32[]{:S(2)}, u32[]{:S(2)}) collective-permute-start(f32[15,8,4,8,128]{4,3,2,1,0:T(8,128)} %get-tuple-element.20.refs_5_), channel_id=1, source_target_pairs={{0,8},{8,16},{16,24},{1,9},{9,17},{17,25},{2,10},{10,18},{18,26},{... | collective-permute-start | bytes 5898248 | tf_op jit(solution)/shard_map/ppermute | solution.py:29
  12.4 1.9 %collective-permute-start.10 = (f32[15,8,4,8,128]{4,3,2,1,0:T(8,128)}, f32[15,8,4,8,128]{4,3,2,1,0:T(8,128)}, u32[]{:S(2)}, u32[]{:S(2)}) collective-permute-start(f32[15,8,4,8,128]{4,3,2,1,0:T(8,128)} %get-tuple-element.21.refs_4_), channel_id=1, source_target_pairs={{8,0},{16,8},{24,16},{9,1},{17,9},{25,17},{10,2},{18,10},{26,18},{... | collective-permute-start | bytes 5898248 | tf_op jit(solution)/shard_map/ppermute | solution.py:29
  14.3 0.0 copy-done.2
  14.4 0.0 copy-done.3
  14.4 0.0 copy-done.4
  14.4 0.1 select_select_fusion.refs_0_
  14.5 0.2 collective-permute-start.2
  14.7 2.3 %collective-permute-start.1 = (f32[3,16,512]{2,1,0:T(8,128)S(1)}, f32[3,16,512]{2,1,0:T(8,128)S(1)}, u32[]{:S(2)}, u32[]{:S(2)}) collective-permute-start(f32[3,16,512]{2,1,0:T(8,128)S(1)} %select_select_fusion.refs_0_), channel_id=1, source_target_pairs={{0,4},{1,5},{2,6},{3,7},{4,0},{5,1},{6,2},{7,3},{8,12},{9,13},{10,... | collective-permute-start | bytes 294920 | tf_op jit(solution)/shard_map/ppermute | solution.py:417
  17.0 2.2 %collective-permute-start = (f32[3,16,512]{2,1,0:T(8,128)S(1)}, f32[3,16,512]{2,1,0:T(8,128)S(1)}, u32[]{:S(2)}, u32[]{:S(2)}) collective-permute-start(f32[3,16,512]{2,1,0:T(8,128)S(1)} %select_select_fusion.refs_0_), channel_id=1, source_target_pairs={{0,2},{1,3},{2,4},{3,5},{4,6},{5,7},{6,0},{7,1},{8,10},{9,11},{10,... | collective-permute-start | bytes 294920 | tf_op jit(solution)/shard_map/ppermute | solution.py:417
  19.2 5.6 %arrange.2 = (f32[9,8,4,8,128]{4,3,2,1,0:T(8,128)}, f32[9,8,4,8,128]{4,3,2,1,0:T(8,128)}) custom-call(f32[24,8,16,512]{3,2,1,0:T(8,128)} %mass.3), custom_call_target="tpu_custom_call" | custom-call | tf_op jit(solution)/shard_map/arrange/pallas_call | solution.py:344
  24.7 0.0 copy-start
  24.8 0.0 copy-start.1
  24.8 0.0 collective-permute-done.2
  24.8 0.3 collective-permute-start.3
  25.1 0.0 collective-permute-done.1
  25.1 4.8 %collective-permute-start.7 = (f32[9,8,4,8,128]{4,3,2,1,0:T(8,128)}, f32[9,8,4,8,128]{4,3,2,1,0:T(8,128)}, u32[]{:S(2)}, u32[]{:S(2)}) collective-permute-start(f32[9,8,4,8,128]{4,3,2,1,0:T(8,128)} %get-tuple-element.15.refs_8_), channel_id=1, source_target_pairs={{0,8},{8,16},{16,24},{1,9},{9,17},{17,25},{2,10},{10,18},{18,26},{... | collective-permute-start | bytes 3538952 | tf_op jit(solution)/shard_map/ppermute | solution.py:29
  29.8 0.0 collective-permute-done
  29.9 1.3 %collective-permute-start.4 = (f32[9,16,512]{2,1,0:T(8,128)S(1)}, f32[9,16,512]{2,1,0:T(8,128)S(1)}, u32[]{:S(2)}, u32[]{:S(2)}) collective-permute-start(f32[9,16,512]{2,1,0:T(8,128)S(1)} %pad_maximum_fusion.2.refs_1_), channel_id=1, source_target_pairs={{0,1},{1,0},{2,3},{3,2},{4,5},{5,4},{6,7},{7,6},{8,9},{9,8},{10,11... | collective-permute-start | bytes 884744 | tf_op jit(solution)/shard_map/ppermute | solution.py:411
  31.2 0.0 collective-permute-done.3.refs_2_
  31.2 1.9 %collective-permute-start.8 = (f32[9,8,4,8,128]{4,3,2,1,0:T(8,128)}, f32[9,8,4,8,128]{4,3,2,1,0:T(8,128)}, u32[]{:S(2)}, u32[]{:S(2)}) collective-permute-start(f32[9,8,4,8,128]{4,3,2,1,0:T(8,128)} %get-tuple-element.16.refs_7_), channel_id=1, source_target_pairs={{8,0},{16,8},{24,16},{9,1},{17,9},{25,17},{10,2},{18,10},{26,18},{... | collective-permute-start | bytes 3538952 | tf_op jit(solution)/shard_map/ppermute | solution.py:29
  33.1 4.7 %collective-permute-done.4.refs_3_ = f32[9,16,512]{2,1,0:T(8,128)S(1)} collective-permute-done((f32[9,16,512]{2,1,0:T(8,128)S(1)}, f32[9,16,512]{2,1,0:T(8,128)S(1)}, u32[]{:S(2)}, u32[]{:S(2)}) %collective-permute-start.4) | collective-permute-done | bytes 294944 | tf_op jit(solution)/shard_map/ppermute | solution.py:411
  37.9 2.3 %collective-permute-start.5 = (f32[24,8,512]{2,1,0:T(8,128)S(1)}, f32[24,8,512]{2,1,0:T(8,128)S(1)}, u32[]{:S(2)}, u32[]{:S(2)}) collective-permute-start(f32[24,8,512]{2,1,0:T(8,128)S(1)} %pad_maximum_fusion), channel_id=1, source_target_pairs={{0,8},{8,16},{16,24},{1,9},{9,17},{17,25},{2,10},{10,18},{18,26},{... | collective-permute-start | bytes 1179656 | tf_op jit(solution)/shard_map/ppermute | solution.py:29
  40.2 0.8 pad_maximum_fusion.1
  40.9 10.1 %collective-permute-done.5.refs_4_ = f32[24,8,512]{2,1,0:T(8,128)S(1)} collective-permute-done((f32[24,8,512]{2,1,0:T(8,128)S(1)}, f32[24,8,512]{2,1,0:T(8,128)S(1)}, u32[]{:S(2)}, u32[]{:S(2)}) %collective-permute-start.5) | collective-permute-done | bytes 393248 | tf_op jit(solution)/shard_map/ppermute | solution.py:29
  51.0 2.1 %collective-permute-start.6 = (f32[24,8,512]{2,1,0:T(8,128)}, f32[24,8,512]{2,1,0:T(8,128)S(1)}, u32[]{:S(2)}, u32[]{:S(2)}) collective-permute-start(f32[24,8,512]{2,1,0:T(8,128)} %pad_maximum_fusion.1), channel_id=1, source_target_pairs={{8,0},{16,8},{24,16},{9,1},{17,9},{25,17},{10,2},{18,10},{26,18},{... | collective-permute-start | bytes 1179656 | tf_op jit(solution)/shard_map/ppermute | solution.py:29
  53.1 0.1 pad_add_fusion.place
  53.2 7.9 %collective-permute-done.6.refs_5_ = f32[24,8,512]{2,1,0:T(8,128)S(1)} collective-permute-done((f32[24,8,512]{2,1,0:T(8,128)}, f32[24,8,512]{2,1,0:T(8,128)S(1)}, u32[]{:S(2)}, u32[]{:S(2)}) %collective-permute-start.6) | collective-permute-done | bytes 393248 | tf_op jit(solution)/shard_map/ppermute | solution.py:29
  61.1 0.0 collective-permute-done.7.refs_6_
  61.1 0.0 collective-permute-done.8.refs_9_
  61.1 0.0 copy-done
  61.1 0.0 copy-done.1
  61.1 22.4 %tracers.2 = (f32[24,8,16,512]{3,2,1,0:T(8,128)}, f32[1,16,512]{2,1,0:T(8,128)}, f32[1,16,512]{2,1,0:T(8,128)}, f32[1,16,512]{2,1,0:T(8,128)}, f32[4,32,4,8,128]...) custom-call(s32[3]{0:T(128)S(1)} %pad_add_fusion.place, s32[8]{0:T(128)S(1)} %copy-done, ...), custom_call_target="tpu_custom_call" | custom-call | tf_op jit(solution)/shard_map/tracers/pallas_call | solution.py:382
  83.5 0.0 collective-permute-done.9.refs_3_
  83.5 0.0 collective-permute-done.10.refs_6_
  83.5 26.1 %tracers.3 = f32[24,8,16,512]{3,2,1,0:T(8,128)} custom-call(s32[3]{0:T(128)S(1)} %pad_add_fusion.place, s32[8]{0:T(128)S(1)} %copy-done, s32[96]{0:T(128)S(1)} %copy-done.1, f32[4,32,4,8,128]{4,3,2,1,0:T(8,128)} %get-tuple-element.17.refs_0_, f32[4,32,4,8,128]{4,3,2,1,0:T(8,128)} %get-tuple-element.18.refs_1_, ...), custom_call_target="tpu_custom_call", output_to_operand_aliasing={{}: (10, {})} | custom-call | tf_op jit(solution)/shard_map/tracers/pallas_call | solution.py:382
  (7 shorter events, 0.1 us)
Async XLA Ops:
  0.6 13.7 %copy-start.2 = (f32[1,16,512]{2,1,0:T(8,128)S(1)}, f32[1,16,512]{2,1,0:T(8,128)}, u32[]{:S(2)}) copy-start(f32[1,16,512]{2,1,0:T(8,128)} %param.9) | copy-start | bytes 98308
  0.6 13.7 %copy-start.3 = (f32[1,16,512]{2,1,0:T(8,128)S(1)}, f32[1,16,512]{2,1,0:T(8,128)}, u32[]{:S(2)}) copy-start(f32[1,16,512]{2,1,0:T(8,128)} %param.8) | copy-start | bytes 98308
  0.7 13.7 %copy-start.4 = (f32[1,16,512]{2,1,0:T(8,128)S(1)}, f32[1,16,512]{2,1,0:T(8,128)}, u32[]{:S(2)}) copy-start(f32[1,16,512]{2,1,0:T(8,128)} %param.7) | copy-start | bytes 98308
  8.7 74.8 %collective-permute-start.9 = (f32[15,8,4,8,128]{4,3,2,1,0:T(8,128)}, f32[15,8,4,8,128]{4,3,2,1,0:T(8,128)S(1)}, u32[]{:S(2)}, u32[]{:S(2)}) collective-permute-start(f32[15,8,4,8,128]{4,3,2,1,0:T(8,128)} %get-tuple-element.20.refs_5_), channel_id=1, source_target_pairs={{0,8},{8,16},{16,24},{1,9},{9,17},{17,25},{2,10},{10,18},{18,26},{... | collective-permute-start | bytes 5898248 | tf_op jit(solution)/shard_map/ppermute | solution.py:29
  12.4 71.1 %collective-permute-start.10 = (f32[15,8,4,8,128]{4,3,2,1,0:T(8,128)}, f32[15,8,4,8,128]{4,3,2,1,0:T(8,128)}, u32[]{:S(2)}, u32[]{:S(2)}) collective-permute-start(f32[15,8,4,8,128]{4,3,2,1,0:T(8,128)} %get-tuple-element.21.refs_4_), channel_id=1, source_target_pairs={{8,0},{16,8},{24,16},{9,1},{17,9},{25,17},{10,2},{18,10},{26,18},{... | collective-permute-start | bytes 5898248 | tf_op jit(solution)/shard_map/ppermute | solution.py:29
  14.5 10.3 %collective-permute-start.2 = (f32[3,16,512]{2,1,0:T(8,128)S(1)}, f32[3,16,512]{2,1,0:T(8,128)S(1)}, u32[]{:S(2)}, u32[]{:S(2)}) collective-permute-start(f32[3,16,512]{2,1,0:T(8,128)S(1)} %select_select_fusion.refs_0_), channel_id=1, source_target_pairs={{0,6},{1,7},{2,0},{3,1},{4,2},{5,3},{6,4},{7,5},{8,14},{9,15},{10,... | collective-permute-start | bytes 294920 | tf_op jit(solution)/shard_map/ppermute | solution.py:417
  14.7 10.4 %collective-permute-start.1 = (f32[3,16,512]{2,1,0:T(8,128)S(1)}, f32[3,16,512]{2,1,0:T(8,128)S(1)}, u32[]{:S(2)}, u32[]{:S(2)}) collective-permute-start(f32[3,16,512]{2,1,0:T(8,128)S(1)} %select_select_fusion.refs_0_), channel_id=1, source_target_pairs={{0,4},{1,5},{2,6},{3,7},{4,0},{5,1},{6,2},{7,3},{8,12},{9,13},{10,... | collective-permute-start | bytes 294920 | tf_op jit(solution)/shard_map/ppermute | solution.py:417
  17.0 12.9 %collective-permute-start = (f32[3,16,512]{2,1,0:T(8,128)S(1)}, f32[3,16,512]{2,1,0:T(8,128)S(1)}, u32[]{:S(2)}, u32[]{:S(2)}) collective-permute-start(f32[3,16,512]{2,1,0:T(8,128)S(1)} %select_select_fusion.refs_0_), channel_id=1, source_target_pairs={{0,2},{1,3},{2,4},{3,5},{4,6},{5,7},{6,0},{7,1},{8,10},{9,11},{10,... | collective-permute-start | bytes 294920 | tf_op jit(solution)/shard_map/ppermute | solution.py:417
  24.7 36.3 %copy-start = (s32[8]{0:T(128)S(1)}, s32[8]{0:T(128)}, u32[]{:S(2)}) copy-start(s32[8]{0:T(128)} %counts.3) | copy-start | bytes 100
  24.8 36.3 %copy-start.1 = (s32[96]{0:T(128)S(1)}, s32[96]{0:T(128)}, u32[]{:S(2)}) copy-start(s32[96]{0:T(128)} %flags.3) | copy-start | bytes 1156
  24.8 6.4 %collective-permute-start.3 = (f32[3,16,512]{2,1,0:T(8,128)S(1)}, f32[3,16,512]{2,1,0:T(8,128)S(1)}, u32[]{:S(2)}, u32[]{:S(2)}) collective-permute-start(f32[3,16,512]{2,1,0:T(8,128)S(1)} %select_select_fusion.refs_0_), channel_id=1, source_target_pairs={{0,1},{1,0},{2,3},{3,2},{4,5},{5,4},{6,7},{7,6},{8,9},{9,8},{10,11... | collective-permute-start | bytes 294920 | tf_op jit(solution)/shard_map/ppermute | solution.py:411
  25.1 36.0 %collective-permute-start.7 = (f32[9,8,4,8,128]{4,3,2,1,0:T(8,128)}, f32[9,8,4,8,128]{4,3,2,1,0:T(8,128)}, u32[]{:S(2)}, u32[]{:S(2)}) collective-permute-start(f32[9,8,4,8,128]{4,3,2,1,0:T(8,128)} %get-tuple-element.15.refs_8_), channel_id=1, source_target_pairs={{0,8},{8,16},{16,24},{1,9},{9,17},{17,25},{2,10},{10,18},{18,26},{... | collective-permute-start | bytes 3538952 | tf_op jit(solution)/shard_map/ppermute | solution.py:29
  29.9 7.9 %collective-permute-start.4 = (f32[9,16,512]{2,1,0:T(8,128)S(1)}, f32[9,16,512]{2,1,0:T(8,128)S(1)}, u32[]{:S(2)}, u32[]{:S(2)}) collective-permute-start(f32[9,16,512]{2,1,0:T(8,128)S(1)} %pad_maximum_fusion.2.refs_1_), channel_id=1, source_target_pairs={{0,1},{1,0},{2,3},{3,2},{4,5},{5,4},{6,7},{7,6},{8,9},{9,8},{10,11... | collective-permute-start | bytes 884744 | tf_op jit(solution)/shard_map/ppermute | solution.py:411
  31.2 29.9 %collective-permute-start.8 = (f32[9,8,4,8,128]{4,3,2,1,0:T(8,128)}, f32[9,8,4,8,128]{4,3,2,1,0:T(8,128)}, u32[]{:S(2)}, u32[]{:S(2)}) collective-permute-start(f32[9,8,4,8,128]{4,3,2,1,0:T(8,128)} %get-tuple-element.16.refs_7_), channel_id=1, source_target_pairs={{8,0},{16,8},{24,16},{9,1},{17,9},{25,17},{10,2},{18,10},{26,18},{... | collective-permute-start | bytes 3538952 | tf_op jit(solution)/shard_map/ppermute | solution.py:29
  37.9 13.1 %collective-permute-start.5 = (f32[24,8,512]{2,1,0:T(8,128)S(1)}, f32[24,8,512]{2,1,0:T(8,128)S(1)}, u32[]{:S(2)}, u32[]{:S(2)}) collective-permute-start(f32[24,8,512]{2,1,0:T(8,128)S(1)} %pad_maximum_fusion), channel_id=1, source_target_pairs={{0,8},{8,16},{16,24},{1,9},{9,17},{17,25},{2,10},{10,18},{18,26},{... | collective-permute-start | bytes 1179656 | tf_op jit(solution)/shard_map/ppermute | solution.py:29
  51.0 10.0 %collective-permute-start.6 = (f32[24,8,512]{2,1,0:T(8,128)}, f32[24,8,512]{2,1,0:T(8,128)S(1)}, u32[]{:S(2)}, u32[]{:S(2)}) collective-permute-start(f32[24,8,512]{2,1,0:T(8,128)} %pad_maximum_fusion.1), channel_id=1, source_target_pairs={{8,0},{16,8},{24,16},{9,1},{17,9},{25,17},{10,2},{18,10},{26,18},{... | collective-permute-start | bytes 1179656 | tf_op jit(solution)/shard_map/ppermute | solution.py:29
